TPU v7x, 512 devices: a whole 4x8x8 slice. The times are simulated.
512 devices in a mesh: py: 32 (over y, x), pz: 16 (over z, core).
Axes of the slice: x: 4, y: 8, z: 8, core: 2. Of those that a mesh axis runs over, the one named last changes fastest.
Arguments:
- velocity: float32 [3, 32, 1024, 1024], P(None, 'py', 'pz'), may hold values from -14 to 14
Outputs:
- nu_t: float32 [32, 1024, 1024], P('py', 'pz')
- filtered_velocity: bfloat16 [3, 32, 1024, 1024], P(None, 'py', None, 'pz')
All inputs are finite; a program needn't handle non-finite values.
Results may differ from a plain program's by a relative error of at most 0.012.
The roundings to bfloat16 on the way count: a program that leaves them out, or rounds other values in their place, can miss the bound.
Values may be sent and summed in bfloat16 or wider, within the bound.
No kernel may reach another device: no remote copies, remote signals or barrier semaphores. Data moves between devices by JAX's collectives and lax.ppermute only.
A program may use at most 64 MiB of HBM per device.

v0:
```python
import math

import jax
import jax.numpy as jnp
import numpy as np
from jax import lax
from jax.sharding import PartitionSpec as P

index_pairs = ((0, 0), (1, 1), (2, 2), (0, 1), (0, 2), (1, 2))
pair_weights = (1.0, 1.0, 1.0, 2.0, 2.0, 2.0)
epsilon = 1e-06


def extended(x, sides, width):
    edges = {}
    for axis, dim in sides:
        devices, length = (lax.axis_size(axis), x.shape[dim])
        up = [(i, (i + 1) % devices) for i in range(devices)]
        last = lax.slice_in_dim(x, length - width, length, axis=dim)
        initial = lax.slice_in_dim(x, 0, width, axis=dim)
        edges[dim] = (
            lax.ppermute(last, axis, up),
            lax.ppermute(initial, axis, [(b, a) for a, b in up]),
        )
    done = []
    for _, dim in sides:
        low, high = edges[dim]
        around = [(width, width) if d in done else (0, 0) for d in range(x.ndim)]
        x = jnp.concatenate([jnp.pad(low, around), x, jnp.pad(high, around)], axis=dim)
        done.append(dim)
    return x


def copy_for_each(x, axis):
    copies = jnp.broadcast_to(x, (lax.axis_size(axis), *x.shape))
    return lax.all_to_all(copies, axis, split_axis=0, concat_axis=0, tiled=True)


def taken_together(x, axis):
    return copy_for_each(x, axis).sum(axis=0)


def packed_total(arrays, axis):
    line, at, gathered = (jnp.concatenate([a.reshape(-1) for a in arrays]), 0, [])
    running = taken_together(line, axis)
    for a in arrays:
        gathered.append(running[at : at + a.size].reshape(a.shape))
        at += a.size
    return tuple(gathered)


def filter_table(length):
    offsets = np.arange(length, dtype=np.int64)
    wavenumbers = np.arange(1, length // 4, dtype=np.int64)
    phase = offsets[:, None] * wavenumbers[None, :] % length
    kernel = (1.0 + 2.0 * np.cos(phase * (2.0 * math.pi / length)).sum(axis=1)) / length
    kernel = kernel.astype(np.float32)
    lagged = (offsets[:, None] - offsets[None, :]) % length
    return jnp.asarray(kernel[lagged], dtype=jnp.float32).astype(jnp.bfloat16)


def seal_walls(padded):
    device_index = lax.axis_index("py")
    last_index = lax.axis_size("py") - 1
    lower_rim = jnp.where(device_index == 0, jnp.zeros_like(padded[:, :1]), padded[:, :1])
    upper_rim = jnp.where(
        device_index == last_index, jnp.zeros_like(padded[:, -1:]), padded[:, -1:]
    )
    return jnp.concatenate([lower_rim, padded[:, 1:-1], upper_rim], axis=1)


def derivatives(padded, rim_axis):
    padded = padded.astype(jnp.float32)
    if rim_axis == 2:
        interior = padded[:, 1:-1, 1:-1, :]
        slope_rim = (padded[:, 1:-1, 2:, :] - padded[:, 1:-1, :-2, :]) * 0.5
        slope_roll = (jnp.roll(interior, -1, 3) - jnp.roll(interior, 1, 3)) * 0.5
        slope_y = (padded[:, 2:, 1:-1, :] - padded[:, :-2, 1:-1, :]) * 0.5
        return (slope_roll, slope_y, slope_rim)
    interior = padded[:, 1:-1, :, 1:-1]
    slope_rim = (padded[:, 1:-1, :, 2:] - padded[:, 1:-1, :, :-2]) * 0.5
    slope_roll = (jnp.roll(interior, -1, 2) - jnp.roll(interior, 1, 2)) * 0.5
    slope_y = (padded[:, 2:, :, 1:-1] - padded[:, :-2, :, 1:-1]) * 0.5
    return (slope_rim, slope_y, slope_roll)


def strain(gradients):
    strain_parts = [0.5 * (gradients[b][a] + gradients[a][b]) for a, b in index_pairs]
    squares_sum = pair_weights[0] * strain_parts[0] * strain_parts[0]
    for weight, part_value in zip(pair_weights[1:], strain_parts[1:]):
        squares_sum = squares_sum + weight * part_value * part_value
    return (strain_parts, jnp.sqrt(2.0 * squares_sum))


def lilly_sums(filtered, padded_hat, rim_axis):
    hat_parts, magnitude_hat = strain(derivatives(padded_hat, rim_axis))
    smooth_velocity = filtered[:3].astype(jnp.float32)
    numerator = jnp.zeros_like(magnitude_hat)
    denominator = jnp.zeros_like(magnitude_hat)
    for pair_index, (a, b) in enumerate(index_pairs):
        leonard = (
            filtered[3 + pair_index].astype(jnp.float32) - smooth_velocity[a] * smooth_velocity[b]
        )
        model_term = (
            filtered[9 + pair_index].astype(jnp.float32)
            - 4.0 * magnitude_hat * hat_parts[pair_index]
        )
        numerator = numerator + pair_weights[pair_index] * leonard * model_term
        denominator = denominator + pair_weights[pair_index] * model_term * model_term
    return (jnp.sum(numerator, axis=(1, 2)), jnp.sum(denominator, axis=(1, 2)))


def body(velocity):
    padded = extended(velocity, (("py", 1), ("pz", 2)), 1)
    strain_parts, magnitude = strain(derivatives(seal_walls(padded), 2))
    pieces = [velocity[a].astype(jnp.bfloat16) for a in range(3)]
    pieces = pieces + [(velocity[a] * velocity[b]).astype(jnp.bfloat16) for a, b in index_pairs]
    pieces = pieces + [(magnitude * part_value).astype(jnp.bfloat16) for part_value in strain_parts]
    fields = jnp.stack(pieces)
    table_x = filter_table(velocity.shape[3])
    table_z = filter_table(velocity.shape[2] * lax.axis_size("pz"))
    along_x = jnp.einsum(
        "fyzx,xv->fyzv", fields, table_x, preferred_element_type=jnp.float32
    ).astype(jnp.bfloat16)
    filtered = jnp.einsum(
        "wz,fyzx->fywx",
        table_z,
        lax.all_to_all(along_x, "pz", split_axis=3, concat_axis=2, tiled=True),
        preferred_element_type=jnp.float32,
    ).astype(jnp.bfloat16)
    padded_hat = extended(filtered[:3], (("py", 1), ("pz", 3)), 1)
    numerator, denominator = lilly_sums(filtered, seal_walls(padded_hat), 3)
    numerator, denominator = packed_total((numerator, denominator), "pz")
    plane_cells = velocity.shape[3] * velocity.shape[2] * lax.axis_size("pz")
    coefficient = numerator / plane_cells / (2.0 * (denominator / plane_cells + epsilon))
    nu_t = coefficient[:, None, None] * magnitude
    return (nu_t, filtered[:3])


def solution(mesh):
    in_specs = (P(None, "py", "pz", None),)
    out_specs = (P("py", "pz", None), P(None, "py", None, "pz"))
    return jax.shard_map(body, mesh=mesh, in_specs=in_specs, out_specs=out_specs, check_vma=False)
```

profile of v0, /device:TPU:1, one launch (start us, length us, event | category | flops | bytes accessed | tf_op | source)
XLA Modules:
  0.0 176.1 jit_solution(13759545348752628538)
XLA Ops:
  0.6 0.0 copy-start
  0.6 4.1 %collective-permute-start.1 = (f32[3,1,64,1024]{3,2,1,0:T(8,128)}, f32[3,1,64,1024]{3,2,1,0:T(8,128)S(1)}, u32[]{:S(2)}, u32[]{:S(2)}) collective-permute-start(f32[3,1,64,1024]{3,2,1,0:T(8,128)} %param.3), channel_id=1, source_target_pairs={{0,16},{16,32},{32,48},{48,64},{64,80},{80,96},{96,112},{112,128},... | collective-permute-start | bytes 2359304 | tf_op jit(solution)/shard_map/ppermute | solution.py:22
  4.7 6.1 %collective-permute-start.2 = (f32[3,1,64,1024]{3,2,1,0:T(8,128)}, f32[3,1,64,1024]{3,2,1,0:T(8,128)S(1)}, u32[]{:S(2)}, u32[]{:S(2)}) collective-permute-start(f32[3,1,64,1024]{3,2,1,0:T(8,128)} %param.3), channel_id=1, source_target_pairs={{16,0},{32,16},{48,32},{64,48},{80,64},{96,80},{112,96},{128,112},... | collective-permute-start | bytes 2359304 | tf_op jit(solution)/shard_map/ppermute | solution.py:23
  10.8 1.0 fusion.91
  11.8 2.9 %collective-permute-start = (f32[3,1,1,1024]{3,2,1,0:T(1,128)S(1)}, f32[3,1,1,1024]{3,2,1,0:T(1,128)S(1)}, u32[]{:S(2)}, u32[]{:S(2)}) collective-permute-start(f32[3,1,1,1024]{3,2,1,0:T(1,128)S(1)} %get-tuple-element.24), channel_id=1, source_target_pairs={{0,1},{1,2},{2,3},{3,4},{4,5},{5,6},{6,7},{7,8},{8,9},{9,10},{10,1... | collective-permute-start | bytes 36872 | tf_op jit(solution)/shard_map/ppermute | solution.py:22
  14.7 3.1 %collective-permute-start.3 = (f32[3,1,1,1024]{3,2,1,0:T(1,128)S(1)}, f32[3,1,1,1024]{3,2,1,0:T(1,128)S(1)}, u32[]{:S(2)}, u32[]{:S(2)}) collective-permute-start(f32[3,1,1,1024]{3,2,1,0:T(1,128)S(1)} %get-tuple-element.25), channel_id=1, source_target_pairs={{1,0},{2,1},{3,2},{4,3},{5,4},{6,5},{7,6},{8,7},{9,8},{10,9},{11,1... | collective-permute-start | bytes 36872 | tf_op jit(solution)/shard_map/ppermute | solution.py:23
  17.8 1.0 fusion.66
  18.8 1.0 fusion.67
  19.8 1.0 fusion.68
  20.8 1.0 fusion.69
  21.7 1.0 fusion.70
  22.7 1.0 fusion.71
  23.7 0.0 copy-done
  23.8 0.0 copy-start.2
  23.8 1.3 copy-done.2
  25.1 0.1 fusion.92
  25.2 0.3 fusion.93
  25.5 0.3 fusion.16
  25.8 0.0 collective-permute-done.3
  25.9 0.0 collective-permute-done
  25.9 0.0 collective-permute-done.1
  25.9 0.1 constant_dynamic-update-slice_fusion.2
  26.0 0.1 constant_dynamic-update-slice_fusion.1
  26.0 0.0 collective-permute-done.2
  26.0 0.1 constant_dynamic-update-slice_fusion
  26.1 0.0 copy-start.3
  26.1 0.3 fusion.11
  26.4 1.2 copy-done.3
  27.7 0.3 fusion.79
  27.9 0.0 copy-start.4
  28.2 1.3 copy-done.4
  29.5 3.5 %convert_bitcast_fusion = bf16[15,1,64,1024]{3,2,0,1:T(8,128)(2,1)} fusion(bf16[1024,1024,1]{1,0,2:T(8,128)(2,1)S(1)} %copy-done.4, bf16[15,1,64,1024]{3,2,0,1:T(8,128)(2,1)S(1)} %fusion.80), kind=kOutput, calls=%fused_computation.6 | convolution fusion | flops 2014248960 | bytes 6029312 | tf_op jit(solution)/shard_map/fyzx,xv->fyzv/dot_general | solution.py:122
  33.0 6.2 %copy.154 = bf16[15,1,64,1024]{2,0,1,3:T(8,128)(2,1)} copy(bf16[15,1,64,1024]{3,2,0,1:T(8,128)(2,1)} %convert_bitcast_fusion) | data formatting | bytes 3932160 | tf_op jit(solution)/shard_map/convert_element_type | solution.py:124
  39.2 7.3 %reshape.1162 = bf16[16,2,30720]{2,1,0:T(2,128)(2,1)} reshape(bf16[1024,1,15,64]{3,2,1,0:T(8,128)(2,1)} %bitcast.264) | data formatting | bytes 3932160
  46.5 61.5 %all_to_all.21 = bf16[16,2,30720]{2,1,0:T(2,128)(2,1)} all-to-all(bf16[16,2,30720]{2,1,0:T(2,128)(2,1)} %reshape.1162), channel_id=1, replica_groups=mesh['py'=32,'pz'=16] {'pz'}, dimensions={0} | all-to-all | bytes 3932160 | tf_op jit(solution)/shard_map/all_to_all | solution.py:128
  108.0 7.5 %reshape.1163 = bf16[1024,1,15,64]{3,2,1,0:T(8,128)(2,1)} reshape(bf16[16,2,30720]{2,1,0:T(2,128)(2,1)} %all_to_all.21) | data formatting | bytes 3932160
  115.5 5.8 %copy.155 = bf16[15,1,64,1024]{3,2,0,1:T(8,128)(2,1)} copy(bf16[15,1,64,1024]{2,0,1,3:T(8,128)(2,1)} %bitcast.265) | data formatting | bytes 3932160 | tf_op jit(solution)/shard_map/all_to_all | solution.py:128
  121.2 6.1 %reshape.1156 = bf16[15,1024,64]{2,1,0:T(8,128)(2,1)} reshape(bf16[15,1,64,1024]{3,2,0,1:T(8,128)(2,1)} %copy.155) | data formatting | bytes 3932160 | tf_op jit(solution)/shard_map/wz,fyzx->fywx/dot_general | solution.py:125
  127.3 7.0 %convolution_convert_fusion = bf16[15,64,1024]{2,1,0:T(8,128)(2,1)S(1)} fusion(bf16[15,1024,64]{2,1,0:T(8,128)(2,1)} %reshape.1156, bf16[1024,1024,1]{1,0,2:T(8,128)(2,1)} %constant.58), kind=kOutput, calls=%fused_computation.7 | convolution fusion | flops 2014248960 | bytes 6029312 | tf_op jit(solution)/shard_map/wz,fyzx->fywx/dot_general | solution.py:125
  134.3 0.1 fusion.87
  134.4 0.0 copy-start.1
  134.4 7.3 %collective-permute-start.6 = (bf16[3,1,1024,64]{2,3,1,0:T(8,128)(2,1)S(1)}, bf16[3,1,1024,64]{2,3,1,0:T(8,128)(2,1)S(1)}, u32[]{:S(2)}, u32[]{:S(2)}) collective-permute-start(bf16[3,1,1024,64]{2,3,1,0:T(8,128)(2,1)S(1)} %get-tuple-element.8), channel_id=1, source_target_pairs={{16,0},{32,16},{48,32},{64,48},{80,64},{96,80},{112,96},{128,112},... | collective-permute-start | bytes 1179656 | tf_op jit(solution)/shard_map/ppermute | solution.py:23
  141.8 1.9 %collective-permute-start.5 = (bf16[3,1,1024,64]{2,3,1,0:T(8,128)(2,1)S(1)}, bf16[3,1,1024,64]{2,3,1,0:T(8,128)(2,1)S(1)}, u32[]{:S(2)}, u32[]{:S(2)}) collective-permute-start(bf16[3,1,1024,64]{2,3,1,0:T(8,128)(2,1)S(1)} %get-tuple-element.8), channel_id=1, source_target_pairs={{0,16},{16,32},{32,48},{48,64},{64,80},{80,96},{96,112},{112,128},... | collective-permute-start | bytes 1179656 | tf_op jit(solution)/shard_map/ppermute | solution.py:22
  143.7 0.0 collective-permute-start.4
  143.8 0.5 collective-permute-start.7
  144.3 0.7 collective-permute-done.4
  144.9 2.3 %collective-permute-done.7 = bf16[3,1,1024,1]{2,3,1,0:T(2,128)(2,1)S(1)} collective-permute-done((bf16[3,1,1024,1]{2,3,1,0:T(2,128)(2,1)S(1)}, bf16[3,1,1024,1]{2,3,1,0:T(2,128)(2,1)S(1)}, u32[]{:S(2)}, u32[]{:S(2)}) %collective-permute-start.7) | collective-permute-done | bytes 6176 | tf_op jit(solution)/shard_map/ppermute | solution.py:23
  147.2 3.2 %collective-permute-done.6 = bf16[3,1,1024,64]{2,3,1,0:T(8,128)(2,1)S(1)} collective-permute-done((bf16[3,1,1024,64]{2,3,1,0:T(8,128)(2,1)S(1)}, bf16[3,1,1024,64]{2,3,1,0:T(8,128)(2,1)S(1)}, u32[]{:S(2)}, u32[]{:S(2)}) %collective-permute-start.6) | collective-permute-done | bytes 393248 | tf_op jit(solution)/shard_map/ppermute | solution.py:23
  150.4 7.7 %collective-permute-done.5 = bf16[3,1,1024,64]{2,3,1,0:T(8,128)(2,1)S(1)} collective-permute-done((bf16[3,1,1024,64]{2,3,1,0:T(8,128)(2,1)S(1)}, bf16[3,1,1024,64]{2,3,1,0:T(8,128)(2,1)S(1)}, u32[]{:S(2)}, u32[]{:S(2)}) %collective-permute-start.5) | collective-permute-done | bytes 393248 | tf_op jit(solution)/shard_map/ppermute | solution.py:22
  158.1 0.4 fusion.6
  158.5 0.1 slice_select_fusion.1
  158.6 0.0 copy-done.1
  158.6 0.1 maximum_convert_fusion.1
  158.7 0.2 maximum_convert_fusion
  159.0 0.3 fusion.89
  159.3 0.6 fusion.8
  159.9 1.4 fusion.59
  161.3 0.8 fusion.38
  162.1 1.3 pad_maximum_fusion.6
  163.4 9.8 %all_to_all.22 = f32[16,1,2]{2,1,0:T(1,128)S(1)} all-to-all(f32[16,1,2]{2,1,0:T(1,128)S(1)} %broadcast_in_dim.4), channel_id=1, replica_groups=mesh['py'=32,'pz'=16] {'pz'}, dimensions={0} | all-to-all | bytes 256 | tf_op jit(solution)/shard_map/all_to_all | solution.py:36
  173.3 0.6 fusion.94
  175.1 1.0 fusion.44
  (13 shorter events, 0.4 us)
Async XLA Ops:
  0.6 23.0 %copy-start = (f32[3,1,64,1024]{3,2,1,0:T(8,128)S(1)}, f32[3,1,64,1024]{3,2,1,0:T(8,128)}, u32[]{:S(2)}) copy-start(f32[3,1,64,1024]{3,2,1,0:T(8,128)} %param.3) | copy-start | bytes 2359300
  0.6 25.3 %collective-permute-start.1 = (f32[3,1,64,1024]{3,2,1,0:T(8,128)}, f32[3,1,64,1024]{3,2,1,0:T(8,128)S(1)}, u32[]{:S(2)}, u32[]{:S(2)}) collective-permute-start(f32[3,1,64,1024]{3,2,1,0:T(8,128)} %param.3), channel_id=1, source_target_pairs={{0,16},{16,32},{32,48},{48,64},{64,80},{80,96},{96,112},{112,128},... | collective-permute-start | bytes 2359304 | tf_op jit(solution)/shard_map/ppermute | solution.py:22
  4.7 21.3 %collective-permute-start.2 = (f32[3,1,64,1024]{3,2,1,0:T(8,128)}, f32[3,1,64,1024]{3,2,1,0:T(8,128)S(1)}, u32[]{:S(2)}, u32[]{:S(2)}) collective-permute-start(f32[3,1,64,1024]{3,2,1,0:T(8,128)} %param.3), channel_id=1, source_target_pairs={{16,0},{32,16},{48,32},{64,48},{80,64},{96,80},{112,96},{128,112},... | collective-permute-start | bytes 2359304 | tf_op jit(solution)/shard_map/ppermute | solution.py:23
  11.8 14.1 %collective-permute-start = (f32[3,1,1,1024]{3,2,1,0:T(1,128)S(1)}, f32[3,1,1,1024]{3,2,1,0:T(1,128)S(1)}, u32[]{:S(2)}, u32[]{:S(2)}) collective-permute-start(f32[3,1,1,1024]{3,2,1,0:T(1,128)S(1)} %get-tuple-element.24), channel_id=1, source_target_pairs={{0,1},{1,2},{2,3},{3,4},{4,5},{5,6},{6,7},{7,8},{8,9},{9,10},{10,1... | collective-permute-start | bytes 36872 | tf_op jit(solution)/shard_map/ppermute | solution.py:22
  14.7 11.1 %collective-permute-start.3 = (f32[3,1,1,1024]{3,2,1,0:T(1,128)S(1)}, f32[3,1,1,1024]{3,2,1,0:T(1,128)S(1)}, u32[]{:S(2)}, u32[]{:S(2)}) collective-permute-start(f32[3,1,1,1024]{3,2,1,0:T(1,128)S(1)} %get-tuple-element.25), channel_id=1, source_target_pairs={{1,0},{2,1},{3,2},{4,3},{5,4},{6,5},{7,6},{8,7},{9,8},{10,9},{11,1... | collective-permute-start | bytes 36872 | tf_op jit(solution)/shard_map/ppermute | solution.py:23
  23.8 1.3 copy-start.2
  26.1 1.5 copy-start.3
  27.9 1.6 copy-start.4
  134.4 24.2 %copy-start.1 = (bf16[3,1,1024,64]{2,3,1,0:T(8,128)(2,1)}, bf16[3,1,1024,64]{2,3,1,0:T(8,128)(2,1)S(1)}, u32[]{:S(2)}) copy-start(bf16[3,1,1024,64]{2,3,1,0:T(8,128)(2,1)S(1)} %get-tuple-element.8) | copy-start | bytes 1179652
  134.4 16.0 %collective-permute-start.6 = (bf16[3,1,1024,64]{2,3,1,0:T(8,128)(2,1)S(1)}, bf16[3,1,1024,64]{2,3,1,0:T(8,128)(2,1)S(1)}, u32[]{:S(2)}, u32[]{:S(2)}) collective-permute-start(bf16[3,1,1024,64]{2,3,1,0:T(8,128)(2,1)S(1)} %get-tuple-element.8), channel_id=1, source_target_pairs={{16,0},{32,16},{48,32},{64,48},{80,64},{96,80},{112,96},{128,112},... | collective-permute-start | bytes 1179656 | tf_op jit(solution)/shard_map/ppermute | solution.py:23
  141.8 16.3 %collective-permute-start.5 = (bf16[3,1,1024,64]{2,3,1,0:T(8,128)(2,1)S(1)}, bf16[3,1,1024,64]{2,3,1,0:T(8,128)(2,1)S(1)}, u32[]{:S(2)}, u32[]{:S(2)}) collective-permute-start(bf16[3,1,1024,64]{2,3,1,0:T(8,128)(2,1)S(1)} %get-tuple-element.8), channel_id=1, source_target_pairs={{0,16},{16,32},{32,48},{48,64},{64,80},{80,96},{96,112},{112,128},... | collective-permute-start | bytes 1179656 | tf_op jit(solution)/shard_map/ppermute | solution.py:22
  143.7 1.2 collective-permute-start.4
  143.8 3.4 %collective-permute-start.7 = (bf16[3,1,1024,1]{2,3,1,0:T(2,128)(2,1)S(1)}, bf16[3,1,1024,1]{2,3,1,0:T(2,128)(2,1)S(1)}, u32[]{:S(2)}, u32[]{:S(2)}) collective-permute-start(bf16[3,1,1024,1]{2,3,1,0:T(2,128)(2,1)S(1)} %get-tuple-element.18), channel_id=1, source_target_pairs={{1,0},{2,1},{3,2},{4,3},{5,4},{6,5},{7,6},{8,7},{9,8},{10,9},{11,1... | collective-permute-start | bytes 18440 | tf_op jit(solution)/shard_map/ppermute | solution.py:23
where the time goes:
time: 177 us; the launch traced here: 176 us
  blocking collectives  71.3 us (40%)
  local copies, waits for them, and re-layouts  42 us (24%)
  starting transfers between devices  26 us (15%)
  waiting for transfers between devices  13.9 us (8%)
  matrix products  10.5 us (6%)
  other arithmetic  10.2 us (6%)
  between operations  2.21 us (1%)
    all_to_all x1, blocking collectives, body(): lax.all_to_all(along_x, 'pz', split_axis=3, concat_axis=2, tiled=True)  61.5 us
    unnamed x17, local copies, waits for them, and re-layouts  21.6 us
    ppermute x4, starting transfers between devices, extended(): lax.ppermute(initial, axis, [(b, a) for a, b in up])  17 us
    all_to_all x1, blocking collectives, copy_for_each(): return lax.all_to_all(copies, axis, split_axis=0, concat_axis=0, tiled=True)  9.84 us
    ppermute x4, starting transfers between devices, extended(): lax.ppermute(last, axis, up)  8.97 us
    ppermute x4, waiting for transfers between devices, extended(): lax.ppermute(last, axis, up)  8.38 us
    dot_general x1, matrix products, body(): jnp.einsum('wz,fyzx->fywx', table_z, lax.all_to_all(along_x, 'pz', split_...  7.04 us
    convert_element_type x1, local copies, waits for them, and re-layouts, body(): along_x = jnp.einsum('fyzx,xv->fyzv', fields, table_x, preferred_element_...  6.18 us
  transfers between devices with their start and end apart: 8, of which 4 were waited for; matrix products, arithmetic and copies ran while one was open for 4% of the time, Pallas kernels for 0%

commit v1 on v0

v1 whole, which is shorter than its diff:
```python
import math

import jax
import jax.numpy as jnp
import numpy as np
from jax import lax
from jax.experimental import pallas as pl
from jax.experimental.pallas import tpu as pltpu
from jax.sharding import PartitionSpec as P

index_pairs = ((0, 0), (1, 1), (2, 2), (0, 1), (0, 2), (1, 2))
pair_weights = (1.0, 1.0, 1.0, 2.0, 2.0, 2.0)
epsilon = 1e-06
LANES = 128


def filter_table(length):
    offsets = np.arange(length, dtype=np.int64)
    wavenumbers = np.arange(1, length // 4, dtype=np.int64)
    phase = offsets[:, None] * wavenumbers[None, :] % length
    kernel = (1.0 + 2.0 * np.cos(phase * (2.0 * math.pi / length)).sum(axis=1)) / length
    kernel = kernel.astype(np.float32)
    lagged = (offsets[:, None] - offsets[None, :]) % length
    return kernel[lagged].astype(jnp.bfloat16)


def call(kernel, out_shape, flops, moved, scratch=(), name=None, smem=()):
    def run(*args):
        specs = [
            pl.BlockSpec(memory_space=pltpu.SMEM if i in smem else pltpu.VMEM)
            for i in range(len(args))
        ]
        return pl.pallas_call(
            kernel,
            out_shape=out_shape,
            in_specs=specs,
            out_specs=jax.tree.map(lambda _: pl.BlockSpec(memory_space=pltpu.VMEM), out_shape),
            scratch_shapes=list(scratch),
            cost_estimate=pl.CostEstimate(flops=flops, bytes_accessed=moved, transcendentals=0),
            compiler_params=pltpu.CompilerParams(vmem_limit_bytes=12 * 1024 * 1024),
            name=name,
        )(*args)

    return run


def nt(a, b):
    return lax.dot_general(a, b, (((1,), (1,)), ((), ())), preferred_element_type=jnp.float32)


def send_blocks(table_ref, fields_ref, out_ref, count, depth):
    receivers, _, _ = out_ref.shape
    width = table_ref.shape[0] // receivers
    per = LANES // depth
    group = 2 * per
    full = count // per
    for first in range(0, full * per, group):
        here = min(group, full * per - first)
        got = nt(table_ref[...], fields_ref[first * depth : (first + here) * depth, :])
        got = got.astype(jnp.bfloat16)
        for j in range(here // per):
            slot = first // per + j
            block = got[:, j * LANES : (j + 1) * LANES].reshape(receivers, width, LANES)
            out_ref[:, slot * width : (slot + 1) * width, :] = block
    if count % per:
        last = fields_ref[full * per * depth : count * depth, :]
        got = nt(table_ref[...], jnp.concatenate([last, last], axis=0))
        got = got.reshape(receivers, width, LANES)
        half = width // 2
        lane = lax.broadcasted_iota(jnp.int32, (receivers, half, LANES), 2)
        block = jnp.where(lane < depth, got[:, :half, :], got[:, half:, :])
        out_ref[:, full * width :, :] = block.astype(jnp.bfloat16)


def swapped(x):
    return pltpu.roll(x.astype(jnp.float32), LANES // 2, 1).astype(x.dtype)


def gather_pair(recv_ref, slot, lines_ref, at, width):
    senders = recv_ref.shape[0]
    lane = lax.broadcasted_iota(jnp.int32, (width, LANES), 1)
    low = lane < LANES // 2
    rows = slice(slot * width, (slot + 1) * width)
    for t in range(senders // 2):
        even = recv_ref[2 * t, rows, :].astype(jnp.float32)
        odd = recv_ref[2 * t + 1, rows, :].astype(jnp.float32)
        one = jnp.where(low, even, pltpu.roll(odd, LANES // 2, 1))
        two = jnp.where(low, pltpu.roll(even, LANES // 2, 1), odd)
        cols = slice(t * LANES, (t + 1) * LANES)
        lines_ref[at * width : (at + 1) * width, cols] = one.astype(jnp.bfloat16)
        if (at + 2) * width <= lines_ref.shape[0]:
            lines_ref[(at + 1) * width : (at + 2) * width, cols] = two.astype(jnp.bfloat16)


def gather_second(recv_ref, slot, lines_ref, at, width):
    senders = recv_ref.shape[0]
    low = lax.broadcasted_iota(jnp.int32, (width, LANES), 1) < LANES // 2
    rows = slice(slot * width, (slot + 1) * width)
    for t in range(senders // 2):
        even = recv_ref[2 * t, rows, :].astype(jnp.float32)
        odd = recv_ref[2 * t + 1, rows, :].astype(jnp.float32)
        two = jnp.where(low, pltpu.roll(even, LANES // 2, 1), odd)
        cols = slice(t * LANES, (t + 1) * LANES)
        lines_ref[at * width : (at + 1) * width, cols] = two.astype(jnp.bfloat16)


def gather_single(recv_ref, slot, lines_ref, at, width):
    senders = recv_ref.shape[0]
    half = width // 2
    low = lax.broadcasted_iota(jnp.int32, (half, LANES), 1) < LANES // 2
    rows = slice(slot * width, slot * width + half)
    for t in range(senders // 2):
        even = recv_ref[2 * t, rows, :].astype(jnp.float32)
        odd = recv_ref[2 * t + 1, rows, :].astype(jnp.float32)
        top = jnp.where(low, even, pltpu.roll(odd, LANES // 2, 1))
        bottom = jnp.where(low, pltpu.roll(even, LANES // 2, 1), odd)
        cols = slice(t * LANES, (t + 1) * LANES)
        lines_ref[at * width : at * width + half, cols] = top.astype(jnp.bfloat16)
        lines_ref[at * width + half : (at + 1) * width, cols] = bottom.astype(jnp.bfloat16)


def products_kernel(table_ref, velocity_ref, out_ref, fields_ref):
    depth = velocity_ref.shape[1]
    parts = [velocity_ref[a] for a in range(3)]
    for a in range(3):
        fields_ref[a * depth : (a + 1) * depth, :] = parts[a].astype(jnp.bfloat16)
    for p, (a, b) in enumerate(index_pairs):
        at = (3 + p) * depth
        fields_ref[at : at + depth, :] = (parts[a] * parts[b]).astype(jnp.bfloat16)
    send_blocks(table_ref, fields_ref, out_ref, 9, depth)


def strain(gradients):
    strain_parts = [0.5 * (gradients[b][a] + gradients[a][b]) for a, b in index_pairs]
    squares_sum = pair_weights[0] * strain_parts[0] * strain_parts[0]
    for weight, part_value in zip(pair_weights[1:], strain_parts[1:]):
        squares_sum = squares_sum + weight * part_value * part_value
    return (strain_parts, jnp.sqrt(2.0 * squares_sum))


def slopes(center, below, above, first, last):
    rows, length = center.shape
    row = lax.broadcasted_iota(jnp.int32, center.shape, 0)
    along = (pltpu.roll(center, length - 1, 1) - pltpu.roll(center, 1, 1)) * 0.5
    following = jnp.where(row == rows - 1, last, pltpu.roll(center, rows - 1, 0))
    previous = jnp.where(row == 0, first, pltpu.roll(center, 1, 0))
    return (along, (above - below) * 0.5, (following - previous) * 0.5)


def strain_kernel(
    table_ref, velocity_ref, below_ref, above_ref, first_ref, last_ref, out_ref, magnitude_ref, fields_ref
):
    depth = velocity_ref.shape[1]
    gradients = [
        slopes(velocity_ref[a], below_ref[a], above_ref[a], first_ref[a], last_ref[a])
        for a in range(3)
    ]
    strain_parts, magnitude = strain(gradients)
    magnitude_ref[...] = magnitude
    for p, part_value in enumerate(strain_parts):
        fields_ref[p * depth : (p + 1) * depth, :] = (magnitude * part_value).astype(jnp.bfloat16)
    send_blocks(table_ref, fields_ref, out_ref, 6, depth)


def smooth_kernel(table_ref, recv_ref, smooth_ref, first_ref, last_ref, lines_ref):
    width = smooth_ref.shape[1]
    gather_pair(recv_ref, 0, lines_ref, 0, width)
    gather_pair(recv_ref, 1, lines_ref, 2, width)
    got = nt(lines_ref[...], table_ref[...]).astype(jnp.bfloat16)
    for a in range(3):
        smooth_ref[a] = got[a * width : (a + 1) * width, :]
        first_ref[a] = got[a * width : a * width + 1, :]
        last_ref[a] = got[(a + 1) * width - 1 : (a + 1) * width, :]


def leonard_kernel(table_ref, recv_ref, smooth_ref, leonard_ref, lines_ref):
    width = smooth_ref.shape[1]
    gather_second(recv_ref, 1, lines_ref, 0, width)
    gather_pair(recv_ref, 2, lines_ref, 1, width)
    gather_pair(recv_ref, 3, lines_ref, 3, width)
    gather_single(recv_ref, 4, lines_ref, 5, width)
    got = nt(lines_ref[...], table_ref[...]).astype(jnp.bfloat16)
    for p, (a, b) in enumerate(index_pairs):
        product = smooth_ref[a].astype(jnp.float32) * smooth_ref[b].astype(jnp.float32)
        leonard_ref[p] = got[p * width : (p + 1) * width, :].astype(jnp.float32) - product


def model_kernel(smooth_ref, below_ref, above_ref, first_ref, last_ref, model_ref):
    gradients = []
    for a in range(3):
        arrays = [
            ref[a].astype(jnp.float32)
            for ref in (smooth_ref, below_ref, above_ref, first_ref, last_ref)
        ]
        along, across, between = slopes(*arrays)
        gradients.append((between, across, along))
    strain_parts, magnitude = strain(gradients)
    for p, part_value in enumerate(strain_parts):
        model_ref[p] = 4.0 * magnitude * part_value


def sums_kernel(table_ref, recv_ref, leonard_ref, model_ref, out_ref, lines_ref):
    width = leonard_ref.shape[1]
    for j in range(3):
        gather_pair(recv_ref, j, lines_ref, 2 * j, width)
    got = nt(lines_ref[...], table_ref[...]).astype(jnp.bfloat16)
    numerator = jnp.zeros(leonard_ref.shape[1:], jnp.float32)
    denominator = jnp.zeros(leonard_ref.shape[1:], jnp.float32)
    for p, weight in enumerate(pair_weights):
        model_term = got[p * width : (p + 1) * width, :].astype(jnp.float32) - model_ref[p]
        numerator = numerator + weight * leonard_ref[p] * model_term
        denominator = denominator + weight * model_term * model_term

    def lanes(x):
        x = x.reshape(width // 8, 8, x.shape[1]).sum(axis=0)
        total = x[:, :LANES]
        for at in range(LANES, x.shape[1], LANES):
            total = total + x[:, at : at + LANES]
        return total

    pair = jnp.concatenate([lanes(numerator), lanes(denominator)], axis=0)
    out_ref[...] = jnp.broadcast_to(pair, out_ref.shape)


def viscosity_kernel(cells, sums_ref, magnitude_ref, out_ref):
    total = sums_ref[...].sum(axis=0)
    numerator = jnp.sum(total[:8, :])
    denominator = jnp.sum(total[8:, :])
    down = jnp.full((8, LANES), 2.0 * (denominator / cells + epsilon), jnp.float32)
    coefficient = (jnp.full((8, LANES), numerator / cells, jnp.float32) / down)[:1, :1]
    out_ref[...] = magnitude_ref[...] * coefficient


def body(velocity):
    _, _, depth, nx = velocity.shape
    parts = lax.axis_size("pz")
    rows = lax.axis_size("py")
    nz = depth * parts
    width = nx // parts
    f32, bf16 = jnp.float32, jnp.bfloat16
    table_x = filter_table(nx)
    table_z = filter_table(nz)
    lanes_x = jnp.asarray(np.ascontiguousarray(table_x.T))
    lanes_z = lanes_x if np.array_equal(table_x.T, table_z) else jnp.asarray(table_z)
    up = [(i, i + 1) for i in range(rows - 1)]
    down = [(b, a) for a, b in up]
    around = [(i, (i + 1) % parts) for i in range(parts)]
    back = [(b, a) for a, b in around]
    velocity = velocity.reshape(3, depth, nx)

    send = call(
        products_kernel,
        jax.ShapeDtypeStruct((parts, 9 * width // 2, LANES), bf16),
        2 * 9 * depth * nx * nx,
        12 * depth * nx + 2 * nx * nx,
        [pltpu.VMEM((9 * depth, nx), bf16)],
        "products",
    )(lanes_x, velocity)
    received = lax.all_to_all(send, "pz", 0, 0, tiled=True)

    below = lax.ppermute(velocity, "py", up)
    above = lax.ppermute(velocity, "py", down)
    first = lax.ppermute(velocity[:, -1:], "pz", around)
    last = lax.ppermute(velocity[:, :1], "pz", back)
    send_strain, magnitude = call(
        strain_kernel,
        (
            jax.ShapeDtypeStruct((parts, 3 * width, LANES), bf16),
            jax.ShapeDtypeStruct((depth, nx), f32),
        ),
        2 * 6 * depth * nx * nx,
        36 * depth * nx + 2 * nx * nx,
        [pltpu.VMEM((6 * depth, nx), bf16)],
        "strain",
    )(lanes_x, velocity, below, above, first, last)
    received_strain = lax.all_to_all(send_strain, "pz", 0, 0, tiled=True)

    edge = jax.ShapeDtypeStruct((3, 1, nz), bf16)
    smooth, smooth_first, smooth_last = call(
        smooth_kernel,
        (jax.ShapeDtypeStruct((3, width, nz), bf16), edge, edge),
        2 * 4 * width * nz * nz,
        2 * nz * nz,
        [pltpu.VMEM((4 * width, nz), bf16)],
        "smooth",
    )(lanes_z, received)
    smooth_below = lax.ppermute(smooth, "py", up)
    smooth_above = lax.ppermute(smooth, "py", down)
    first_hat = lax.ppermute(smooth_last, "pz", around)
    last_hat = lax.ppermute(smooth_first, "pz", back)
    leonard = call(
        leonard_kernel,
        jax.ShapeDtypeStruct((6, width, nz), f32),
        2 * 6 * width * nz * nz,
        24 * width * nz + 2 * nz * nz,
        [pltpu.VMEM((6 * width, nz), bf16)],
        "leonard",
    )(lanes_z, received, smooth)
    model = call(
        model_kernel,
        jax.ShapeDtypeStruct((6, width, nz), f32),
        100 * width * nz,
        24 * width * nz,
        (),
        "model",
    )(smooth, smooth_below, smooth_above, first_hat, last_hat)
    sums = call(
        sums_kernel,
        jax.ShapeDtypeStruct((parts, 16, LANES), f32),
        2 * 6 * width * nz * nz,
        48 * width * nz + 2 * nz * nz,
        [pltpu.VMEM((6 * width, nz), bf16)],
        "sums",
    )(lanes_z, received_strain, leonard, model)
    totals = lax.all_to_all(sums, "pz", 0, 0, tiled=True)
    cells = nx * nz
    nu_t = call(
        lambda *refs: viscosity_kernel(cells, *refs),
        jax.ShapeDtypeStruct((depth, nx), f32),
        2 * depth * nx,
        8 * depth * nx,
        (),
        "viscosity",
    )(totals, magnitude)
    filtered_velocity = jnp.transpose(smooth, (0, 2, 1))
    return (nu_t[None], filtered_velocity[:, None])


def solution(mesh):
    in_specs = (P(None, "py", "pz", None),)
    out_specs = (P("py", "pz", None), P(None, "py", None, "pz"))
    return jax.shard_map(body, mesh=mesh, in_specs=in_specs, out_specs=out_specs, check_vma=False)
```

time: 177 us -> 103 us (0.58)
  the two profiles are of different devices: /device:TPU:1 before, /device:TPU:33 now
where the time goes in v1:
time: 103 us
  starting transfers between devices  34.8 us (34%)
  waiting for transfers between devices  27.6 us (27%)
  blocking collectives  15.9 us (15%)
  local copies, waits for them, and re-layouts  12.9 us (13%)
  Pallas kernels  10.6 us (10%)
    ppermute x1, waiting for transfers between devices, body(): last = lax.ppermute(velocity[:, :1], 'pz', back)  19.2 us
    all_to_all x1, blocking collectives, body(): totals = lax.all_to_all(sums, 'pz', 0, 0, tiled=True)  15.9 us
    unnamed x24, local copies, waits for them, and re-layouts  11.9 us
    all_to_all x1, starting transfers between devices, body(): received = lax.all_to_all(send, 'pz', 0, 0, tiled=True)  11.1 us
    pallas_call x7, Pallas kernels, run(): pl.pallas_call(kernel, out_shape=out_shape, in_specs=specs, out_specs=jax...  10.6 us
    all_to_all x1, starting transfers between devices, body(): received_strain = lax.all_to_all(send_strain, 'pz', 0, 0, tiled=True)  8.02 us
    ppermute x1, waiting for transfers between devices, body(): last_hat = lax.ppermute(smooth_first, 'pz', back)  4.32 us
    ppermute x1, starting transfers between devices, body(): above = lax.ppermute(velocity, 'py', down)  4.29 us
  transfers between devices with their start and end apart: 10, of which 5 were waited for; matrix products, arithmetic and copies ran while one was open for 1% of the time, Pallas kernels for 5%

profile of v1, /device:TPU:33, one launch (start us, length us, event | category | flops | bytes accessed | tf_op | source)
XLA Modules:
  0.0 102.5 jit_solution(1847420455569794691)
XLA Ops:
  0.6 0.0 copy-start
  0.6 1.6 %copy-done = bf16[1024,1024]{1,0:T(8,128)(2,1)S(1)} copy-done((bf16[1024,1024]{1,0:T(8,128)(2,1)S(1)}, bf16[1024,1024]{1,0:T(8,128)(2,1)}, u32[]{:S(2)}) %copy-start) | copy-done | bytes 2097176
  2.2 0.0 copy-start.9
  2.2 1.1 %copy-done.9 = f32[3,1,64,1024]{3,2,1,0:T(8,128)S(1)} copy-done((f32[3,1,64,1024]{3,2,1,0:T(8,128)S(1)}, f32[3,1,64,1024]{3,2,1,0:T(8,128)}, u32[]{:S(2)}) %copy-start.9) | copy-done | bytes 786456
  3.4 1.8 %products.1 = bf16[16,288,128]{2,1,0:T(8,128)(2,1)S(1)} custom-call(bf16[1024,1024]{1,0:T(8,128)(2,1)S(1)} %copy-done, f32[3,64,1024]{2,1,0:T(8,128)S(1)} %bitcast.11), custom_call_target="tpu_custom_call" | custom-call | flops 1207959552 | bytes 2883584 | tf_op jit(solution)/shard_map/products/pallas_call | solution.py:33
  5.2 0.0 copy-start.8
  5.2 1.0 %copy-done.8 = bf16[16,288,128]{2,1,0:T(8,128)(2,1)} copy-done((bf16[16,288,128]{2,1,0:T(8,128)(2,1)}, bf16[16,288,128]{2,1,0:T(8,128)(2,1)S(1)}, u32[]{:S(2)}) %copy-start.8) | copy-done | bytes 1179672
  6.2 0.0 copy-start.1
  6.2 11.1 %all-to-all-start.1 = ((bf16[16,288,128]{2,1,0:T(8,128)(2,1)}), bf16[16,288,128]{2,1,0:T(8,128)(2,1)S(1)}, u32[]{:S(2)}, u32[]{:S(2)}) async-start(bf16[16,288,128]{2,1,0:T(8,128)(2,1)} %copy-done.8), calls=%async_computation.1 | async-start | bytes 2359296 | tf_op jit(solution)/shard_map/all_to_all | solution.py:259
  17.4 4.3 %collective-permute-start.1 = (f32[3,64,1024]{2,1,0:T(8,128)}, f32[3,64,1024]{2,1,0:T(8,128)S(1)}, u32[]{:S(2)}, u32[]{:S(2)}) collective-permute-start(f32[3,64,1024]{2,1,0:T(8,128)} %bitcast.8), channel_id=1, source_target_pairs={{16,0},{32,16},{48,32},{64,48},{80,64},{96,80},{112,96},{128,112},... | collective-permute-start | bytes 2359304 | tf_op jit(solution)/shard_map/ppermute | solution.py:262
  21.7 1.9 %collective-permute-start = (f32[3,64,1024]{2,1,0:T(8,128)}, f32[3,64,1024]{2,1,0:T(8,128)S(1)}, u32[]{:S(2)}, u32[]{:S(2)}) collective-permute-start(f32[3,64,1024]{2,1,0:T(8,128)} %bitcast.9), channel_id=1, source_target_pairs={{0,16},{16,32},{32,48},{48,64},{64,80},{80,96},{96,112},{112,128},... | collective-permute-start | bytes 2359304 | tf_op jit(solution)/shard_map/ppermute | solution.py:261
  23.6 1.0 fusion
  24.6 0.4 collective-permute-start.3
  24.9 1.5 %collective-permute-start.2 = (f32[3,1,1024]{2,1,0:T(1,128)S(1)}, f32[3,1,1024]{2,1,0:T(1,128)S(1)}, u32[]{:S(2)}, u32[]{:S(2)}) collective-permute-start(f32[3,1,1024]{2,1,0:T(1,128)S(1)} %get-tuple-element.15), channel_id=1, source_target_pairs={{0,1},{1,2},{2,3},{3,4},{4,5},{5,6},{6,7},{7,8},{8,9},{9,10},{10,1... | collective-permute-start | bytes 36872 | tf_op jit(solution)/shard_map/ppermute | solution.py:263
  26.5 19.2 %collective-permute-done.3.last_ref = f32[3,1,1024]{2,1,0:T(1,128)S(1)} collective-permute-done((f32[3,1,1024]{2,1,0:T(1,128)S(1)}, f32[3,1,1024]{2,1,0:T(1,128)S(1)}, u32[]{:S(2)}, u32[]{:S(2)}) %collective-permute-start.3) | collective-permute-done | bytes 12320 | tf_op jit(solution)/shard_map/ppermute | solution.py:264
  45.7 0.0 collective-permute-done.2.first_ref
  45.7 0.0 collective-permute-done.1.above_ref
  45.7 0.2 collective-permute-done.below_ref
  45.9 0.0 copy-done.1
  45.9 0.0 copy-start.10
  45.9 1.1 %copy-done.10 = f32[3,1,64,1024]{3,2,1,0:T(8,128)S(1)} copy-done((f32[3,1,64,1024]{3,2,1,0:T(8,128)S(1)}, f32[3,1,64,1024]{3,2,1,0:T(8,128)}, u32[]{:S(2)}) %copy-start.10) | copy-done | bytes 786456
  47.0 1.8 %strain.1 = (bf16[16,192,128]{2,1,0:T(8,128)(2,1)S(1)}, f32[64,1024]{1,0:T(8,128)S(1)}) custom-call(bf16[1024,1024]{1,0:T(8,128)(2,1)S(1)} %copy-done.1, f32[3,64,1024]{2,1,0:T(8,128)S(1)} %bitcast.12, f32[3,64,1024]{2,1,0:T(8,128)S(1)} %collective-permute-done.below_ref, f32[3,64,1024]{2,1,0:T(8,128)S(1)} %collective-permute-done.1.above_ref, ...), custom_call_target="tpu_custom_call" | custom-call | flops 805306368 | bytes 4456448 | tf_op jit(solution)/shard_map/strain/pallas_call | solution.py:33
  48.8 0.0 copy-start.11
  48.8 0.9 copy-done.11
  49.7 0.0 all-to-all-done.1.recv_ref
  49.7 8.0 %all-to-all-start = ((bf16[16,192,128]{2,1,0:T(8,128)(2,1)}), bf16[16,192,128]{2,1,0:T(8,128)(2,1)}, u32[]{:S(2)}, u32[]{:S(2)}) async-start(bf16[16,192,128]{2,1,0:T(8,128)(2,1)} %copy-done.11), calls=%async_computation | async-start | bytes 1572864 | tf_op jit(solution)/shard_map/all_to_all | solution.py:276
  57.7 1.5 %smooth.1 = (bf16[3,64,1024]{2,1,0:T(8,128)(2,1)}, bf16[3,1,1024]{2,1,0:T(2,128)(2,1)S(1)}, bf16[3,1,1024]{2,1,0:T(2,128)(2,1)S(1)}) custom-call(bf16[1024,1024]{1,0:T(8,128)(2,1)S(1)} %copy-done.1, bf16[16,288,128]{2,1,0:T(8,128)(2,1)S(1)} %all-to-all-done.1.recv_ref), custom_call_target="tpu_custom_call" | custom-call | flops 536870912 | bytes 2097152 | tf_op jit(solution)/shard_map/smooth/pallas_call | solution.py:33
  59.2 2.2 %collective-permute-start.5 = (bf16[3,64,1024]{2,1,0:T(8,128)(2,1)}, bf16[3,64,1024]{2,1,0:T(8,128)(2,1)S(1)}, u32[]{:S(2)}, u32[]{:S(2)}) collective-permute-start(bf16[3,64,1024]{2,1,0:T(8,128)(2,1)} %get-tuple-element.8.smooth_ref), channel_id=1, source_target_pairs={{16,0},{32,16},{48,32},{64,48},{80,64},{96,80},{112,96},{128,112},... | collective-permute-start | bytes 1179656 | tf_op jit(solution)/shard_map/ppermute | solution.py:288
  61.4 3.1 %collective-permute-start.4 = (bf16[3,64,1024]{2,1,0:T(8,128)(2,1)}, bf16[3,64,1024]{2,1,0:T(8,128)(2,1)S(1)}, u32[]{:S(2)}, u32[]{:S(2)}) collective-permute-start(bf16[3,64,1024]{2,1,0:T(8,128)(2,1)} %get-tuple-element.8.smooth_ref), channel_id=1, source_target_pairs={{0,16},{16,32},{32,48},{48,64},{64,80},{80,96},{96,112},{112,128},... | collective-permute-start | bytes 1179656 | tf_op jit(solution)/shard_map/ppermute | solution.py:287
  64.5 2.2 %collective-permute-start.6 = (bf16[3,1,1024]{2,1,0:T(2,128)(2,1)S(1)}, bf16[3,1,1024]{2,1,0:T(2,128)(2,1)S(1)}, u32[]{:S(2)}, u32[]{:S(2)}) collective-permute-start(bf16[3,1,1024]{2,1,0:T(2,128)(2,1)S(1)} %get-tuple-element.9), channel_id=1, source_target_pairs={{0,1},{1,2},{2,3},{3,4},{4,5},{5,6},{6,7},{7,8},{8,9},{9,10},{10,1... | collective-permute-start | bytes 18440 | tf_op jit(solution)/shard_map/ppermute | solution.py:289
  66.7 0.0 collective-permute-start.7
  66.7 0.0 copy-start.6
  66.7 1.0 copy-done.6
  67.7 0.0 copy-start.7
  67.7 1.1 %leonard.1.leonard_ref = f32[6,64,1024]{2,1,0:T(8,128)S(1)} custom-call(bf16[1024,1024]{1,0:T(8,128)(2,1)S(1)} %copy-done.1, bf16[16,288,128]{2,1,0:T(8,128)(2,1)S(1)} %all-to-all-done.1.recv_ref, bf16[3,64,1024]{2,1,0:T(8,128)(2,1)S(1)} %copy-done.6), custom_call_target="tpu_custom_call" | custom-call | flops 805306368 | bytes 3670016 | tf_op jit(solution)/shard_map/leonard/pallas_call | solution.py:33
  68.9 0.0 copy-start.2
  68.9 1.2 %copy-done.2 = f32[6,64,1024]{2,1,0:T(8,128)} copy-done((f32[6,64,1024]{2,1,0:T(8,128)}, f32[6,64,1024]{2,1,0:T(8,128)S(1)}, u32[]{:S(2)}) %copy-start.2) | copy-done | bytes 1572888
  70.0 3.3 %collective-permute-done.6.first_ref = bf16[3,1,1024]{2,1,0:T(2,128)(2,1)S(1)} collective-permute-done((bf16[3,1,1024]{2,1,0:T(2,128)(2,1)S(1)}, bf16[3,1,1024]{2,1,0:T(2,128)(2,1)S(1)}, u32[]{:S(2)}, u32[]{:S(2)}) %collective-permute-start.6) | collective-permute-done | bytes 6176 | tf_op jit(solution)/shard_map/ppermute | solution.py:289
  73.3 4.3 %collective-permute-done.7.last_ref = bf16[3,1,1024]{2,1,0:T(2,128)(2,1)S(1)} collective-permute-done((bf16[3,1,1024]{2,1,0:T(2,128)(2,1)S(1)}, bf16[3,1,1024]{2,1,0:T(2,128)(2,1)S(1)}, u32[]{:S(2)}, u32[]{:S(2)}) %collective-permute-start.7) | collective-permute-done | bytes 6176 | tf_op jit(solution)/shard_map/ppermute | solution.py:290
  77.7 0.0 collective-permute-done.5.above_ref
  77.7 0.0 collective-permute-done.4.below_ref
  77.7 0.0 copy-done.7
  77.7 1.0 %model.1.model_ref = f32[6,64,1024]{2,1,0:T(8,128)S(1)} custom-call(bf16[3,64,1024]{2,1,0:T(8,128)(2,1)S(1)} %copy-done.7, bf16[3,64,1024]{2,1,0:T(8,128)(2,1)S(1)} %collective-permute-done.4.below_ref, bf16[3,64,1024]{2,1,0:T(8,128)(2,1)S(1)} %collective-permute-done.5.above_ref, bf16[3,1,1024]{2,1,0:T(2,128)(2,1)S(1)} %collective-permute-done.6.first_ref, ...), custom_call_target="tpu_custom_call" | custom-call | flops 6553600 | bytes 1572864 | tf_op jit(solution)/shard_map/model/pallas_call | solution.py:33
  78.7 0.0 copy-start.4
  78.7 1.1 %copy-done.4 = f32[6,64,1024]{2,1,0:T(8,128)} copy-done((f32[6,64,1024]{2,1,0:T(8,128)}, f32[6,64,1024]{2,1,0:T(8,128)S(1)}, u32[]{:S(2)}) %copy-start.4) | copy-done | bytes 1572888
  79.9 0.6 all-to-all-done.recv_ref
  80.5 0.0 copy-start.3
  80.5 1.4 %copy-done.3 = f32[6,64,1024]{2,1,0:T(8,128)S(1)} copy-done((f32[6,64,1024]{2,1,0:T(8,128)S(1)}, f32[6,64,1024]{2,1,0:T(8,128)}, u32[]{:S(2)}) %copy-start.3) | copy-done | bytes 1572888
  81.9 0.0 copy-start.5
  81.9 1.4 %copy-done.5 = f32[6,64,1024]{2,1,0:T(8,128)S(1)} copy-done((f32[6,64,1024]{2,1,0:T(8,128)S(1)}, f32[6,64,1024]{2,1,0:T(8,128)}, u32[]{:S(2)}) %copy-start.5) | copy-done | bytes 1572888
  83.3 2.4 %sums.1 = f32[16,16,128]{2,1,0:T(8,128)S(1)} custom-call(bf16[1024,1024]{1,0:T(8,128)(2,1)S(1)} %copy-done.1, bf16[16,192,128]{2,1,0:T(8,128)(2,1)} %all-to-all-done.recv_ref, f32[6,64,1024]{2,1,0:T(8,128)S(1)} %copy-done.3, f32[6,64,1024]{2,1,0:T(8,128)S(1)} %copy-done.5), custom_call_target="tpu_custom_call" | custom-call | flops 805306368 | bytes 5242880 | tf_op jit(solution)/shard_map/sums/pallas_call | solution.py:33
  85.8 15.9 %all_to_all.15.refs_0_ = f32[16,16,128]{2,1,0:T(8,128)S(1)} all-to-all(f32[16,16,128]{2,1,0:T(8,128)S(1)} %sums.1), channel_id=1, replica_groups=mesh['py'=32,'pz'=16] {'pz'}, dimensions={0} | all-to-all | bytes 262144 | tf_op jit(solution)/shard_map/all_to_all | solution.py:315
  101.6 0.9 viscosity.1
Async XLA Ops:
  0.6 1.6 %copy-start = (bf16[1024,1024]{1,0:T(8,128)(2,1)S(1)}, bf16[1024,1024]{1,0:T(8,128)(2,1)}, u32[]{:S(2)}) copy-start(bf16[1024,1024]{1,0:T(8,128)(2,1)} %constant.2.clone.table_ref) | copy-start | bytes 6291460
  2.2 1.1 %copy-start.9 = (f32[3,1,64,1024]{3,2,1,0:T(8,128)S(1)}, f32[3,1,64,1024]{3,2,1,0:T(8,128)}, u32[]{:S(2)}) copy-start(f32[3,1,64,1024]{3,2,1,0:T(8,128)} %param.2) | copy-start | bytes 2359300
  5.2 1.1 %copy-start.8 = (bf16[16,288,128]{2,1,0:T(8,128)(2,1)}, bf16[16,288,128]{2,1,0:T(8,128)(2,1)S(1)}, u32[]{:S(2)}) copy-start(bf16[16,288,128]{2,1,0:T(8,128)(2,1)S(1)} %products.1) | copy-start | bytes 3538948
  6.2 39.6 %copy-start.1 = (bf16[1024,1024]{1,0:T(8,128)(2,1)S(1)}, bf16[1024,1024]{1,0:T(8,128)(2,1)}, u32[]{:S(2)}) copy-start(bf16[1024,1024]{1,0:T(8,128)(2,1)} %constant.2.clone.table_ref) | copy-start | bytes 6291460
  6.2 43.5 %all-to-all-start.1 = ((bf16[16,288,128]{2,1,0:T(8,128)(2,1)}), bf16[16,288,128]{2,1,0:T(8,128)(2,1)S(1)}, u32[]{:S(2)}, u32[]{:S(2)}) async-start(bf16[16,288,128]{2,1,0:T(8,128)(2,1)} %copy-done.8), calls=%async_computation.1 | async-start | bytes 2359296 | tf_op jit(solution)/shard_map/all_to_all | solution.py:259
  17.4 28.3 %collective-permute-start.1 = (f32[3,64,1024]{2,1,0:T(8,128)}, f32[3,64,1024]{2,1,0:T(8,128)S(1)}, u32[]{:S(2)}, u32[]{:S(2)}) collective-permute-start(f32[3,64,1024]{2,1,0:T(8,128)} %bitcast.8), channel_id=1, source_target_pairs={{16,0},{32,16},{48,32},{64,48},{80,64},{96,80},{112,96},{128,112},... | collective-permute-start | bytes 2359304 | tf_op jit(solution)/shard_map/ppermute | solution.py:262
  21.7 24.2 %collective-permute-start = (f32[3,64,1024]{2,1,0:T(8,128)}, f32[3,64,1024]{2,1,0:T(8,128)S(1)}, u32[]{:S(2)}, u32[]{:S(2)}) collective-permute-start(f32[3,64,1024]{2,1,0:T(8,128)} %bitcast.9), channel_id=1, source_target_pairs={{0,16},{16,32},{32,48},{48,64},{64,80},{80,96},{96,112},{112,128},... | collective-permute-start | bytes 2359304 | tf_op jit(solution)/shard_map/ppermute | solution.py:261
  24.6 21.1 %collective-permute-start.3 = (f32[3,1,1024]{2,1,0:T(1,128)S(1)}, f32[3,1,1024]{2,1,0:T(1,128)S(1)}, u32[]{:S(2)}, u32[]{:S(2)}) collective-permute-start(f32[3,1,1024]{2,1,0:T(1,128)S(1)} %get-tuple-element.14), channel_id=1, source_target_pairs={{1,0},{2,1},{3,2},{4,3},{5,4},{6,5},{7,6},{8,7},{9,8},{10,9},{11,1... | collective-permute-start | bytes 36872 | tf_op jit(solution)/shard_map/ppermute | solution.py:264
  24.9 20.7 %collective-permute-start.2 = (f32[3,1,1024]{2,1,0:T(1,128)S(1)}, f32[3,1,1024]{2,1,0:T(1,128)S(1)}, u32[]{:S(2)}, u32[]{:S(2)}) collective-permute-start(f32[3,1,1024]{2,1,0:T(1,128)S(1)} %get-tuple-element.15), channel_id=1, source_target_pairs={{0,1},{1,2},{2,3},{3,4},{4,5},{5,6},{6,7},{7,8},{8,9},{9,10},{10,1... | collective-permute-start | bytes 36872 | tf_op jit(solution)/shard_map/ppermute | solution.py:263
  45.9 1.1 %copy-start.10 = (f32[3,1,64,1024]{3,2,1,0:T(8,128)S(1)}, f32[3,1,64,1024]{3,2,1,0:T(8,128)}, u32[]{:S(2)}) copy-start(f32[3,1,64,1024]{3,2,1,0:T(8,128)} %param.2) | copy-start | bytes 2359300
  48.8 0.9 copy-start.11
  49.7 30.8 %all-to-all-start = ((bf16[16,192,128]{2,1,0:T(8,128)(2,1)}), bf16[16,192,128]{2,1,0:T(8,128)(2,1)}, u32[]{:S(2)}, u32[]{:S(2)}) async-start(bf16[16,192,128]{2,1,0:T(8,128)(2,1)} %copy-done.11), calls=%async_computation | async-start | bytes 1572864 | tf_op jit(solution)/shard_map/all_to_all | solution.py:276
  59.2 18.4 %collective-permute-start.5 = (bf16[3,64,1024]{2,1,0:T(8,128)(2,1)}, bf16[3,64,1024]{2,1,0:T(8,128)(2,1)S(1)}, u32[]{:S(2)}, u32[]{:S(2)}) collective-permute-start(bf16[3,64,1024]{2,1,0:T(8,128)(2,1)} %get-tuple-element.8.smooth_ref), channel_id=1, source_target_pairs={{16,0},{32,16},{48,32},{64,48},{80,64},{96,80},{112,96},{128,112},... | collective-permute-start | bytes 1179656 | tf_op jit(solution)/shard_map/ppermute | solution.py:288
  61.4 16.3 %collective-permute-start.4 = (bf16[3,64,1024]{2,1,0:T(8,128)(2,1)}, bf16[3,64,1024]{2,1,0:T(8,128)(2,1)S(1)}, u32[]{:S(2)}, u32[]{:S(2)}) collective-permute-start(bf16[3,64,1024]{2,1,0:T(8,128)(2,1)} %get-tuple-element.8.smooth_ref), channel_id=1, source_target_pairs={{0,16},{16,32},{32,48},{48,64},{64,80},{80,96},{96,112},{112,128},... | collective-permute-start | bytes 1179656 | tf_op jit(solution)/shard_map/ppermute | solution.py:287
  64.5 8.8 %collective-permute-start.6 = (bf16[3,1,1024]{2,1,0:T(2,128)(2,1)S(1)}, bf16[3,1,1024]{2,1,0:T(2,128)(2,1)S(1)}, u32[]{:S(2)}, u32[]{:S(2)}) collective-permute-start(bf16[3,1,1024]{2,1,0:T(2,128)(2,1)S(1)} %get-tuple-element.9), channel_id=1, source_target_pairs={{0,1},{1,2},{2,3},{3,4},{4,5},{5,6},{6,7},{7,8},{8,9},{9,10},{10,1... | collective-permute-start | bytes 18440 | tf_op jit(solution)/shard_map/ppermute | solution.py:289
  66.7 10.9 %collective-permute-start.7 = (bf16[3,1,1024]{2,1,0:T(2,128)(2,1)S(1)}, bf16[3,1,1024]{2,1,0:T(2,128)(2,1)S(1)}, u32[]{:S(2)}, u32[]{:S(2)}) collective-permute-start(bf16[3,1,1024]{2,1,0:T(2,128)(2,1)S(1)} %get-tuple-element.10), channel_id=1, source_target_pairs={{1,0},{2,1},{3,2},{4,3},{5,4},{6,5},{7,6},{8,7},{9,8},{10,9},{11,1... | collective-permute-start | bytes 18440 | tf_op jit(solution)/shard_map/ppermute | solution.py:290
  66.7 1.0 copy-start.6
  67.7 9.9 %copy-start.7 = (bf16[3,64,1024]{2,1,0:T(8,128)(2,1)S(1)}, bf16[3,64,1024]{2,1,0:T(8,128)(2,1)}, u32[]{:S(2)}) copy-start(bf16[3,64,1024]{2,1,0:T(8,128)(2,1)} %get-tuple-element.8.smooth_ref) | copy-start | bytes 1179652
  68.9 1.2 %copy-start.2 = (f32[6,64,1024]{2,1,0:T(8,128)}, f32[6,64,1024]{2,1,0:T(8,128)S(1)}, u32[]{:S(2)}) copy-start(f32[6,64,1024]{2,1,0:T(8,128)S(1)} %leonard.1.leonard_ref) | copy-start | bytes 4718596
  78.7 1.1 %copy-start.4 = (f32[6,64,1024]{2,1,0:T(8,128)}, f32[6,64,1024]{2,1,0:T(8,128)S(1)}, u32[]{:S(2)}) copy-start(f32[6,64,1024]{2,1,0:T(8,128)S(1)} %model.1.model_ref) | copy-start | bytes 4718596
  80.5 1.4 %copy-start.3 = (f32[6,64,1024]{2,1,0:T(8,128)S(1)}, f32[6,64,1024]{2,1,0:T(8,128)}, u32[]{:S(2)}) copy-start(f32[6,64,1024]{2,1,0:T(8,128)} %copy-done.2) | copy-start | bytes 4718596
  81.9 1.4 %copy-start.5 = (f32[6,64,1024]{2,1,0:T(8,128)S(1)}, f32[6,64,1024]{2,1,0:T(8,128)}, u32[]{:S(2)}) copy-start(f32[6,64,1024]{2,1,0:T(8,128)} %copy-done.4) | copy-start | bytes 4718596

commit v2 on v1

v2 whole, which is shorter than its diff:
```python
import math

import jax
import jax.numpy as jnp
import numpy as np
from jax import lax
from jax.experimental import pallas as pl
from jax.experimental.pallas import tpu as pltpu
from jax.sharding import PartitionSpec as P

index_pairs = ((0, 0), (1, 1), (2, 2), (0, 1), (0, 2), (1, 2))
pair_weights = (1.0, 1.0, 1.0, 2.0, 2.0, 2.0)
epsilon = 1e-06
LANES = 128


def filter_table(length):
    offsets = np.arange(length, dtype=np.int64)
    wavenumbers = np.arange(1, length // 4, dtype=np.int64)
    phase = offsets[:, None] * wavenumbers[None, :] % length
    kernel = (1.0 + 2.0 * np.cos(phase * (2.0 * math.pi / length)).sum(axis=1)) / length
    kernel = kernel.astype(np.float32)
    lagged = (offsets[:, None] - offsets[None, :]) % length
    return kernel[lagged].astype(jnp.bfloat16)


def call(kernel, out_shape, flops, moved, scratch=(), name=None, far=(), room=24):
    outs = jax.tree.leaves(out_shape)

    def space(i):
        return pl.BlockSpec(memory_space=pltpu.HBM if i in far else pltpu.VMEM)

    def run(*args):
        out_specs = [space(len(args) + i) for i in range(len(outs))]
        return pl.pallas_call(
            kernel,
            out_shape=out_shape,
            in_specs=[space(i) for i in range(len(args))],
            out_specs=out_specs if isinstance(out_shape, tuple) else out_specs[0],
            scratch_shapes=list(scratch),
            cost_estimate=pl.CostEstimate(flops=flops, bytes_accessed=moved, transcendentals=0),
            compiler_params=pltpu.CompilerParams(vmem_limit_bytes=room * 1024 * 1024),
            name=name,
        )(*args)

    return run


def nt(a, b):
    return lax.dot_general(a, b, (((1,), (1,)), ((), ())), preferred_element_type=jnp.float32)


def send_blocks(table_ref, fields_ref, block_ref, out_ref, sem, count, depth, edges, tables=()):
    receivers = block_ref.shape[0]
    width = fields_ref.shape[1] // receivers
    per = LANES // depth
    full = count // per
    if edges:
        tables[0].wait()
        beside = table_ref[receivers * width :, :]
        got = nt(beside, fields_ref[: 2 * per * depth, :])
        row = lax.broadcasted_iota(jnp.int32, (receivers * 8, LANES), 0) % 8
        got = jnp.where(row < 2, got[:, :LANES], got[:, LANES:]).reshape(receivers, 8, LANES)
        block_ref[:, count * width // per :, :] = got.astype(jnp.bfloat16)
    chunks = 2
    some = receivers // chunks
    copies = []
    for c in range(chunks):
        mine = slice(c * some, (c + 1) * some)
        if tables:
            tables[1 + c].wait()
        table = table_ref[c * some * width : (c + 1) * some * width, :]
        for first in range(0, full, 2):
            here = min(2, full - first)
            got = nt(table, fields_ref[first * LANES : (first + here) * LANES, :])
            got = got.astype(jnp.bfloat16)
            for j in range(here):
                block = got[:, j * LANES : (j + 1) * LANES].reshape(some, width, LANES)
                block_ref[mine, (first + j) * width : (first + j + 1) * width, :] = block
        if count % per:
            last = fields_ref[full * LANES : count * depth, :]
            got = nt(table, jnp.concatenate([last, last], axis=0))
            got = got.reshape(some, width, LANES)
            half = width // 2
            lane = lax.broadcasted_iota(jnp.int32, (some, half, LANES), 2)
            block = jnp.where(lane < depth, got[:, :half, :], got[:, half:, :])
            at = full * width
            block_ref[mine, at : at + half, :] = block.astype(jnp.bfloat16)
        copies.append(pltpu.make_async_copy(block_ref.at[mine], out_ref.at[mine], sem.at[c]))
        copies[-1].start()
    for copy in copies:
        copy.wait()


def sorted_lines(recv_ref, t, start, count):
    low = lax.broadcasted_iota(jnp.int32, (count, LANES), 1) < LANES // 2
    even = recv_ref[2 * t, start : start + count, :].astype(jnp.float32)
    odd = recv_ref[2 * t + 1, start : start + count, :].astype(jnp.float32)
    one = jnp.where(low, even, pltpu.roll(odd, LANES // 2, 1))
    two = jnp.where(low, pltpu.roll(even, LANES // 2, 1), odd)
    return one, two


def place(lines_ref, at, t, rows):
    lines_ref[at : at + rows.shape[0], t * LANES : (t + 1) * LANES] = rows.astype(jnp.bfloat16)


def products_kernel(
    table_far, velocity_far, out_ref, table_ref, velocity_ref, fields_ref, block_ref, sem, table_sem, velocity_sem
):
    depth = velocity_ref.shape[1]
    length = velocity_ref.shape[2]
    components, tables = [], []
    for a in range(3):
        components.append(
            pltpu.make_async_copy(velocity_far.at[a], velocity_ref.at[a], velocity_sem.at[a])
        )
        components[-1].start()
    bounds = ((length, table_far.shape[0]), (0, length // 2), (length // 2, length))
    for i, (low, high) in enumerate(bounds):
        tables.append(
            pltpu.make_async_copy(
                table_far.at[low:high], table_ref.at[low:high], table_sem.at[i]
            )
        )
        tables[-1].start()
    parts = []
    for a in range(3):
        components[a].wait()
        parts.append(velocity_ref[a])
        fields_ref[a * depth : (a + 1) * depth, :] = parts[a].astype(jnp.bfloat16)
    for p, (a, b) in enumerate(index_pairs):
        at = (3 + p) * depth
        fields_ref[at : at + depth, :] = (parts[a] * parts[b]).astype(jnp.bfloat16)
    send_blocks(table_ref, fields_ref, block_ref, out_ref, sem, 9, depth, True, tables)


def strain(gradients):
    strain_parts = [0.5 * (gradients[b][a] + gradients[a][b]) for a, b in index_pairs]
    squares_sum = pair_weights[0] * strain_parts[0] * strain_parts[0]
    for weight, part_value in zip(pair_weights[1:], strain_parts[1:]):
        squares_sum = squares_sum + weight * part_value * part_value
    return (strain_parts, jnp.sqrt(2.0 * squares_sum))


def slopes(center, below, above, first, last):
    rows, length = center.shape
    row = lax.broadcasted_iota(jnp.int32, center.shape, 0)
    along = (pltpu.roll(center, length - 1, 1) - pltpu.roll(center, 1, 1)) * 0.5
    following = jnp.where(row == rows - 1, last, pltpu.roll(center, rows - 1, 0))
    previous = jnp.where(row == 0, first, pltpu.roll(center, 1, 0))
    return (along, (above - below) * 0.5, (following - previous) * 0.5)


def strain_kernel(
    table_ref, velocity_ref, below_ref, above_ref, first_ref, last_ref, out_ref, magnitude_ref,
    fields_ref, block_ref, sem,
):
    depth = velocity_ref.shape[1]
    gradients = [
        slopes(velocity_ref[a], below_ref[a], above_ref[a], first_ref[a], last_ref[a])
        for a in range(3)
    ]
    strain_parts, magnitude = strain(gradients)
    magnitude_ref[...] = magnitude
    for p, part_value in enumerate(strain_parts):
        fields_ref[p * depth : (p + 1) * depth, :] = (magnitude * part_value).astype(jnp.bfloat16)
    send_blocks(table_ref, fields_ref, block_ref, out_ref, sem, 6, depth, False)


def smooth_kernel(table_ref, recv_ref, smooth_ref, edges_ref, lines_ref):
    senders = recv_ref.shape[0]
    _, width, length = smooth_ref.shape
    for t in range(senders // 2):
        one, two = sorted_lines(recv_ref, t, 0, width)
        place(lines_ref, 0, t, one)
        place(lines_ref, width, t, two)
        one, two = sorted_lines(recv_ref, t, width, width)
        place(lines_ref, 2 * width, t, one)
        one, two = sorted_lines(recv_ref, t, 9 * width // 2, 8)
        place(lines_ref, 3 * width, t, jnp.concatenate([one, two], axis=0))
    got = nt(lines_ref[...], table_ref[:length, :]).astype(jnp.bfloat16)
    for a in range(3):
        smooth_ref[a] = got[a * width : (a + 1) * width, :]
    edges_ref[...] = got[3 * width :, :].astype(jnp.float32)


def leonard_kernel(table_ref, recv_ref, smooth_ref, out_ref, lines_ref, leonard_ref, sem):
    senders = recv_ref.shape[0]
    _, width, length = smooth_ref.shape
    half = width // 2
    for t in range(senders // 2):
        place(lines_ref, 0, t, sorted_lines(recv_ref, t, width, width)[1])
        for j in range(2):
            one, two = sorted_lines(recv_ref, t, (2 + j) * width, width)
            place(lines_ref, (1 + 2 * j) * width, t, one)
            place(lines_ref, (2 + 2 * j) * width, t, two)
        one, two = sorted_lines(recv_ref, t, 4 * width, half)
        place(lines_ref, 5 * width, t, one)
        place(lines_ref, 5 * width + half, t, two)
    got = nt(lines_ref[...], table_ref[:length, :]).astype(jnp.bfloat16)
    for p, (a, b) in enumerate(index_pairs):
        product = smooth_ref[a].astype(jnp.float32) * smooth_ref[b].astype(jnp.float32)
        leonard_ref[p] = got[p * width : (p + 1) * width, :].astype(jnp.float32) - product
    copy = pltpu.make_async_copy(leonard_ref, out_ref, sem)
    copy.start()
    copy.wait()


def model_kernel(smooth_ref, below_ref, above_ref, edges_ref, out_ref, model_ref, sem):
    gradients = []
    for a, at in zip(range(3), (0, 8, 2)):
        center, below, above = (
            ref[a].astype(jnp.float32) for ref in (smooth_ref, below_ref, above_ref)
        )
        first, last = edges_ref[at : at + 1, :], edges_ref[at + 1 : at + 2, :]
        along, across, between = slopes(center, below, above, first, last)
        gradients.append((between, across, along))
    strain_parts, magnitude = strain(gradients)
    for p, part_value in enumerate(strain_parts):
        model_ref[p] = 4.0 * magnitude * part_value
    copy = pltpu.make_async_copy(model_ref, out_ref, sem)
    copy.start()
    copy.wait()


def sums_kernel(
    table_far, recv_far, leonard_far, model_far, out_ref,
    table_ref, recv_ref, leonard_ref, model_ref, lines_ref, table_sem, recv_sem, leonard_sem, model_sem,
):
    senders = recv_ref.shape[0]
    _, width, length = leonard_ref.shape
    groups = recv_sem.shape[0]
    some = senders // groups
    arrivals = []
    for g in range(groups):
        mine = slice(g * some, (g + 1) * some)
        arrivals.append(pltpu.make_async_copy(recv_far.at[mine], recv_ref.at[mine], recv_sem.at[g]))
        arrivals[-1].start()
    table = pltpu.make_async_copy(table_far.at[:length], table_ref, table_sem)
    table.start()
    terms = []
    for p in range(6):
        terms.append(
            (
                pltpu.make_async_copy(model_far.at[p], model_ref.at[p], model_sem.at[p]),
                pltpu.make_async_copy(leonard_far.at[p], leonard_ref.at[p], leonard_sem.at[p]),
            )
        )
        for copy in terms[-1]:
            copy.start()
    for g in range(groups):
        arrivals[g].wait()
        for t in range(g * some // 2, (g + 1) * some // 2):
            for j in range(3):
                one, two = sorted_lines(recv_ref, t, j * width, width)
                place(lines_ref, 2 * j * width, t, one)
                place(lines_ref, (2 * j + 1) * width, t, two)
    table.wait()
    got = nt(lines_ref[...], table_ref[...]).astype(jnp.bfloat16)
    numerator = jnp.zeros((8, length), jnp.float32)
    denominator = jnp.zeros((8, length), jnp.float32)
    for p, weight in enumerate(pair_weights):
        for copy in terms[p]:
            copy.wait()
        model_term = got[p * width : (p + 1) * width, :].astype(jnp.float32) - model_ref[p]
        top = leonard_ref[p] * model_term
        bottom = model_term * model_term
        numerator = numerator + weight * top.reshape(width // 8, 8, length).sum(axis=0)
        denominator = denominator + weight * bottom.reshape(width // 8, 8, length).sum(axis=0)

    def lanes(x):
        total = x[:, :LANES]
        for at in range(LANES, length, LANES):
            total = total + x[:, at : at + LANES]
        total = total.sum(axis=0, keepdims=True)
        return total + pltpu.roll(total, LANES // 2, 1)

    low = lax.broadcasted_iota(jnp.int32, (1, LANES), 1) < LANES // 2
    pair = jnp.where(low, lanes(numerator), lanes(denominator))
    out_ref[...] = jnp.broadcast_to(pair, out_ref.shape)


def viscosity_kernel(cells, sums_ref, magnitude_ref, out_ref):
    total = sums_ref[...].sum(axis=0)
    low = lax.broadcasted_iota(jnp.int32, total.shape, 1) < LANES // 2
    numerator = jnp.sum(jnp.where(low, total, 0.0), axis=1, keepdims=True)
    denominator = jnp.sum(jnp.where(low, 0.0, total), axis=1, keepdims=True)
    coefficient = numerator / cells / (2.0 * (denominator / cells + epsilon))
    out_ref[...] = magnitude_ref[...] * coefficient


def body(velocity):
    _, _, depth, nx = velocity.shape
    parts = lax.axis_size("pz")
    rows = lax.axis_size("py")
    nz = depth * parts
    width = nx // parts
    f32, bf16 = jnp.float32, jnp.bfloat16
    table_x = filter_table(nx).T
    table_z = filter_table(nz)
    beside = np.zeros((parts, 8, nx), bf16)
    for r in range(parts):
        beside[r, :4] = table_x[[r * width - 1, (r + 1) * width % nx] * 2]
    lanes_x = jnp.asarray(np.concatenate([table_x, beside.reshape(parts * 8, nx)]))
    lanes_z = lanes_x if np.array_equal(table_x, table_z) else jnp.asarray(table_z)
    up = [(i, i + 1) for i in range(rows - 1)]
    down = [(b, a) for a, b in up]
    around = [(i, (i + 1) % parts) for i in range(parts)]
    back = [(b, a) for a, b in around]
    velocity = velocity.reshape(3, depth, nx)
    vmem, dma = pltpu.VMEM, pltpu.SemaphoreType.DMA

    first = lax.ppermute(velocity[:, -1:], "pz", around)
    last = lax.ppermute(velocity[:, :1], "pz", back)
    send_shape = (parts, 9 * width // 2 + 8, LANES)
    send = call(
        products_kernel,
        jax.ShapeDtypeStruct(send_shape, bf16),
        2 * 9 * depth * nx * nx,
        12 * depth * nx + 2 * nx * nx,
        [
            vmem(lanes_x.shape, bf16), vmem(velocity.shape, f32),
            vmem((9 * depth, nx), bf16), vmem(send_shape, bf16), dma((2,)), dma((3,)), dma((3,)),
        ],
        "products",
        (0, 1, 2),
        58,
    )(lanes_x, velocity)
    send, first, last = lax.optimization_barrier((send, first, last))
    received = lax.all_to_all(send, "pz", 0, 0, tiled=True)

    below = lax.ppermute(velocity, "py", up)
    above = lax.ppermute(velocity, "py", down)
    strain_shape = (parts, 3 * width, LANES)
    send_strain, magnitude = call(
        strain_kernel,
        (jax.ShapeDtypeStruct(strain_shape, bf16), jax.ShapeDtypeStruct((depth, nx), f32)),
        2 * 6 * depth * nx * nx,
        36 * depth * nx + 2 * nx * nx,
        [vmem((6 * depth, nx), bf16), vmem(strain_shape, bf16), dma((2,))],
        "strain",
        (6,),
    )(lanes_x, velocity, below, above, first, last)
    received_strain = lax.all_to_all(send_strain, "pz", 0, 0, tiled=True)

    smooth, edges = call(
        smooth_kernel,
        (jax.ShapeDtypeStruct((3, width, nz), bf16), jax.ShapeDtypeStruct((16, nz), f32)),
        2 * 4 * width * nz * nz,
        2 * nz * nz,
        [vmem((3 * width + 16, nz), bf16)],
        "smooth",
    )(lanes_z, received)
    smooth_below = lax.ppermute(smooth, "py", up)
    smooth_above = lax.ppermute(smooth, "py", down)
    six = jax.ShapeDtypeStruct((6, width, nz), f32)
    leonard = call(
        leonard_kernel,
        six,
        2 * 6 * width * nz * nz,
        24 * width * nz + 2 * nz * nz,
        [vmem((6 * width, nz), bf16), vmem(six.shape, f32), dma],
        "leonard",
        (3,),
        58,
    )(lanes_z, received, smooth)
    model = call(
        model_kernel,
        six,
        100 * width * nz,
        24 * width * nz,
        [vmem(six.shape, f32), dma],
        "model",
        (4,),
        58,
    )(smooth, smooth_below, smooth_above, edges)
    sums = call(
        sums_kernel,
        jax.ShapeDtypeStruct((parts, 1, LANES), f32),
        2 * 6 * width * nz * nz,
        48 * width * nz + 2 * nz * nz,
        [
            vmem((nz, nz), bf16), vmem(strain_shape, bf16), vmem(six.shape, f32),
            vmem(six.shape, f32), vmem((6 * width, nz), bf16), dma, dma((4,)), dma((6,)), dma((6,)),
        ],
        "sums",
        (0, 1, 2, 3),
        58,
    )(lanes_z, received_strain, leonard, model)
    totals = lax.all_to_all(sums, "pz", 0, 0, tiled=True)
    cells = nx * nz
    nu_t = call(
        lambda *refs: viscosity_kernel(cells, *refs),
        jax.ShapeDtypeStruct((depth, nx), f32),
        2 * depth * nx,
        8 * depth * nx,
        (),
        "viscosity",
    )(totals, magnitude)
    filtered_velocity = jnp.transpose(smooth, (0, 2, 1))
    return (nu_t[None], filtered_velocity[:, None])


def solution(mesh):
    in_specs = (P(None, "py", "pz", None),)
    out_specs = (P("py", "pz", None), P(None, "py", None, "pz"))
    return jax.shard_map(body, mesh=mesh, in_specs=in_specs, out_specs=out_specs, check_vma=False)
```

time: 103 us -> 107 us (1.039)
  Pallas kernels: 10.6 us -> 24.7 us
  local copies, waits for them, and re-layouts: 12.9 us -> 2.61 us
  waiting for transfers between devices: 27.6 us -> 31.7 us
  starting transfers between devices: 34.8 us -> 31.7 us
  blocking collectives: 15.9 us -> 14.8 us
    ppermute x1, waiting for transfers between devices: 19.2 us -> 0.01 us  [body(): last = lax.ppermute(velocity[:, :1], 'pz', back)]
    ppermute x1, waiting for transfers between devices: 0.01 us -> 14.8 us  [body(): above = lax.ppermute(velocity, 'py', down)]
    pallas_call x7, Pallas kernels: 10.6 us -> 24.7 us  [run(): pl.pallas_call(kernel, out_shape=out_shape, in_specs=[space(i) for i in r...]
    unnamed x24 -> x12, local copies, waits for them, and re-layouts: 11.9 us -> 1.65 us
    ppermute x2 -> x0, waiting for transfers between devices: 7.62 us -> none  [the longest x1 4.32 us: body(): last_hat = lax.ppermute(smooth_first, 'pz', back)]
    ppermute x1, waiting for transfers between devices: 0.2 us -> 7.22 us  [body(): below = lax.ppermute(velocity, 'py', up)]
    ppermute x1, waiting for transfers between devices: 0.01 us -> 5.14 us  [body(): smooth_below = lax.ppermute(smooth, 'py', up)]
    ppermute x1, waiting for transfers between devices: 0.01 us -> 3.11 us  [body(): smooth_above = lax.ppermute(smooth, 'py', down)]
  transfers between devices with their start and end apart: 10 -> 8, of which waited for: 5 -> 5; matrix products, arithmetic and copies ran while one was open for 1% -> 0% of each run, Pallas kernels for 5% -> 18%
where the time goes in v2:
time: 107 us; the launch traced here: 106 us
  starting transfers between devices  31.7 us (30%)
  waiting for transfers between devices  31.7 us (30%)
  Pallas kernels  24.7 us (23%)
  blocking collectives  14.8 us (14%)
  local copies, waits for them, and re-layouts  2.61 us (2%)
    pallas_call x7, Pallas kernels, run(): pl.pallas_call(kernel, out_shape=out_shape, in_specs=[space(i) for i in r...  24.7 us
    ppermute x1, waiting for transfers between devices, body(): above = lax.ppermute(velocity, 'py', down)  14.8 us
    all_to_all x1, blocking collectives, body(): totals = lax.all_to_all(sums, 'pz', 0, 0, tiled=True)  14.8 us
    all_to_all x1, starting transfers between devices, body(): received = lax.all_to_all(send, 'pz', 0, 0, tiled=True)  9.49 us
    all_to_all x1, starting transfers between devices, body(): received_strain = lax.all_to_all(send_strain, 'pz', 0, 0, tiled=True)  8.05 us
    ppermute x1, waiting for transfers between devices, body(): below = lax.ppermute(velocity, 'py', up)  7.22 us
    ppermute x1, waiting for transfers between devices, body(): smooth_below = lax.ppermute(smooth, 'py', up)  5.14 us
    ppermute x1, starting transfers between devices, body(): above = lax.ppermute(velocity, 'py', down)  4.27 us
  transfers between devices with their start and end apart: 8, of which 5 were waited for; matrix products, arithmetic and copies ran while one was open for 0% of the time, Pallas kernels for 18%

profile of v2, /device:TPU:33, one launch (start us, length us, event | category | flops | bytes accessed | tf_op | source)
XLA Modules:
  0.0 106.2 jit_solution(13545902959486845412)
XLA Ops:
  0.6 1.0 fusion
  1.6 0.7 collective-permute-start.3
  2.3 2.0 %collective-permute-start.2 = (f32[3,1,1024]{2,1,0:T(1,128)S(1)}, f32[3,1,1024]{2,1,0:T(1,128)S(1)}, u32[]{:S(2)}, u32[]{:S(2)}) collective-permute-start(f32[3,1,1024]{2,1,0:T(1,128)S(1)} %get-tuple-element.19), channel_id=1, source_target_pairs={{0,1},{1,2},{2,3},{3,4},{4,5},{5,6},{6,7},{7,8},{8,9},{9,10},{10,1... | collective-permute-start | bytes 36872 | tf_op jit(solution)/shard_map/ppermute | solution.py:314
  4.3 0.0 copy-start.1
  4.3 5.7 %products.1 = bf16[16,296,128]{2,1,0:T(8,128)(2,1)} custom-call(bf16[1152,1024]{1,0:T(8,128)(2,1)} %constant.2.clone.table_far.table_ref, f32[3,64,1024]{2,1,0:T(8,128)} %bitcast.8), custom_call_target="tpu_custom_call" | custom-call | flops 1207959552 | bytes 2883584 | tf_op jit(solution)/shard_map/products/pallas_call | solution.py:35
  10.0 0.0 copy-start
  10.0 0.0 collective-permute-done.3.last_ref
  10.1 1.4 %collective-permute-done.2.first_ref = f32[3,1,1024]{2,1,0:T(1,128)S(1)} collective-permute-done((f32[3,1,1024]{2,1,0:T(1,128)S(1)}, f32[3,1,1024]{2,1,0:T(1,128)S(1)}, u32[]{:S(2)}, u32[]{:S(2)}) %collective-permute-start.2) | collective-permute-done | bytes 12320 | tf_op jit(solution)/shard_map/ppermute | solution.py:314
  11.4 9.5 %all-to-all-start.1 = ((bf16[16,296,128]{2,1,0:T(8,128)(2,1)}), bf16[16,296,128]{2,1,0:T(8,128)(2,1)}, u32[]{:S(2)}, u32[]{:S(2)}) async-start(bf16[16,296,128]{2,1,0:T(8,128)(2,1)} %products.1), calls=%async_computation.1 | async-start | bytes 2424832 | tf_op jit(solution)/shard_map/all_to_all | solution.py:331
  20.9 0.0 copy-done.1
  20.9 4.3 %collective-permute-start.1 = (f32[3,64,1024]{2,1,0:T(8,128)S(1)}, f32[3,64,1024]{2,1,0:T(8,128)S(1)}, u32[]{:S(2)}, u32[]{:S(2)}) collective-permute-start(f32[3,64,1024]{2,1,0:T(8,128)S(1)} %bitcast.9), channel_id=1, source_target_pairs={{16,0},{32,16},{48,32},{64,48},{80,64},{96,80},{112,96},{128,112},... | collective-permute-start | bytes 2359304 | tf_op jit(solution)/shard_map/ppermute | solution.py:334
  25.2 1.9 %collective-permute-start = (f32[3,64,1024]{2,1,0:T(8,128)S(1)}, f32[3,64,1024]{2,1,0:T(8,128)S(1)}, u32[]{:S(2)}, u32[]{:S(2)}) collective-permute-start(f32[3,64,1024]{2,1,0:T(8,128)S(1)} %bitcast.10), channel_id=1, source_target_pairs={{0,16},{16,32},{32,48},{48,64},{64,80},{80,96},{96,112},{112,128},... | collective-permute-start | bytes 2359304 | tf_op jit(solution)/shard_map/ppermute | solution.py:333
  27.1 14.8 %collective-permute-done.1.above_ref = f32[3,64,1024]{2,1,0:T(8,128)S(1)} collective-permute-done((f32[3,64,1024]{2,1,0:T(8,128)S(1)}, f32[3,64,1024]{2,1,0:T(8,128)S(1)}, u32[]{:S(2)}, u32[]{:S(2)}) %collective-permute-start.1) | collective-permute-done | bytes 786464 | tf_op jit(solution)/shard_map/ppermute | solution.py:334
  42.0 7.2 %collective-permute-done.below_ref = f32[3,64,1024]{2,1,0:T(8,128)S(1)} collective-permute-done((f32[3,64,1024]{2,1,0:T(8,128)S(1)}, f32[3,64,1024]{2,1,0:T(8,128)S(1)}, u32[]{:S(2)}, u32[]{:S(2)}) %collective-permute-start) | collective-permute-done | bytes 786464 | tf_op jit(solution)/shard_map/ppermute | solution.py:333
  49.2 0.0 copy-done
  49.2 2.5 %strain.1 = (bf16[16,192,128]{2,1,0:T(8,128)(2,1)S(1)}, f32[64,1024]{1,0:T(8,128)S(1)}) custom-call(bf16[1152,1024]{1,0:T(8,128)(2,1)S(1)} %copy-done, f32[3,64,1024]{2,1,0:T(8,128)S(1)} %bitcast.11, f32[3,64,1024]{2,1,0:T(8,128)S(1)} %collective-permute-done.below_ref, f32[3,64,1024]{2,1,0:T(8,128)S(1)} %collective-permute-done.1.above_ref, ...), custom_call_target="tpu_custom_call" | custom-call | flops 805306368 | bytes 4456448 | tf_op jit(solution)/shard_map/strain/pallas_call | solution.py:35
  51.7 0.0 copy-start.2
  51.7 0.9 copy-done.2
  52.6 0.0 all-to-all-done.1.recv_ref
  52.6 8.0 %all-to-all-start = ((bf16[16,192,128]{2,1,0:T(8,128)(2,1)}), bf16[16,192,128]{2,1,0:T(8,128)(2,1)}, u32[]{:S(2)}, u32[]{:S(2)}) async-start(bf16[16,192,128]{2,1,0:T(8,128)(2,1)} %copy-done.2), calls=%async_computation | async-start | bytes 1572864 | tf_op jit(solution)/shard_map/all_to_all | solution.py:345
  60.7 2.9 %smooth.1 = (bf16[3,64,1024]{2,1,0:T(8,128)(2,1)}, f32[16,1024]{1,0:T(8,128)S(1)}) custom-call(bf16[1152,1024]{1,0:T(8,128)(2,1)S(1)} %copy-done, bf16[16,296,128]{2,1,0:T(8,128)(2,1)} %all-to-all-done.1.recv_ref), custom_call_target="tpu_custom_call" | custom-call | flops 536870912 | bytes 2097152 | tf_op jit(solution)/shard_map/smooth/pallas_call | solution.py:35
  63.6 0.0 copy-start.3
  63.6 1.9 %collective-permute-start.5 = (bf16[3,64,1024]{2,1,0:T(8,128)(2,1)}, bf16[3,64,1024]{2,1,0:T(8,128)(2,1)S(1)}, u32[]{:S(2)}, u32[]{:S(2)}) collective-permute-start(bf16[3,64,1024]{2,1,0:T(8,128)(2,1)} %get-tuple-element.13.smooth_ref), channel_id=1, source_target_pairs={{16,0},{32,16},{48,32},{64,48},{80,64},{96,80},{112,96},{128,112},... | collective-permute-start | bytes 1179656 | tf_op jit(solution)/shard_map/ppermute | solution.py:356
  65.5 3.4 %collective-permute-start.4 = (bf16[3,64,1024]{2,1,0:T(8,128)(2,1)}, bf16[3,64,1024]{2,1,0:T(8,128)(2,1)S(1)}, u32[]{:S(2)}, u32[]{:S(2)}) collective-permute-start(bf16[3,64,1024]{2,1,0:T(8,128)(2,1)} %get-tuple-element.13.smooth_ref), channel_id=1, source_target_pairs={{0,16},{16,32},{32,48},{48,64},{64,80},{80,96},{96,112},{112,128},... | collective-permute-start | bytes 1179656 | tf_op jit(solution)/shard_map/ppermute | solution.py:355
  68.9 4.4 %leonard.1.leonard_far = f32[6,64,1024]{2,1,0:T(8,128)} custom-call(bf16[1152,1024]{1,0:T(8,128)(2,1)} %constant.2.clone.table_far.table_ref, bf16[16,296,128]{2,1,0:T(8,128)(2,1)} %all-to-all-done.1.recv_ref, bf16[3,64,1024]{2,1,0:T(8,128)(2,1)} %get-tuple-element.13.smooth_ref), custom_call_target="tpu_custom_call" | custom-call | flops 805306368 | bytes 3670016 | tf_op jit(solution)/shard_map/leonard/pallas_call | solution.py:35
  73.2 0.0 copy-done.3
  73.2 3.1 %collective-permute-done.5.above_ref = bf16[3,64,1024]{2,1,0:T(8,128)(2,1)S(1)} collective-permute-done((bf16[3,64,1024]{2,1,0:T(8,128)(2,1)}, bf16[3,64,1024]{2,1,0:T(8,128)(2,1)S(1)}, u32[]{:S(2)}, u32[]{:S(2)}) %collective-permute-start.5) | collective-permute-done | bytes 393248 | tf_op jit(solution)/shard_map/ppermute | solution.py:356
  76.3 0.0 copy-start.4
  76.3 5.1 %collective-permute-done.4.below_ref = bf16[3,64,1024]{2,1,0:T(8,128)(2,1)S(1)} collective-permute-done((bf16[3,64,1024]{2,1,0:T(8,128)(2,1)}, bf16[3,64,1024]{2,1,0:T(8,128)(2,1)S(1)}, u32[]{:S(2)}, u32[]{:S(2)}) %collective-permute-start.4) | collective-permute-done | bytes 393248 | tf_op jit(solution)/shard_map/ppermute | solution.py:355
  81.5 0.0 copy-start.5
  81.5 0.0 copy-done.4
  81.5 0.7 copy-done.5
  82.2 3.4 %model.1.model_far = f32[6,64,1024]{2,1,0:T(8,128)} custom-call(bf16[3,64,1024]{2,1,0:T(8,128)(2,1)} %get-tuple-element.13.smooth_ref, bf16[3,64,1024]{2,1,0:T(8,128)(2,1)} %copy-done.5, bf16[3,64,1024]{2,1,0:T(8,128)(2,1)} %copy-done.4, f32[16,1024]{1,0:T(8,128)} %copy-done.3), custom_call_target="tpu_custom_call" | custom-call | flops 6553600 | bytes 1572864 | tf_op jit(solution)/shard_map/model/pallas_call | solution.py:35
  85.7 0.0 all-to-all-done.recv_far
  85.7 4.9 %sums.1 = f32[16,1,128]{2,1,0:T(1,128)} custom-call(bf16[1152,1024]{1,0:T(8,128)(2,1)} %constant.2.clone.table_far.table_ref, bf16[16,192,128]{2,1,0:T(8,128)(2,1)} %all-to-all-done.recv_far, f32[6,64,1024]{2,1,0:T(8,128)} %leonard.1.leonard_far, f32[6,64,1024]{2,1,0:T(8,128)} %model.1.model_far), custom_call_target="tpu_custom_call" | custom-call | flops 805306368 | bytes 5242880 | tf_op jit(solution)/shard_map/sums/pallas_call | solution.py:35
  90.6 14.8 %all_to_all.15.refs_0_ = f32[16,1,128]{2,1,0:T(1,128)S(1)} all-to-all(f32[16,1,128]{2,1,0:T(1,128)} %sums.1), channel_id=1, replica_groups=mesh['py'=32,'pz'=16] {'pz'}, dimensions={0} | all-to-all | bytes 16384 | tf_op jit(solution)/shard_map/all_to_all | solution.py:391
  105.4 0.8 viscosity.1
Async XLA Ops:
  1.6 8.4 %collective-permute-start.3 = (f32[3,1,1024]{2,1,0:T(1,128)S(1)}, f32[3,1,1024]{2,1,0:T(1,128)S(1)}, u32[]{:S(2)}, u32[]{:S(2)}) collective-permute-start(f32[3,1,1024]{2,1,0:T(1,128)S(1)} %get-tuple-element.18), channel_id=1, source_target_pairs={{1,0},{2,1},{3,2},{4,3},{5,4},{6,5},{7,6},{8,7},{9,8},{10,9},{11,1... | collective-permute-start | bytes 36872 | tf_op jit(solution)/shard_map/ppermute | solution.py:315
  2.3 9.2 %collective-permute-start.2 = (f32[3,1,1024]{2,1,0:T(1,128)S(1)}, f32[3,1,1024]{2,1,0:T(1,128)S(1)}, u32[]{:S(2)}, u32[]{:S(2)}) collective-permute-start(f32[3,1,1024]{2,1,0:T(1,128)S(1)} %get-tuple-element.19), channel_id=1, source_target_pairs={{0,1},{1,2},{2,3},{3,4},{4,5},{5,6},{6,7},{7,8},{8,9},{9,10},{10,1... | collective-permute-start | bytes 36872 | tf_op jit(solution)/shard_map/ppermute | solution.py:314
  4.3 16.6 %copy-start.1 = (f32[3,1,64,1024]{3,2,1,0:T(8,128)S(1)}, f32[3,1,64,1024]{3,2,1,0:T(8,128)}, u32[]{:S(2)}) copy-start(f32[3,1,64,1024]{3,2,1,0:T(8,128)} %param.2) | copy-start | bytes 2359300
  10.0 39.2 %copy-start = (bf16[1152,1024]{1,0:T(8,128)(2,1)S(1)}, bf16[1152,1024]{1,0:T(8,128)(2,1)}, u32[]{:S(2)}) copy-start(bf16[1152,1024]{1,0:T(8,128)(2,1)} %constant.2.clone.table_far.table_ref) | copy-start | bytes 7077892
  11.4 41.2 %all-to-all-start.1 = ((bf16[16,296,128]{2,1,0:T(8,128)(2,1)}), bf16[16,296,128]{2,1,0:T(8,128)(2,1)}, u32[]{:S(2)}, u32[]{:S(2)}) async-start(bf16[16,296,128]{2,1,0:T(8,128)(2,1)} %products.1), calls=%async_computation.1 | async-start | bytes 2424832 | tf_op jit(solution)/shard_map/all_to_all | solution.py:331
  20.9 21.0 %collective-permute-start.1 = (f32[3,64,1024]{2,1,0:T(8,128)S(1)}, f32[3,64,1024]{2,1,0:T(8,128)S(1)}, u32[]{:S(2)}, u32[]{:S(2)}) collective-permute-start(f32[3,64,1024]{2,1,0:T(8,128)S(1)} %bitcast.9), channel_id=1, source_target_pairs={{16,0},{32,16},{48,32},{64,48},{80,64},{96,80},{112,96},{128,112},... | collective-permute-start | bytes 2359304 | tf_op jit(solution)/shard_map/ppermute | solution.py:334
  25.2 24.0 %collective-permute-start = (f32[3,64,1024]{2,1,0:T(8,128)S(1)}, f32[3,64,1024]{2,1,0:T(8,128)S(1)}, u32[]{:S(2)}, u32[]{:S(2)}) collective-permute-start(f32[3,64,1024]{2,1,0:T(8,128)S(1)} %bitcast.10), channel_id=1, source_target_pairs={{0,16},{16,32},{32,48},{48,64},{64,80},{80,96},{96,112},{112,128},... | collective-permute-start | bytes 2359304 | tf_op jit(solution)/shard_map/ppermute | solution.py:333
  51.7 0.9 copy-start.2
  52.6 33.0 %all-to-all-start = ((bf16[16,192,128]{2,1,0:T(8,128)(2,1)}), bf16[16,192,128]{2,1,0:T(8,128)(2,1)}, u32[]{:S(2)}, u32[]{:S(2)}) async-start(bf16[16,192,128]{2,1,0:T(8,128)(2,1)} %copy-done.2), calls=%async_computation | async-start | bytes 1572864 | tf_op jit(solution)/shard_map/all_to_all | solution.py:345
  63.6 9.7 %copy-start.3 = (f32[16,1024]{1,0:T(8,128)}, f32[16,1024]{1,0:T(8,128)S(1)}, u32[]{:S(2)}) copy-start(f32[16,1024]{1,0:T(8,128)S(1)} %get-tuple-element.14.edges_ref) | copy-start | bytes 196612
  63.6 12.8 %collective-permute-start.5 = (bf16[3,64,1024]{2,1,0:T(8,128)(2,1)}, bf16[3,64,1024]{2,1,0:T(8,128)(2,1)S(1)}, u32[]{:S(2)}, u32[]{:S(2)}) collective-permute-start(bf16[3,64,1024]{2,1,0:T(8,128)(2,1)} %get-tuple-element.13.smooth_ref), channel_id=1, source_target_pairs={{16,0},{32,16},{48,32},{64,48},{80,64},{96,80},{112,96},{128,112},... | collective-permute-start | bytes 1179656 | tf_op jit(solution)/shard_map/ppermute | solution.py:356
  65.5 16.0 %collective-permute-start.4 = (bf16[3,64,1024]{2,1,0:T(8,128)(2,1)}, bf16[3,64,1024]{2,1,0:T(8,128)(2,1)S(1)}, u32[]{:S(2)}, u32[]{:S(2)}) collective-permute-start(bf16[3,64,1024]{2,1,0:T(8,128)(2,1)} %get-tuple-element.13.smooth_ref), channel_id=1, source_target_pairs={{0,16},{16,32},{32,48},{48,64},{64,80},{80,96},{96,112},{112,128},... | collective-permute-start | bytes 1179656 | tf_op jit(solution)/shard_map/ppermute | solution.py:355
  76.3 5.1 %copy-start.4 = (bf16[3,64,1024]{2,1,0:T(8,128)(2,1)}, bf16[3,64,1024]{2,1,0:T(8,128)(2,1)S(1)}, u32[]{:S(2)}) copy-start(bf16[3,64,1024]{2,1,0:T(8,128)(2,1)S(1)} %collective-permute-done.5.above_ref) | copy-start | bytes 1179652
  81.5 0.8 copy-start.5

commit v3 on v2

--- a/solution.py
+++ b/solution.py
@@ -50,14 +50,25 @@
     return lax.dot_general(a, b, (((1,), (1,)), ((), ())), preferred_element_type=jnp.float32)
 
 
-def send_blocks(table_ref, fields_ref, block_ref, out_ref, sem, count, depth, edges, tables=()):
+def turned(rows, blocks):
+    at = rows.shape[1] - blocks * LANES
+    return rows if blocks == 0 else jnp.concatenate([rows[:, at:], rows[:, :at]], axis=1)
+
+
+def table_rows(band_ref, first, last):
+    band = band_ref[:LANES, :]
+    return jnp.concatenate([turned(band, a) for a in range(first, last)], axis=0)
+
+
+def send_blocks(table_ref, fields_ref, block_ref, out_ref, sem, count, depth, edges):
     receivers = block_ref.shape[0]
     width = fields_ref.shape[1] // receivers
     per = LANES // depth
     full = count // per
     if edges:
-        tables[0].wait()
-        beside = table_ref[receivers * width :, :]
+        seed = table_ref[LANES:, :]
+        beside = [turned(seed, q) for q in range(receivers * width // LANES)]
+        beside = jnp.concatenate(beside, axis=0)
         got = nt(beside, fields_ref[: 2 * per * depth, :])
         row = lax.broadcasted_iota(jnp.int32, (receivers * 8, LANES), 0) % 8
         got = jnp.where(row < 2, got[:, :LANES], got[:, LANES:]).reshape(receivers, 8, LANES)
@@ -67,9 +78,8 @@
     copies = []
     for c in range(chunks):
         mine = slice(c * some, (c + 1) * some)
-        if tables:
-            tables[1 + c].wait()
-        table = table_ref[c * some * width : (c + 1) * some * width, :]
+        blocks = some * width // LANES
+        table = table_rows(table_ref, c * blocks, (c + 1) * blocks)
         for first in range(0, full, 2):
             here = min(2, full - first)
             got = nt(table, fields_ref[first * LANES : (first + here) * LANES, :])
@@ -105,34 +115,15 @@
     lines_ref[at : at + rows.shape[0], t * LANES : (t + 1) * LANES] = rows.astype(jnp.bfloat16)
 
 
-def products_kernel(
-    table_far, velocity_far, out_ref, table_ref, velocity_ref, fields_ref, block_ref, sem, table_sem, velocity_sem
-):
+def products_kernel(table_ref, velocity_ref, out_ref, fields_ref, block_ref, sem):
     depth = velocity_ref.shape[1]
-    length = velocity_ref.shape[2]
-    components, tables = [], []
+    parts = [velocity_ref[a] for a in range(3)]
     for a in range(3):
-        components.append(
-            pltpu.make_async_copy(velocity_far.at[a], velocity_ref.at[a], velocity_sem.at[a])
-        )
-        components[-1].start()
-    bounds = ((length, table_far.shape[0]), (0, length // 2), (length // 2, length))
-    for i, (low, high) in enumerate(bounds):
-        tables.append(
-            pltpu.make_async_copy(
-                table_far.at[low:high], table_ref.at[low:high], table_sem.at[i]
-            )
-        )
-        tables[-1].start()
-    parts = []
-    for a in range(3):
-        components[a].wait()
-        parts.append(velocity_ref[a])
         fields_ref[a * depth : (a + 1) * depth, :] = parts[a].astype(jnp.bfloat16)
     for p, (a, b) in enumerate(index_pairs):
         at = (3 + p) * depth
         fields_ref[at : at + depth, :] = (parts[a] * parts[b]).astype(jnp.bfloat16)
-    send_blocks(table_ref, fields_ref, block_ref, out_ref, sem, 9, depth, True, tables)
+    send_blocks(table_ref, fields_ref, block_ref, out_ref, sem, 9, depth, True)
 
 
 def strain(gradients):
@@ -179,13 +170,13 @@
         place(lines_ref, 2 * width, t, one)
         one, two = sorted_lines(recv_ref, t, 9 * width // 2, 8)
         place(lines_ref, 3 * width, t, jnp.concatenate([one, two], axis=0))
-    got = nt(lines_ref[...], table_ref[:length, :]).astype(jnp.bfloat16)
+    got = nt(lines_ref[...], table_rows(table_ref, 0, length // LANES)).astype(jnp.bfloat16)
     for a in range(3):
         smooth_ref[a] = got[a * width : (a + 1) * width, :]
     edges_ref[...] = got[3 * width :, :].astype(jnp.float32)
 
 
-def leonard_kernel(table_ref, recv_ref, smooth_ref, out_ref, lines_ref, leonard_ref, sem):
+def leonard_kernel(table_ref, recv_ref, smooth_ref, leonard_ref, lines_ref):
     senders = recv_ref.shape[0]
     _, width, length = smooth_ref.shape
     half = width // 2
@@ -198,16 +189,13 @@
         one, two = sorted_lines(recv_ref, t, 4 * width, half)
         place(lines_ref, 5 * width, t, one)
         place(lines_ref, 5 * width + half, t, two)
-    got = nt(lines_ref[...], table_ref[:length, :]).astype(jnp.bfloat16)
+    got = nt(lines_ref[...], table_rows(table_ref, 0, length // LANES)).astype(jnp.bfloat16)
     for p, (a, b) in enumerate(index_pairs):
         product = smooth_ref[a].astype(jnp.float32) * smooth_ref[b].astype(jnp.float32)
         leonard_ref[p] = got[p * width : (p + 1) * width, :].astype(jnp.float32) - product
-    copy = pltpu.make_async_copy(leonard_ref, out_ref, sem)
-    copy.start()
-    copy.wait()
-
-
-def model_kernel(smooth_ref, below_ref, above_ref, edges_ref, out_ref, model_ref, sem):
+
+
+def model_kernel(smooth_ref, below_ref, above_ref, edges_ref, model_ref):
     gradients = []
     for a, at in zip(range(3), (0, 8, 2)):
         center, below, above = (
@@ -219,50 +207,20 @@
     strain_parts, magnitude = strain(gradients)
     for p, part_value in enumerate(strain_parts):
         model_ref[p] = 4.0 * magnitude * part_value
-    copy = pltpu.make_async_copy(model_ref, out_ref, sem)
-    copy.start()
-    copy.wait()
-
-
-def sums_kernel(
-    table_far, recv_far, leonard_far, model_far, out_ref,
-    table_ref, recv_ref, leonard_ref, model_ref, lines_ref, table_sem, recv_sem, leonard_sem, model_sem,
-):
+
+
+def sums_kernel(table_ref, recv_ref, leonard_ref, model_ref, out_ref, lines_ref):
     senders = recv_ref.shape[0]
     _, width, length = leonard_ref.shape
-    groups = recv_sem.shape[0]
-    some = senders // groups
-    arrivals = []
-    for g in range(groups):
-        mine = slice(g * some, (g + 1) * some)
-        arrivals.append(pltpu.make_async_copy(recv_far.at[mine], recv_ref.at[mine], recv_sem.at[g]))
-        arrivals[-1].start()
-    table = pltpu.make_async_copy(table_far.at[:length], table_ref, table_sem)
-    table.start()
-    terms = []
-    for p in range(6):
-        terms.append(
-            (
-                pltpu.make_async_copy(model_far.at[p], model_ref.at[p], model_sem.at[p]),
-                pltpu.make_async_copy(leonard_far.at[p], leonard_ref.at[p], leonard_sem.at[p]),
-            )
-        )
-        for copy in terms[-1]:
-            copy.start()
-    for g in range(groups):
-        arrivals[g].wait()
-        for t in range(g * some // 2, (g + 1) * some // 2):
-            for j in range(3):
-                one, two = sorted_lines(recv_ref, t, j * width, width)
-                place(lines_ref, 2 * j * width, t, one)
-                place(lines_ref, (2 * j + 1) * width, t, two)
-    table.wait()
-    got = nt(lines_ref[...], table_ref[...]).astype(jnp.bfloat16)
+    for t in range(senders // 2):
+        for j in range(3):
+            one, two = sorted_lines(recv_ref, t, j * width, width)
+            place(lines_ref, 2 * j * width, t, one)
+            place(lines_ref, (2 * j + 1) * width, t, two)
+    got = nt(lines_ref[...], table_rows(table_ref, 0, length // LANES)).astype(jnp.bfloat16)
     numerator = jnp.zeros((8, length), jnp.float32)
     denominator = jnp.zeros((8, length), jnp.float32)
     for p, weight in enumerate(pair_weights):
-        for copy in terms[p]:
-            copy.wait()
         model_term = got[p * width : (p + 1) * width, :].astype(jnp.float32) - model_ref[p]
         top = leonard_ref[p] * model_term
         bottom = model_term * model_term
@@ -299,11 +257,12 @@
     f32, bf16 = jnp.float32, jnp.bfloat16
     table_x = filter_table(nx).T
     table_z = filter_table(nz)
-    beside = np.zeros((parts, 8, nx), bf16)
-    for r in range(parts):
-        beside[r, :4] = table_x[[r * width - 1, (r + 1) * width % nx] * 2]
-    lanes_x = jnp.asarray(np.concatenate([table_x, beside.reshape(parts * 8, nx)]))
-    lanes_z = lanes_x if np.array_equal(table_x, table_z) else jnp.asarray(table_z)
+    beside = np.zeros((2, 8, nx), bf16)
+    for r in range(2):
+        beside[r, :4] = table_x[[r * width - 1, (r + 1) * width] * 2]
+    lanes_x = jnp.asarray(np.concatenate([table_x[:LANES], beside.reshape(16, nx)]))
+    same = np.array_equal(table_x[:LANES], table_z[:LANES])
+    lanes_z = lanes_x if same else jnp.asarray(table_z[:LANES])
     up = [(i, i + 1) for i in range(rows - 1)]
     down = [(b, a) for a, b in up]
     around = [(i, (i + 1) % parts) for i in range(parts)]
@@ -319,12 +278,9 @@
         jax.ShapeDtypeStruct(send_shape, bf16),
         2 * 9 * depth * nx * nx,
         12 * depth * nx + 2 * nx * nx,
-        [
-            vmem(lanes_x.shape, bf16), vmem(velocity.shape, f32),
-            vmem((9 * depth, nx), bf16), vmem(send_shape, bf16), dma((2,)), dma((3,)), dma((3,)),
-        ],
+        [vmem((9 * depth, nx), bf16), vmem(send_shape, bf16), dma((2,))],
         "products",
-        (0, 1, 2),
+        (2,),
         58,
     )(lanes_x, velocity)
     send, first, last = lax.optimization_barrier((send, first, last))
@@ -360,33 +316,24 @@
         six,
         2 * 6 * width * nz * nz,
         24 * width * nz + 2 * nz * nz,
-        [vmem((6 * width, nz), bf16), vmem(six.shape, f32), dma],
+        [vmem((6 * width, nz), bf16)],
         "leonard",
-        (3,),
-        58,
     )(lanes_z, received, smooth)
     model = call(
         model_kernel,
         six,
         100 * width * nz,
         24 * width * nz,
-        [vmem(six.shape, f32), dma],
+        (),
         "model",
-        (4,),
-        58,
     )(smooth, smooth_below, smooth_above, edges)
     sums = call(
         sums_kernel,
         jax.ShapeDtypeStruct((parts, 1, LANES), f32),
         2 * 6 * width * nz * nz,
         48 * width * nz + 2 * nz * nz,
-        [
-            vmem((nz, nz), bf16), vmem(strain_shape, bf16), vmem(six.shape, f32),
-            vmem(six.shape, f32), vmem((6 * width, nz), bf16), dma, dma((4,)), dma((6,)), dma((6,)),
-        ],
+        [vmem((6 * width, nz), bf16)],
         "sums",
-        (0, 1, 2, 3),
-        58,
     )(lanes_z, received_strain, leonard, model)
     totals = lax.all_to_all(sums, "pz", 0, 0, tiled=True)
     cells = nx * nz

time: 107 us -> 98.9 us (0.924)
  Pallas kernels: 24.7 us -> 13.6 us
  waiting for transfers between devices: 31.7 us -> 37.8 us
  blocking collectives: 14.8 us -> 12.4 us
  starting transfers between devices: 31.7 us -> 30.1 us
    pallas_call x7, Pallas kernels: 24.7 us -> 13.6 us  [run(): pl.pallas_call(kernel, out_shape=out_shape, in_specs=[space(i) for i in r...]
    all_to_all x1, blocking collectives: 14.8 us -> 12.4 us  [body(): totals = lax.all_to_all(sums, 'pz', 0, 0, tiled=True)]
    ppermute x1, waiting for transfers between devices: 3.11 us -> 5.36 us  [body(): smooth_above = lax.ppermute(smooth, 'py', down)]
    all_to_all x1, waiting for transfers between devices: 0.01 us -> 2.12 us  [body(): received_strain = lax.all_to_all(send_strain, 'pz', 0, 0, tiled=True)]
    ppermute x1, waiting for transfers between devices: 1.38 us -> 3.01 us  [body(): first = lax.ppermute(velocity[:, -1:], 'pz', around)]
    all_to_all x1, starting transfers between devices: 9.49 us -> 7.86 us  [body(): received = lax.all_to_all(send, 'pz', 0, 0, tiled=True)]
    unnamed x12 -> x14, local copies, waits for them, and re-layouts: 1.65 us -> 2.68 us
  transfers between devices with their start and end apart: 8 -> 8, of which waited for: 5 -> 6; matrix products, arithmetic and copies ran while one was open for 0% -> 0% of each run, Pallas kernels for 18% -> 11%
where the time goes in v3:
time: 98.9 us; the launch traced here: 98.3 us
  waiting for transfers between devices  37.8 us (38%)
  starting transfers between devices  30.1 us (30%)
  Pallas kernels  13.6 us (14%)
  blocking collectives  12.4 us (13%)
  local copies, waits for them, and re-layouts  3.64 us (4%)
    ppermute x1, waiting for transfers between devices, body(): above = lax.ppermute(velocity, 'py', down)  14.9 us
    pallas_call x7, Pallas kernels, run(): pl.pallas_call(kernel, out_shape=out_shape, in_specs=[space(i) for i in r...  13.6 us
    all_to_all x1, blocking collectives, body(): totals = lax.all_to_all(sums, 'pz', 0, 0, tiled=True)  12.4 us
    all_to_all x1, starting transfers between devices, body(): received_strain = lax.all_to_all(send_strain, 'pz', 0, 0, tiled=True)  8.03 us
    all_to_all x1, starting transfers between devices, body(): received = lax.all_to_all(send, 'pz', 0, 0, tiled=True)  7.86 us
    ppermute x1, waiting for transfers between devices, body(): below = lax.ppermute(velocity, 'py', up)  7.12 us
    ppermute x1, waiting for transfers between devices, body(): smooth_above = lax.ppermute(smooth, 'py', down)  5.36 us
    ppermute x1, waiting for transfers between devices, body(): smooth_below = lax.ppermute(smooth, 'py', up)  5.25 us
  transfers between devices with their start and end apart: 8, of which 6 were waited for; matrix products, arithmetic and copies ran while one was open for 0% of the time, Pallas kernels for 11%

profile of v3, /device:TPU:33, one launch (start us, length us, event | category | flops | bytes accessed | tf_op | source)
XLA Modules:
  0.0 98.3 jit_solution(12648548753258241404)
XLA Ops:
  0.6 1.0 fusion
  1.6 0.7 collective-permute-start.3
  2.3 2.0 %collective-permute-start.2 = (f32[3,1,1024]{2,1,0:T(1,128)S(1)}, f32[3,1,1024]{2,1,0:T(1,128)S(1)}, u32[]{:S(2)}, u32[]{:S(2)}) collective-permute-start(f32[3,1,1024]{2,1,0:T(1,128)S(1)} %get-tuple-element.19), channel_id=1, source_target_pairs={{0,1},{1,2},{2,3},{3,4},{4,5},{5,6},{6,7},{7,8},{8,9},{9,10},{10,1... | collective-permute-start | bytes 36872 | tf_op jit(solution)/shard_map/ppermute | solution.py:273
  4.3 4.1 %products.1 = bf16[16,296,128]{2,1,0:T(8,128)(2,1)} custom-call(bf16[144,1024]{1,0:T(8,128)(2,1)} %constant.2.clone.table_ref, f32[3,64,1024]{2,1,0:T(8,128)} %bitcast.9), custom_call_target="tpu_custom_call" | custom-call | flops 1207959552 | bytes 2883584 | tf_op jit(solution)/shard_map/products/pallas_call | solution.py:35
  8.4 0.0 copy-start.6
  8.4 0.0 copy-start.2
  8.4 0.0 collective-permute-done.3.last_ref
  8.4 3.0 %collective-permute-done.2.first_ref = f32[3,1,1024]{2,1,0:T(1,128)S(1)} collective-permute-done((f32[3,1,1024]{2,1,0:T(1,128)S(1)}, f32[3,1,1024]{2,1,0:T(1,128)S(1)}, u32[]{:S(2)}, u32[]{:S(2)}) %collective-permute-start.2) | collective-permute-done | bytes 12320 | tf_op jit(solution)/shard_map/ppermute | solution.py:273
  11.4 7.9 %all-to-all-start.1 = ((bf16[16,296,128]{2,1,0:T(8,128)(2,1)}), bf16[16,296,128]{2,1,0:T(8,128)(2,1)S(1)}, u32[]{:S(2)}, u32[]{:S(2)}) async-start(bf16[16,296,128]{2,1,0:T(8,128)(2,1)} %products.1), calls=%async_computation.1 | async-start | bytes 2424832 | tf_op jit(solution)/shard_map/all_to_all | solution.py:287
  19.3 0.0 copy-done.6
  19.3 4.3 %collective-permute-start.1 = (f32[3,64,1024]{2,1,0:T(8,128)S(1)}, f32[3,64,1024]{2,1,0:T(8,128)S(1)}, u32[]{:S(2)}, u32[]{:S(2)}) collective-permute-start(f32[3,64,1024]{2,1,0:T(8,128)S(1)} %bitcast.10), channel_id=1, source_target_pairs={{16,0},{32,16},{48,32},{64,48},{80,64},{96,80},{112,96},{128,112},... | collective-permute-start | bytes 2359304 | tf_op jit(solution)/shard_map/ppermute | solution.py:290
  23.6 1.9 %collective-permute-start = (f32[3,64,1024]{2,1,0:T(8,128)S(1)}, f32[3,64,1024]{2,1,0:T(8,128)S(1)}, u32[]{:S(2)}, u32[]{:S(2)}) collective-permute-start(f32[3,64,1024]{2,1,0:T(8,128)S(1)} %bitcast.11), channel_id=1, source_target_pairs={{0,16},{16,32},{32,48},{48,64},{64,80},{80,96},{96,112},{112,128},... | collective-permute-start | bytes 2359304 | tf_op jit(solution)/shard_map/ppermute | solution.py:289
  25.5 14.9 %collective-permute-done.1.above_ref = f32[3,64,1024]{2,1,0:T(8,128)S(1)} collective-permute-done((f32[3,64,1024]{2,1,0:T(8,128)S(1)}, f32[3,64,1024]{2,1,0:T(8,128)S(1)}, u32[]{:S(2)}, u32[]{:S(2)}) %collective-permute-start.1) | collective-permute-done | bytes 786464 | tf_op jit(solution)/shard_map/ppermute | solution.py:290
  40.5 7.1 %collective-permute-done.below_ref = f32[3,64,1024]{2,1,0:T(8,128)S(1)} collective-permute-done((f32[3,64,1024]{2,1,0:T(8,128)S(1)}, f32[3,64,1024]{2,1,0:T(8,128)S(1)}, u32[]{:S(2)}, u32[]{:S(2)}) %collective-permute-start) | collective-permute-done | bytes 786464 | tf_op jit(solution)/shard_map/ppermute | solution.py:289
  47.6 0.0 copy-done.2
  47.6 2.6 %strain.1 = (bf16[16,192,128]{2,1,0:T(8,128)(2,1)}, f32[64,1024]{1,0:T(8,128)S(1)}) custom-call(bf16[144,1024]{1,0:T(8,128)(2,1)S(1)} %copy-done.2, f32[3,64,1024]{2,1,0:T(8,128)S(1)} %bitcast.12, f32[3,64,1024]{2,1,0:T(8,128)S(1)} %collective-permute-done.below_ref, f32[3,64,1024]{2,1,0:T(8,128)S(1)} %collective-permute-done.1.above_ref, ...), custom_call_target="tpu_custom_call" | custom-call | flops 805306368 | bytes 4456448 | tf_op jit(solution)/shard_map/strain/pallas_call | solution.py:35
  50.2 0.0 copy-start.4
  50.2 0.7 copy-done.4
  50.9 0.0 all-to-all-done.1.recv_ref
  50.9 8.0 %all-to-all-start = ((bf16[16,192,128]{2,1,0:T(8,128)(2,1)}), bf16[16,192,128]{2,1,0:T(8,128)(2,1)}, u32[]{:S(2)}, u32[]{:S(2)}) async-start(bf16[16,192,128]{2,1,0:T(8,128)(2,1)} %get-tuple-element.11), calls=%async_computation | async-start | bytes 1572864 | tf_op jit(solution)/shard_map/all_to_all | solution.py:301
  58.9 1.6 %smooth.1 = (bf16[3,64,1024]{2,1,0:T(8,128)(2,1)}, f32[16,1024]{1,0:T(8,128)S(1)}) custom-call(bf16[144,1024]{1,0:T(8,128)(2,1)S(1)} %copy-done.2, bf16[16,296,128]{2,1,0:T(8,128)(2,1)S(1)} %all-to-all-done.1.recv_ref), custom_call_target="tpu_custom_call" | custom-call | flops 536870912 | bytes 2097152 | tf_op jit(solution)/shard_map/smooth/pallas_call | solution.py:35
  60.5 1.9 %collective-permute-start.5 = (bf16[3,64,1024]{2,1,0:T(8,128)(2,1)}, bf16[3,64,1024]{2,1,0:T(8,128)(2,1)S(1)}, u32[]{:S(2)}, u32[]{:S(2)}) collective-permute-start(bf16[3,64,1024]{2,1,0:T(8,128)(2,1)} %get-tuple-element.13.smooth_ref), channel_id=1, source_target_pairs={{16,0},{32,16},{48,32},{64,48},{80,64},{96,80},{112,96},{128,112},... | collective-permute-start | bytes 1179656 | tf_op jit(solution)/shard_map/ppermute | solution.py:312
  62.5 3.4 %collective-permute-start.4 = (bf16[3,64,1024]{2,1,0:T(8,128)(2,1)}, bf16[3,64,1024]{2,1,0:T(8,128)(2,1)S(1)}, u32[]{:S(2)}, u32[]{:S(2)}) collective-permute-start(bf16[3,64,1024]{2,1,0:T(8,128)(2,1)} %get-tuple-element.13.smooth_ref), channel_id=1, source_target_pairs={{0,16},{16,32},{32,48},{48,64},{64,80},{80,96},{96,112},{112,128},... | collective-permute-start | bytes 1179656 | tf_op jit(solution)/shard_map/ppermute | solution.py:311
  65.8 0.0 copy-start
  65.8 1.0 %copy-done = bf16[3,64,1024]{2,1,0:T(8,128)(2,1)S(1)} copy-done((bf16[3,64,1024]{2,1,0:T(8,128)(2,1)S(1)}, bf16[3,64,1024]{2,1,0:T(8,128)(2,1)}, u32[]{:S(2)}) %copy-start) | copy-done | bytes 393240
  66.8 0.0 copy-start.1
  66.8 1.1 %leonard.1.leonard_ref = f32[6,64,1024]{2,1,0:T(8,128)S(1)} custom-call(bf16[144,1024]{1,0:T(8,128)(2,1)S(1)} %copy-done.2, bf16[16,296,128]{2,1,0:T(8,128)(2,1)S(1)} %all-to-all-done.1.recv_ref, bf16[3,64,1024]{2,1,0:T(8,128)(2,1)S(1)} %copy-done), custom_call_target="tpu_custom_call" | custom-call | flops 805306368 | bytes 3670016 | tf_op jit(solution)/shard_map/leonard/pallas_call | solution.py:35
  67.9 5.4 %collective-permute-done.5.above_ref = bf16[3,64,1024]{2,1,0:T(8,128)(2,1)S(1)} collective-permute-done((bf16[3,64,1024]{2,1,0:T(8,128)(2,1)}, bf16[3,64,1024]{2,1,0:T(8,128)(2,1)S(1)}, u32[]{:S(2)}, u32[]{:S(2)}) %collective-permute-start.5) | collective-permute-done | bytes 393248 | tf_op jit(solution)/shard_map/ppermute | solution.py:312
  73.3 5.2 %collective-permute-done.4.below_ref = bf16[3,64,1024]{2,1,0:T(8,128)(2,1)S(1)} collective-permute-done((bf16[3,64,1024]{2,1,0:T(8,128)(2,1)}, bf16[3,64,1024]{2,1,0:T(8,128)(2,1)S(1)}, u32[]{:S(2)}, u32[]{:S(2)}) %collective-permute-start.4) | collective-permute-done | bytes 393248 | tf_op jit(solution)/shard_map/ppermute | solution.py:311
  78.5 0.0 copy-done.1
  78.6 1.0 %model.1.model_ref = f32[6,64,1024]{2,1,0:T(8,128)S(1)} custom-call(bf16[3,64,1024]{2,1,0:T(8,128)(2,1)S(1)} %copy-done.1, bf16[3,64,1024]{2,1,0:T(8,128)(2,1)S(1)} %collective-permute-done.4.below_ref, bf16[3,64,1024]{2,1,0:T(8,128)(2,1)S(1)} %collective-permute-done.5.above_ref, f32[16,1024]{1,0:T(8,128)S(1)} %get-tuple-element.14.edges_ref), custom_call_target="tpu_custom_call" | custom-call | flops 6553600 | bytes 1572864 | tf_op jit(solution)/shard_map/model/pallas_call | solution.py:35
  79.6 2.1 %all-to-all-done.recv_ref = bf16[16,192,128]{2,1,0:T(8,128)(2,1)} async-done(((bf16[16,192,128]{2,1,0:T(8,128)(2,1)}), bf16[16,192,128]{2,1,0:T(8,128)(2,1)}, u32[]{:S(2)}, u32[]{:S(2)}) %all-to-all-start) | async-done | bytes 786464 | tf_op jit(solution)/shard_map/all_to_all | solution.py:301
  81.7 0.0 copy-start.3
  81.7 1.0 copy-done.3
  82.7 0.0 copy-start.5
  82.7 2.4 %sums.1 = f32[16,1,128]{2,1,0:T(1,128)S(1)} custom-call(bf16[144,1024]{1,0:T(8,128)(2,1)S(1)} %copy-done.3, bf16[16,192,128]{2,1,0:T(8,128)(2,1)} %all-to-all-done.recv_ref, f32[6,64,1024]{2,1,0:T(8,128)S(1)} %leonard.1.leonard_ref, f32[6,64,1024]{2,1,0:T(8,128)S(1)} %model.1.model_ref), custom_call_target="tpu_custom_call" | custom-call | flops 805306368 | bytes 5242880 | tf_op jit(solution)/shard_map/sums/pallas_call | solution.py:35
  85.1 12.4 %all_to_all.15.refs_0_ = f32[16,1,128]{2,1,0:T(1,128)S(1)} all-to-all(f32[16,1,128]{2,1,0:T(1,128)S(1)} %sums.1), channel_id=1, replica_groups=mesh['py'=32,'pz'=16] {'pz'}, dimensions={0} | all-to-all | bytes 16384 | tf_op jit(solution)/shard_map/all_to_all | solution.py:338
  97.5 0.0 copy-done.5
  97.5 0.8 viscosity.1
Async XLA Ops:
  1.6 6.8 %collective-permute-start.3 = (f32[3,1,1024]{2,1,0:T(1,128)S(1)}, f32[3,1,1024]{2,1,0:T(1,128)S(1)}, u32[]{:S(2)}, u32[]{:S(2)}) collective-permute-start(f32[3,1,1024]{2,1,0:T(1,128)S(1)} %get-tuple-element.18), channel_id=1, source_target_pairs={{1,0},{2,1},{3,2},{4,3},{5,4},{6,5},{7,6},{8,7},{9,8},{10,9},{11,1... | collective-permute-start | bytes 36872 | tf_op jit(solution)/shard_map/ppermute | solution.py:274
  2.3 9.2 %collective-permute-start.2 = (f32[3,1,1024]{2,1,0:T(1,128)S(1)}, f32[3,1,1024]{2,1,0:T(1,128)S(1)}, u32[]{:S(2)}, u32[]{:S(2)}) collective-permute-start(f32[3,1,1024]{2,1,0:T(1,128)S(1)} %get-tuple-element.19), channel_id=1, source_target_pairs={{0,1},{1,2},{2,3},{3,4},{4,5},{5,6},{6,7},{7,8},{8,9},{9,10},{10,1... | collective-permute-start | bytes 36872 | tf_op jit(solution)/shard_map/ppermute | solution.py:273
  8.4 10.9 %copy-start.6 = (f32[3,1,64,1024]{3,2,1,0:T(8,128)S(1)}, f32[3,1,64,1024]{3,2,1,0:T(8,128)}, u32[]{:S(2)}) copy-start(f32[3,1,64,1024]{3,2,1,0:T(8,128)} %param.2) | copy-start | bytes 2359300
  8.4 39.2 %copy-start.2 = (bf16[144,1024]{1,0:T(8,128)(2,1)S(1)}, bf16[144,1024]{1,0:T(8,128)(2,1)}, u32[]{:S(2)}) copy-start(bf16[144,1024]{1,0:T(8,128)(2,1)} %constant.2.clone.table_ref) | copy-start | bytes 884740
  11.4 39.5 %all-to-all-start.1 = ((bf16[16,296,128]{2,1,0:T(8,128)(2,1)}), bf16[16,296,128]{2,1,0:T(8,128)(2,1)S(1)}, u32[]{:S(2)}, u32[]{:S(2)}) async-start(bf16[16,296,128]{2,1,0:T(8,128)(2,1)} %products.1), calls=%async_computation.1 | async-start | bytes 2424832 | tf_op jit(solution)/shard_map/all_to_all | solution.py:287
  19.3 21.2 %collective-permute-start.1 = (f32[3,64,1024]{2,1,0:T(8,128)S(1)}, f32[3,64,1024]{2,1,0:T(8,128)S(1)}, u32[]{:S(2)}, u32[]{:S(2)}) collective-permute-start(f32[3,64,1024]{2,1,0:T(8,128)S(1)} %bitcast.10), channel_id=1, source_target_pairs={{16,0},{32,16},{48,32},{64,48},{80,64},{96,80},{112,96},{128,112},... | collective-permute-start | bytes 2359304 | tf_op jit(solution)/shard_map/ppermute | solution.py:290
  23.6 24.0 %collective-permute-start = (f32[3,64,1024]{2,1,0:T(8,128)S(1)}, f32[3,64,1024]{2,1,0:T(8,128)S(1)}, u32[]{:S(2)}, u32[]{:S(2)}) collective-permute-start(f32[3,64,1024]{2,1,0:T(8,128)S(1)} %bitcast.11), channel_id=1, source_target_pairs={{0,16},{16,32},{32,48},{48,64},{64,80},{80,96},{96,112},{112,128},... | collective-permute-start | bytes 2359304 | tf_op jit(solution)/shard_map/ppermute | solution.py:289
  50.2 0.7 copy-start.4
  50.9 30.8 %all-to-all-start = ((bf16[16,192,128]{2,1,0:T(8,128)(2,1)}), bf16[16,192,128]{2,1,0:T(8,128)(2,1)}, u32[]{:S(2)}, u32[]{:S(2)}) async-start(bf16[16,192,128]{2,1,0:T(8,128)(2,1)} %get-tuple-element.11), calls=%async_computation | async-start | bytes 1572864 | tf_op jit(solution)/shard_map/all_to_all | solution.py:301
  60.5 12.8 %collective-permute-start.5 = (bf16[3,64,1024]{2,1,0:T(8,128)(2,1)}, bf16[3,64,1024]{2,1,0:T(8,128)(2,1)S(1)}, u32[]{:S(2)}, u32[]{:S(2)}) collective-permute-start(bf16[3,64,1024]{2,1,0:T(8,128)(2,1)} %get-tuple-element.13.smooth_ref), channel_id=1, source_target_pairs={{16,0},{32,16},{48,32},{64,48},{80,64},{96,80},{112,96},{128,112},... | collective-permute-start | bytes 1179656 | tf_op jit(solution)/shard_map/ppermute | solution.py:312
  62.5 16.1 %collective-permute-start.4 = (bf16[3,64,1024]{2,1,0:T(8,128)(2,1)}, bf16[3,64,1024]{2,1,0:T(8,128)(2,1)S(1)}, u32[]{:S(2)}, u32[]{:S(2)}) collective-permute-start(bf16[3,64,1024]{2,1,0:T(8,128)(2,1)} %get-tuple-element.13.smooth_ref), channel_id=1, source_target_pairs={{0,16},{16,32},{32,48},{48,64},{64,80},{80,96},{96,112},{112,128},... | collective-permute-start | bytes 1179656 | tf_op jit(solution)/shard_map/ppermute | solution.py:311
  65.8 1.0 %copy-start = (bf16[3,64,1024]{2,1,0:T(8,128)(2,1)S(1)}, bf16[3,64,1024]{2,1,0:T(8,128)(2,1)}, u32[]{:S(2)}) copy-start(bf16[3,64,1024]{2,1,0:T(8,128)(2,1)} %get-tuple-element.13.smooth_ref) | copy-start | bytes 1179652
  66.8 11.7 %copy-start.1 = (bf16[3,64,1024]{2,1,0:T(8,128)(2,1)S(1)}, bf16[3,64,1024]{2,1,0:T(8,128)(2,1)}, u32[]{:S(2)}) copy-start(bf16[3,64,1024]{2,1,0:T(8,128)(2,1)} %get-tuple-element.13.smooth_ref) | copy-start | bytes 1179652
  81.7 1.0 copy-start.3
  82.7 14.8 %copy-start.5 = (f32[64,1024]{1,0:T(8,128)S(1)}, f32[64,1024]{1,0:T(8,128)}, u32[]{:S(2)}) copy-start(f32[64,1024]{1,0:T(8,128)} %copy-done.4) | copy-start | bytes 786436

commit v4 on v3

--- a/solution.py
+++ b/solution.py
@@ -134,22 +134,22 @@
     return (strain_parts, jnp.sqrt(2.0 * squares_sum))
 
 
-def slopes(center, below, above, first, last):
+def slopes(center, one, two, sense, first, last):
     rows, length = center.shape
     row = lax.broadcasted_iota(jnp.int32, center.shape, 0)
     along = (pltpu.roll(center, length - 1, 1) - pltpu.roll(center, 1, 1)) * 0.5
     following = jnp.where(row == rows - 1, last, pltpu.roll(center, rows - 1, 0))
     previous = jnp.where(row == 0, first, pltpu.roll(center, 1, 0))
-    return (along, (above - below) * 0.5, (following - previous) * 0.5)
+    return (along, (two - one) * sense, (following - previous) * 0.5)
 
 
 def strain_kernel(
-    table_ref, velocity_ref, below_ref, above_ref, first_ref, last_ref, out_ref, magnitude_ref,
+    table_ref, velocity_ref, one_ref, two_ref, sense_ref, first_ref, last_ref, out_ref, magnitude_ref,
     fields_ref, block_ref, sem,
 ):
     depth = velocity_ref.shape[1]
     gradients = [
-        slopes(velocity_ref[a], below_ref[a], above_ref[a], first_ref[a], last_ref[a])
+        slopes(velocity_ref[a], one_ref[a], two_ref[a], sense_ref[...], first_ref[a], last_ref[a])
         for a in range(3)
     ]
     strain_parts, magnitude = strain(gradients)
@@ -176,9 +176,9 @@
     edges_ref[...] = got[3 * width :, :].astype(jnp.float32)
 
 
-def leonard_kernel(table_ref, recv_ref, smooth_ref, leonard_ref, lines_ref):
+def squares_kernel(table_ref, recv_ref, squares_ref, lines_ref):
     senders = recv_ref.shape[0]
-    _, width, length = smooth_ref.shape
+    _, width, length = squares_ref.shape
     half = width // 2
     for t in range(senders // 2):
         place(lines_ref, 0, t, sorted_lines(recv_ref, t, width, width)[1])
@@ -190,39 +190,49 @@
         place(lines_ref, 5 * width, t, one)
         place(lines_ref, 5 * width + half, t, two)
     got = nt(lines_ref[...], table_rows(table_ref, 0, length // LANES)).astype(jnp.bfloat16)
-    for p, (a, b) in enumerate(index_pairs):
-        product = smooth_ref[a].astype(jnp.float32) * smooth_ref[b].astype(jnp.float32)
-        leonard_ref[p] = got[p * width : (p + 1) * width, :].astype(jnp.float32) - product
-
-
-def model_kernel(smooth_ref, below_ref, above_ref, edges_ref, model_ref):
+    for p in range(6):
+        squares_ref[p] = got[p * width : (p + 1) * width, :]
+
+
+def model_kernel(smooth_ref, one_ref, two_ref, sense_ref, edges_ref, model_ref):
     gradients = []
     for a, at in zip(range(3), (0, 8, 2)):
-        center, below, above = (
-            ref[a].astype(jnp.float32) for ref in (smooth_ref, below_ref, above_ref)
-        )
+        center, one, two = (ref[a].astype(jnp.float32) for ref in (smooth_ref, one_ref, two_ref))
         first, last = edges_ref[at : at + 1, :], edges_ref[at + 1 : at + 2, :]
-        along, across, between = slopes(center, below, above, first, last)
+        along, across, between = slopes(center, one, two, sense_ref[...], first, last)
         gradients.append((between, across, along))
     strain_parts, magnitude = strain(gradients)
     for p, part_value in enumerate(strain_parts):
         model_ref[p] = 4.0 * magnitude * part_value
 
 
-def sums_kernel(table_ref, recv_ref, leonard_ref, model_ref, out_ref, lines_ref):
+def sums_kernel(
+    table_ref, recv_far, smooth_ref, squares_ref, model_ref, out_ref, recv_ref, lines_ref, sem
+):
     senders = recv_ref.shape[0]
-    _, width, length = leonard_ref.shape
-    for t in range(senders // 2):
-        for j in range(3):
-            one, two = sorted_lines(recv_ref, t, j * width, width)
-            place(lines_ref, 2 * j * width, t, one)
-            place(lines_ref, (2 * j + 1) * width, t, two)
+    _, width, length = model_ref.shape
+    groups = sem.shape[0]
+    some = senders // groups
+    arrivals = []
+    for g in range(groups):
+        mine = slice(g * some, (g + 1) * some)
+        arrivals.append(pltpu.make_async_copy(recv_far.at[mine], recv_ref.at[mine], sem.at[g]))
+        arrivals[-1].start()
+    for g in range(groups):
+        arrivals[g].wait()
+        for t in range(g * some // 2, (g + 1) * some // 2):
+            for j in range(3):
+                one, two = sorted_lines(recv_ref, t, j * width, width)
+                place(lines_ref, 2 * j * width, t, one)
+                place(lines_ref, (2 * j + 1) * width, t, two)
     got = nt(lines_ref[...], table_rows(table_ref, 0, length // LANES)).astype(jnp.bfloat16)
+    smooth = [smooth_ref[a].astype(jnp.float32) for a in range(3)]
     numerator = jnp.zeros((8, length), jnp.float32)
     denominator = jnp.zeros((8, length), jnp.float32)
-    for p, weight in enumerate(pair_weights):
+    for p, (weight, (a, b)) in enumerate(zip(pair_weights, index_pairs)):
+        leonard = squares_ref[p].astype(jnp.float32) - smooth[a] * smooth[b]
         model_term = got[p * width : (p + 1) * width, :].astype(jnp.float32) - model_ref[p]
-        top = leonard_ref[p] * model_term
+        top = leonard * model_term
         bottom = model_term * model_term
         numerator = numerator + weight * top.reshape(width // 8, 8, length).sum(axis=0)
         denominator = denominator + weight * bottom.reshape(width // 8, 8, length).sum(axis=0)
@@ -263,8 +273,13 @@
     lanes_x = jnp.asarray(np.concatenate([table_x[:LANES], beside.reshape(16, nx)]))
     same = np.array_equal(table_x[:LANES], table_z[:LANES])
     lanes_z = lanes_x if same else jnp.asarray(table_z[:LANES])
-    up = [(i, i + 1) for i in range(rows - 1)]
-    down = [(b, a) for a, b in up]
+    outward, inward = [], []
+    for i in range(rows - 1):
+        for j in range(parts):
+            pair = (i * parts + j, (i + 1) * parts + j)
+            (inward if j % 2 else outward).append(pair)
+            (outward if j % 2 else inward).append(pair[::-1])
+    sense = (0.5 - (lax.axis_index("pz") % 2).astype(f32)).reshape(1, 1)
     around = [(i, (i + 1) % parts) for i in range(parts)]
     back = [(b, a) for a, b in around]
     velocity = velocity.reshape(3, depth, nx)
@@ -286,8 +301,8 @@
     send, first, last = lax.optimization_barrier((send, first, last))
     received = lax.all_to_all(send, "pz", 0, 0, tiled=True)
 
-    below = lax.ppermute(velocity, "py", up)
-    above = lax.ppermute(velocity, "py", down)
+    one = lax.ppermute(velocity, ("py", "pz"), outward)
+    two = lax.ppermute(velocity, ("py", "pz"), inward)
     strain_shape = (parts, 3 * width, LANES)
     send_strain, magnitude = call(
         strain_kernel,
@@ -296,8 +311,8 @@
         36 * depth * nx + 2 * nx * nx,
         [vmem((6 * depth, nx), bf16), vmem(strain_shape, bf16), dma((2,))],
         "strain",
-        (6,),
-    )(lanes_x, velocity, below, above, first, last)
+        (7,),
+    )(lanes_x, velocity, one, two, sense, first, last)
     received_strain = lax.all_to_all(send_strain, "pz", 0, 0, tiled=True)
 
     smooth, edges = call(
@@ -308,33 +323,33 @@
         [vmem((3 * width + 16, nz), bf16)],
         "smooth",
     )(lanes_z, received)
-    smooth_below = lax.ppermute(smooth, "py", up)
-    smooth_above = lax.ppermute(smooth, "py", down)
-    six = jax.ShapeDtypeStruct((6, width, nz), f32)
-    leonard = call(
-        leonard_kernel,
-        six,
+    smooth_one = lax.ppermute(smooth, ("py", "pz"), outward)
+    smooth_two = lax.ppermute(smooth, ("py", "pz"), inward)
+    squares = call(
+        squares_kernel,
+        jax.ShapeDtypeStruct((6, width, nz), bf16),
         2 * 6 * width * nz * nz,
-        24 * width * nz + 2 * nz * nz,
+        24 * width * nz,
         [vmem((6 * width, nz), bf16)],
-        "leonard",
-    )(lanes_z, received, smooth)
+        "squares",
+    )(lanes_z, received)
     model = call(
         model_kernel,
-        six,
+        jax.ShapeDtypeStruct((6, width, nz), f32),
         100 * width * nz,
         24 * width * nz,
         (),
         "model",
-    )(smooth, smooth_below, smooth_above, edges)
+    )(smooth, smooth_one, smooth_two, sense, edges)
     sums = call(
         sums_kernel,
         jax.ShapeDtypeStruct((parts, 1, LANES), f32),
         2 * 6 * width * nz * nz,
-        48 * width * nz + 2 * nz * nz,
-        [vmem((6 * width, nz), bf16)],
+        48 * width * nz,
+        [vmem(strain_shape, bf16), vmem((6 * width, nz), bf16), dma((4,))],
         "sums",
-    )(lanes_z, received_strain, leonard, model)
+        (1,),
+    )(lanes_z, received_strain, smooth, squares, model)
     totals = lax.all_to_all(sums, "pz", 0, 0, tiled=True)
     cells = nx * nz
     nu_t = call(

time: 98.9 us -> 95.7 us (0.968)
  waiting for transfers between devices: 37.8 us -> 31.3 us
  starting transfers between devices: 30.1 us -> 33.3 us
  Pallas kernels: 13.6 us -> 15 us
  local copies, waits for them, and re-layouts: 3.64 us -> 2.64 us
    ppermute x4, waiting for transfers between devices: 32.7 us -> 18.2 us  [the longest x1 11.1 us: body(): two = lax.ppermute(velocity, ('py', 'pz'), inward)]
    ppermute x4, starting transfers between devices: 11.5 us -> 17.3 us  [the longest x1 6.68 us: body(): smooth_one = lax.ppermute(smooth, ('py', 'pz'), outward)]
    all_to_all x1, waiting for transfers between devices: 0.01 us -> 4.54 us  [body(): received = lax.all_to_all(send, 'pz', 0, 0, tiled=True)]
    all_to_all x1, waiting for transfers between devices: 2.12 us -> 5.58 us  [body(): received_strain = lax.all_to_all(send_strain, 'pz', 0, 0, tiled=True)]
    all_to_all x1, starting transfers between devices: 8.03 us -> 5.42 us  [body(): received_strain = lax.all_to_all(send_strain, 'pz', 0, 0, tiled=True)]
    pallas_call x7, Pallas kernels: 13.6 us -> 15 us  [run(): pl.pallas_call(kernel, out_shape=out_shape, in_specs=[space(i) for i in r...]
    unnamed x14 -> x12, local copies, waits for them, and re-layouts: 2.68 us -> 1.68 us
  transfers between devices with their start and end apart: 8 -> 8, of which waited for: 6 -> 7; matrix products, arithmetic and copies ran while one was open for 0% -> 0% of each run, Pallas kernels for 11% -> 12%
where the time goes in v4:
time: 95.7 us; the launch traced here: 95.2 us
  starting transfers between devices  33.3 us (35%)
  waiting for transfers between devices  31.3 us (33%)
  Pallas kernels  15 us (16%)
  blocking collectives  12.2 us (13%)
  local copies, waits for them, and re-layouts  2.64 us (3%)
    pallas_call x7, Pallas kernels, run(): pl.pallas_call(kernel, out_shape=out_shape, in_specs=[space(i) for i in r...  15 us
    all_to_all x1, blocking collectives, body(): totals = lax.all_to_all(sums, 'pz', 0, 0, tiled=True)  12.2 us
    ppermute x1, waiting for transfers between devices, body(): two = lax.ppermute(velocity, ('py', 'pz'), inward)  11.1 us
    all_to_all x1, starting transfers between devices, body(): received = lax.all_to_all(send, 'pz', 0, 0, tiled=True)  7.86 us
    ppermute x1, starting transfers between devices, body(): smooth_one = lax.ppermute(smooth, ('py', 'pz'), outward)  6.68 us
    all_to_all x1, waiting for transfers between devices, body(): received_strain = lax.all_to_all(send_strain, 'pz', 0, 0, tiled=True)  5.58 us
    ppermute x1, starting transfers between devices, body(): one = lax.ppermute(velocity, ('py', 'pz'), outward)  5.48 us
    all_to_all x1, starting transfers between devices, body(): received_strain = lax.all_to_all(send_strain, 'pz', 0, 0, tiled=True)  5.42 us
  transfers between devices with their start and end apart: 8, of which 7 were waited for; matrix products, arithmetic and copies ran while one was open for 0% of the time, Pallas kernels for 12%

profile of v4, /device:TPU:33, one launch (start us, length us, event | category | flops | bytes accessed | tf_op | source)
XLA Modules:
  0.0 95.2 jit_solution(9135859857104985657)
XLA Ops:
  0.6 1.0 %fusion = (f32[3,1,1024]{2,1,0:T(1,128)S(1)}, f32[3,1,1024]{2,1,0:T(1,128)S(1)}) fusion(f32[3,64,1024]{2,1,0:T(8,128)} %bitcast.9), kind=kLoop, calls=%fused_computation | loop fusion | bytes 49152 | tf_op jit(solution)/shard_map/slice | solution.py:289
  1.6 0.7 collective-permute-start.3
  2.3 2.0 %collective-permute-start.2 = (f32[3,1,1024]{2,1,0:T(1,128)S(1)}, f32[3,1,1024]{2,1,0:T(1,128)S(1)}, u32[]{:S(2)}, u32[]{:S(2)}) collective-permute-start(f32[3,1,1024]{2,1,0:T(1,128)S(1)} %get-tuple-element.19), channel_id=1, source_target_pairs={{0,1},{1,2},{2,3},{3,4},{4,5},{5,6},{6,7},{7,8},{8,9},{9,10},{10,1... | collective-permute-start | bytes 36872 | tf_op jit(solution)/shard_map/ppermute | solution.py:288
  4.3 4.1 %products.1 = bf16[16,296,128]{2,1,0:T(8,128)(2,1)} custom-call(bf16[144,1024]{1,0:T(8,128)(2,1)} %constant.21.clone.table_ref, f32[3,64,1024]{2,1,0:T(8,128)} %bitcast.10), custom_call_target="tpu_custom_call" | custom-call | flops 1207959552 | bytes 2883584 | tf_op jit(solution)/shard_map/products/pallas_call | solution.py:35
  8.4 0.0 copy-start.5
  8.4 0.0 copy-start.1
  8.4 0.0 collective-permute-done.3.last_ref
  8.4 3.0 %collective-permute-done.2.first_ref = f32[3,1,1024]{2,1,0:T(1,128)S(1)} collective-permute-done((f32[3,1,1024]{2,1,0:T(1,128)S(1)}, f32[3,1,1024]{2,1,0:T(1,128)S(1)}, u32[]{:S(2)}, u32[]{:S(2)}) %collective-permute-start.2) | collective-permute-done | bytes 12320 | tf_op jit(solution)/shard_map/ppermute | solution.py:288
  11.4 7.9 %all-to-all-start.1 = ((bf16[16,296,128]{2,1,0:T(8,128)(2,1)}), bf16[16,296,128]{2,1,0:T(8,128)(2,1)S(1)}, u32[]{:S(2)}, u32[]{:S(2)}) async-start(bf16[16,296,128]{2,1,0:T(8,128)(2,1)} %products.1), calls=%async_computation.1 | async-start | bytes 2424832 | tf_op jit(solution)/shard_map/all_to_all | solution.py:302
  19.3 0.0 copy-done.5
  19.3 3.1 %collective-permute-start.1 = (f32[3,64,1024]{2,1,0:T(8,128)S(1)}, f32[3,64,1024]{2,1,0:T(8,128)S(1)}, u32[]{:S(2)}, u32[]{:S(2)}) collective-permute-start(f32[3,64,1024]{2,1,0:T(8,128)S(1)} %bitcast.11), channel_id=1, source_target_pairs={{16,0},{1,17},{18,2},{3,19},{20,4},{5,21},{22,6},{7,23},{24,8},{9,... | collective-permute-start | bytes 2359304 | tf_op jit(solution)/shard_map/ppermute | solution.py:305
  22.4 5.5 %collective-permute-start = (f32[3,64,1024]{2,1,0:T(8,128)S(1)}, f32[3,64,1024]{2,1,0:T(8,128)}, u32[]{:S(2)}, u32[]{:S(2)}) collective-permute-start(f32[3,64,1024]{2,1,0:T(8,128)S(1)} %bitcast.12), channel_id=1, source_target_pairs={{0,16},{17,1},{2,18},{19,3},{4,20},{21,5},{6,22},{23,7},{8,24},{25... | collective-permute-start | bytes 2359304 | tf_op jit(solution)/shard_map/ppermute | solution.py:304
  27.9 11.1 %collective-permute-done.1.two_ref = f32[3,64,1024]{2,1,0:T(8,128)S(1)} collective-permute-done((f32[3,64,1024]{2,1,0:T(8,128)S(1)}, f32[3,64,1024]{2,1,0:T(8,128)S(1)}, u32[]{:S(2)}, u32[]{:S(2)}) %collective-permute-start.1) | collective-permute-done | bytes 786464 | tf_op jit(solution)/shard_map/ppermute | solution.py:305
  39.0 2.5 %collective-permute-done.one_ref = f32[3,64,1024]{2,1,0:T(8,128)} collective-permute-done((f32[3,64,1024]{2,1,0:T(8,128)S(1)}, f32[3,64,1024]{2,1,0:T(8,128)}, u32[]{:S(2)}, u32[]{:S(2)}) %collective-permute-start) | collective-permute-done | bytes 786464 | tf_op jit(solution)/shard_map/ppermute | solution.py:304
  41.5 0.0 copy-done.1
  41.5 3.8 %strain.1 = (bf16[16,192,128]{2,1,0:T(8,128)(2,1)}, f32[64,1024]{1,0:T(8,128)S(1)}) custom-call(bf16[144,1024]{1,0:T(8,128)(2,1)S(1)} %copy-done.1, f32[3,64,1024]{2,1,0:T(8,128)S(1)} %bitcast.13, f32[3,64,1024]{2,1,0:T(8,128)} %collective-permute-done.one_ref, f32[3,64,1024]{2,1,0:T(8,128)S(1)} %collective-permute-done.1.two_ref, f32[1,1]{1,0:T(1,128)} %bitcast.1.sense_ref, ...), custom_call_target="tpu_custom_call" | custom-call | flops 805306368 | bytes 4456448 | tf_op jit(solution)/shard_map/strain/pallas_call | solution.py:35
  45.3 0.0 copy-start.3
  45.3 0.7 copy-done.3
  46.0 4.5 %all-to-all-done.1.recv_ref = bf16[16,296,128]{2,1,0:T(8,128)(2,1)S(1)} async-done(((bf16[16,296,128]{2,1,0:T(8,128)(2,1)}), bf16[16,296,128]{2,1,0:T(8,128)(2,1)S(1)}, u32[]{:S(2)}, u32[]{:S(2)}) %all-to-all-start.1) | async-done | bytes 1212448 | tf_op jit(solution)/shard_map/all_to_all | solution.py:302
  50.5 5.4 %all-to-all-start = ((bf16[16,192,128]{2,1,0:T(8,128)(2,1)}), bf16[16,192,128]{2,1,0:T(8,128)(2,1)S(1)}, u32[]{:S(2)}, u32[]{:S(2)}) async-start(bf16[16,192,128]{2,1,0:T(8,128)(2,1)} %get-tuple-element.11), calls=%async_computation | async-start | bytes 1572864 | tf_op jit(solution)/shard_map/all_to_all | solution.py:316
  55.9 1.6 %smooth.1 = (bf16[3,64,1024]{2,1,0:T(8,128)(2,1)}, f32[16,1024]{1,0:T(8,128)S(1)}) custom-call(bf16[144,1024]{1,0:T(8,128)(2,1)S(1)} %copy-done.1, bf16[16,296,128]{2,1,0:T(8,128)(2,1)S(1)} %all-to-all-done.1.recv_ref), custom_call_target="tpu_custom_call" | custom-call | flops 536870912 | bytes 2097152 | tf_op jit(solution)/shard_map/smooth/pallas_call | solution.py:35
  57.5 0.0 copy-start
  57.5 2.0 %collective-permute-start.5 = (bf16[3,64,1024]{2,1,0:T(8,128)(2,1)}, bf16[3,64,1024]{2,1,0:T(8,128)(2,1)S(1)}, u32[]{:S(2)}, u32[]{:S(2)}) collective-permute-start(bf16[3,64,1024]{2,1,0:T(8,128)(2,1)} %get-tuple-element.13.smooth_ref), channel_id=1, source_target_pairs={{16,0},{1,17},{18,2},{3,19},{20,4},{5,21},{22,6},{7,23},{24,8},{9,... | collective-permute-start | bytes 1179656 | tf_op jit(solution)/shard_map/ppermute | solution.py:327
  59.6 6.7 %collective-permute-start.4 = (bf16[3,64,1024]{2,1,0:T(8,128)(2,1)}, bf16[3,64,1024]{2,1,0:T(8,128)(2,1)S(1)}, u32[]{:S(2)}, u32[]{:S(2)}) collective-permute-start(bf16[3,64,1024]{2,1,0:T(8,128)(2,1)} %get-tuple-element.13.smooth_ref), channel_id=1, source_target_pairs={{0,16},{17,1},{2,18},{19,3},{4,20},{21,5},{6,22},{23,7},{8,24},{25... | collective-permute-start | bytes 1179656 | tf_op jit(solution)/shard_map/ppermute | solution.py:326
  66.3 1.0 %squares.1.squares_ref = bf16[6,64,1024]{2,1,0:T(8,128)(2,1)S(1)} custom-call(bf16[144,1024]{1,0:T(8,128)(2,1)S(1)} %copy-done.1, bf16[16,296,128]{2,1,0:T(8,128)(2,1)S(1)} %all-to-all-done.1.recv_ref), custom_call_target="tpu_custom_call" | custom-call | flops 805306368 | bytes 1572864 | tf_op jit(solution)/shard_map/squares/pallas_call | solution.py:35
  67.3 2.7 %collective-permute-done.5.two_ref = bf16[3,64,1024]{2,1,0:T(8,128)(2,1)S(1)} collective-permute-done((bf16[3,64,1024]{2,1,0:T(8,128)(2,1)}, bf16[3,64,1024]{2,1,0:T(8,128)(2,1)S(1)}, u32[]{:S(2)}, u32[]{:S(2)}) %collective-permute-start.5) | collective-permute-done | bytes 393248 | tf_op jit(solution)/shard_map/ppermute | solution.py:327
  70.0 2.0 %collective-permute-done.4.one_ref = bf16[3,64,1024]{2,1,0:T(8,128)(2,1)S(1)} collective-permute-done((bf16[3,64,1024]{2,1,0:T(8,128)(2,1)}, bf16[3,64,1024]{2,1,0:T(8,128)(2,1)S(1)}, u32[]{:S(2)}, u32[]{:S(2)}) %collective-permute-start.4) | collective-permute-done | bytes 393248 | tf_op jit(solution)/shard_map/ppermute | solution.py:326
  72.0 0.0 copy-done
  72.0 1.1 %model.1.model_ref = f32[6,64,1024]{2,1,0:T(8,128)S(1)} custom-call(bf16[3,64,1024]{2,1,0:T(8,128)(2,1)S(1)} %copy-done, bf16[3,64,1024]{2,1,0:T(8,128)(2,1)S(1)} %collective-permute-done.4.one_ref, bf16[3,64,1024]{2,1,0:T(8,128)(2,1)S(1)} %collective-permute-done.5.two_ref, f32[1,1]{1,0:T(1,128)} %bitcast.1.sense_ref, ...), custom_call_target="tpu_custom_call" | custom-call | flops 6553600 | bytes 1572864 | tf_op jit(solution)/shard_map/model/pallas_call | solution.py:35
  73.0 5.6 %all-to-all-done.recv_far = bf16[16,192,128]{2,1,0:T(8,128)(2,1)S(1)} async-done(((bf16[16,192,128]{2,1,0:T(8,128)(2,1)}), bf16[16,192,128]{2,1,0:T(8,128)(2,1)S(1)}, u32[]{:S(2)}, u32[]{:S(2)}) %all-to-all-start) | async-done | bytes 786464 | tf_op jit(solution)/shard_map/all_to_all | solution.py:316
  78.6 0.0 copy-start.2
  78.6 1.0 %copy-done.2 = bf16[144,1024]{1,0:T(8,128)(2,1)S(1)} copy-done((bf16[144,1024]{1,0:T(8,128)(2,1)S(1)}, bf16[144,1024]{1,0:T(8,128)(2,1)}, u32[]{:S(2)}) %copy-start.2) | copy-done | bytes 294936
  79.6 0.0 copy-start.4
  79.6 2.6 %sums.1 = f32[16,1,128]{2,1,0:T(1,128)S(1)} custom-call(bf16[144,1024]{1,0:T(8,128)(2,1)S(1)} %copy-done.2, bf16[16,192,128]{2,1,0:T(8,128)(2,1)S(1)} %all-to-all-done.recv_far, bf16[3,64,1024]{2,1,0:T(8,128)(2,1)S(1)} %copy-done, bf16[6,64,1024]{2,1,0:T(8,128)(2,1)S(1)} %squares.1.squares_ref, f32[6,64,1024]{2,1,0:T(8,128)S(1)} %model.1.model_ref), custom_call_target="tpu_custom_call" | custom-call | flops 805306368 | bytes 3145728 | tf_op jit(solution)/shard_map/sums/pallas_call | solution.py:35
  82.2 12.2 %all_to_all.15.refs_0_ = f32[16,1,128]{2,1,0:T(1,128)S(1)} all-to-all(f32[16,1,128]{2,1,0:T(1,128)S(1)} %sums.1), channel_id=1, replica_groups=mesh['py'=32,'pz'=16] {'pz'}, dimensions={0} | all-to-all | bytes 16384 | tf_op jit(solution)/shard_map/all_to_all | solution.py:353
  94.4 0.0 copy-done.4
  94.4 0.8 viscosity.1
Async XLA Ops:
  1.6 6.8 %collective-permute-start.3 = (f32[3,1,1024]{2,1,0:T(1,128)S(1)}, f32[3,1,1024]{2,1,0:T(1,128)S(1)}, u32[]{:S(2)}, u32[]{:S(2)}) collective-permute-start(f32[3,1,1024]{2,1,0:T(1,128)S(1)} %get-tuple-element.18), channel_id=1, source_target_pairs={{1,0},{2,1},{3,2},{4,3},{5,4},{6,5},{7,6},{8,7},{9,8},{10,9},{11,1... | collective-permute-start | bytes 36872 | tf_op jit(solution)/shard_map/ppermute | solution.py:289
  2.3 9.2 %collective-permute-start.2 = (f32[3,1,1024]{2,1,0:T(1,128)S(1)}, f32[3,1,1024]{2,1,0:T(1,128)S(1)}, u32[]{:S(2)}, u32[]{:S(2)}) collective-permute-start(f32[3,1,1024]{2,1,0:T(1,128)S(1)} %get-tuple-element.19), channel_id=1, source_target_pairs={{0,1},{1,2},{2,3},{3,4},{4,5},{5,6},{6,7},{7,8},{8,9},{9,10},{10,1... | collective-permute-start | bytes 36872 | tf_op jit(solution)/shard_map/ppermute | solution.py:288
  8.4 10.9 %copy-start.5 = (f32[3,1,64,1024]{3,2,1,0:T(8,128)S(1)}, f32[3,1,64,1024]{3,2,1,0:T(8,128)}, u32[]{:S(2)}) copy-start(f32[3,1,64,1024]{3,2,1,0:T(8,128)} %param.2) | copy-start | bytes 2359300
  8.4 33.1 %copy-start.1 = (bf16[144,1024]{1,0:T(8,128)(2,1)S(1)}, bf16[144,1024]{1,0:T(8,128)(2,1)}, u32[]{:S(2)}) copy-start(bf16[144,1024]{1,0:T(8,128)(2,1)} %constant.21.clone.table_ref) | copy-start | bytes 884740
  11.4 39.1 %all-to-all-start.1 = ((bf16[16,296,128]{2,1,0:T(8,128)(2,1)}), bf16[16,296,128]{2,1,0:T(8,128)(2,1)S(1)}, u32[]{:S(2)}, u32[]{:S(2)}) async-start(bf16[16,296,128]{2,1,0:T(8,128)(2,1)} %products.1), calls=%async_computation.1 | async-start | bytes 2424832 | tf_op jit(solution)/shard_map/all_to_all | solution.py:302
  19.3 19.7 %collective-permute-start.1 = (f32[3,64,1024]{2,1,0:T(8,128)S(1)}, f32[3,64,1024]{2,1,0:T(8,128)S(1)}, u32[]{:S(2)}, u32[]{:S(2)}) collective-permute-start(f32[3,64,1024]{2,1,0:T(8,128)S(1)} %bitcast.11), channel_id=1, source_target_pairs={{16,0},{1,17},{18,2},{3,19},{20,4},{5,21},{22,6},{7,23},{24,8},{9,... | collective-permute-start | bytes 2359304 | tf_op jit(solution)/shard_map/ppermute | solution.py:305
  22.4 19.1 %collective-permute-start = (f32[3,64,1024]{2,1,0:T(8,128)S(1)}, f32[3,64,1024]{2,1,0:T(8,128)}, u32[]{:S(2)}, u32[]{:S(2)}) collective-permute-start(f32[3,64,1024]{2,1,0:T(8,128)S(1)} %bitcast.12), channel_id=1, source_target_pairs={{0,16},{17,1},{2,18},{19,3},{4,20},{21,5},{6,22},{23,7},{8,24},{25... | collective-permute-start | bytes 2359304 | tf_op jit(solution)/shard_map/ppermute | solution.py:304
  45.3 0.7 copy-start.3
  50.5 28.1 %all-to-all-start = ((bf16[16,192,128]{2,1,0:T(8,128)(2,1)}), bf16[16,192,128]{2,1,0:T(8,128)(2,1)S(1)}, u32[]{:S(2)}, u32[]{:S(2)}) async-start(bf16[16,192,128]{2,1,0:T(8,128)(2,1)} %get-tuple-element.11), calls=%async_computation | async-start | bytes 1572864 | tf_op jit(solution)/shard_map/all_to_all | solution.py:316
  57.5 14.4 %copy-start = (bf16[3,64,1024]{2,1,0:T(8,128)(2,1)S(1)}, bf16[3,64,1024]{2,1,0:T(8,128)(2,1)}, u32[]{:S(2)}) copy-start(bf16[3,64,1024]{2,1,0:T(8,128)(2,1)} %get-tuple-element.13.smooth_ref) | copy-start | bytes 1179652
  57.5 12.5 %collective-permute-start.5 = (bf16[3,64,1024]{2,1,0:T(8,128)(2,1)}, bf16[3,64,1024]{2,1,0:T(8,128)(2,1)S(1)}, u32[]{:S(2)}, u32[]{:S(2)}) collective-permute-start(bf16[3,64,1024]{2,1,0:T(8,128)(2,1)} %get-tuple-element.13.smooth_ref), channel_id=1, source_target_pairs={{16,0},{1,17},{18,2},{3,19},{20,4},{5,21},{22,6},{7,23},{24,8},{9,... | collective-permute-start | bytes 1179656 | tf_op jit(solution)/shard_map/ppermute | solution.py:327
  59.6 12.4 %collective-permute-start.4 = (bf16[3,64,1024]{2,1,0:T(8,128)(2,1)}, bf16[3,64,1024]{2,1,0:T(8,128)(2,1)S(1)}, u32[]{:S(2)}, u32[]{:S(2)}) collective-permute-start(bf16[3,64,1024]{2,1,0:T(8,128)(2,1)} %get-tuple-element.13.smooth_ref), channel_id=1, source_target_pairs={{0,16},{17,1},{2,18},{19,3},{4,20},{21,5},{6,22},{23,7},{8,24},{25... | collective-permute-start | bytes 1179656 | tf_op jit(solution)/shard_map/ppermute | solution.py:326
  78.6 1.0 %copy-start.2 = (bf16[144,1024]{1,0:T(8,128)(2,1)S(1)}, bf16[144,1024]{1,0:T(8,128)(2,1)}, u32[]{:S(2)}) copy-start(bf16[144,1024]{1,0:T(8,128)(2,1)} %constant.21.clone.table_ref) | copy-start | bytes 884740
  79.6 14.8 %copy-start.4 = (f32[64,1024]{1,0:T(8,128)S(1)}, f32[64,1024]{1,0:T(8,128)}, u32[]{:S(2)}) copy-start(f32[64,1024]{1,0:T(8,128)} %copy-done.3) | copy-start | bytes 786436

commit v5 on v4

--- a/solution.py
+++ b/solution.py
@@ -12,6 +12,7 @@
 pair_weights = (1.0, 1.0, 1.0, 2.0, 2.0, 2.0)
 epsilon = 1e-06
 LANES = 128
+BAND = 32
 
 
 def filter_table(length):
@@ -24,7 +25,7 @@
     return kernel[lagged].astype(jnp.bfloat16)
 
 
-def call(kernel, out_shape, flops, moved, scratch=(), name=None, far=(), room=24):
+def call(kernel, out_shape, flops, moved, scratch=(), name=None, far=(), room=24, aliases=None):
     outs = jax.tree.leaves(out_shape)
 
     def space(i):
@@ -40,6 +41,7 @@
             scratch_shapes=list(scratch),
             cost_estimate=pl.CostEstimate(flops=flops, bytes_accessed=moved, transcendentals=0),
             compiler_params=pltpu.CompilerParams(vmem_limit_bytes=room * 1024 * 1024),
+            input_output_aliases=aliases or {},
             name=name,
         )(*args)
 
@@ -55,49 +57,57 @@
     return rows if blocks == 0 else jnp.concatenate([rows[:, at:], rows[:, :at]], axis=1)
 
 
-def table_rows(band_ref, first, last):
-    band = band_ref[:LANES, :]
-    return jnp.concatenate([turned(band, a) for a in range(first, last)], axis=0)
-
-
-def send_blocks(table_ref, fields_ref, block_ref, out_ref, sem, count, depth, edges):
+def table_rows(band_ref):
+    rows = band_ref[:BAND, :].astype(jnp.float32)
+    rows = [rows] + [pltpu.roll(rows, at, 1) for at in range(BAND, LANES, BAND)]
+    tile = jnp.concatenate(rows, axis=0).astype(jnp.bfloat16)
+    blocks = band_ref.shape[1] // LANES
+    return jnp.concatenate([turned(tile, a) for a in range(blocks)], axis=0)
+
+
+def send_blocks(band_ref, fields_ref, block_ref, out_ref, sem, count, depth, edges):
     receivers = block_ref.shape[0]
     width = fields_ref.shape[1] // receivers
     per = LANES // depth
     full = count // per
+    table = table_rows(band_ref)
+    copies = []
+
+    def send(first, last):
+        rows = slice(first, last)
+        copies.append(
+            pltpu.make_async_copy(
+                block_ref.at[:, rows, :], out_ref.at[:, rows, :], sem.at[len(copies)]
+            )
+        )
+        copies[-1].start()
+
+    for first in range(0, full, 2):
+        here = min(2, full - first)
+        got = nt(table, fields_ref[first * LANES : (first + here) * LANES, :])
+        got = got.astype(jnp.bfloat16)
+        for j in range(here):
+            block = got[:, j * LANES : (j + 1) * LANES].reshape(receivers, width, LANES)
+            block_ref[:, (first + j) * width : (first + j + 1) * width, :] = block
+        send(first * width, (first + here) * width)
+    tail = full * width
+    if count % per:
+        last = fields_ref[full * LANES : count * depth, :]
+        got = nt(table, jnp.concatenate([last, last], axis=0))
+        got = got.reshape(receivers, width, LANES)
+        half = width // 2
+        lane = lax.broadcasted_iota(jnp.int32, (receivers, half, LANES), 2)
+        block = jnp.where(lane < depth, got[:, :half, :], got[:, half:, :])
+        block_ref[:, tail : tail + half, :] = block.astype(jnp.bfloat16)
     if edges:
-        seed = table_ref[LANES:, :]
+        seed = band_ref[BAND:, :]
         beside = [turned(seed, q) for q in range(receivers * width // LANES)]
-        beside = jnp.concatenate(beside, axis=0)
-        got = nt(beside, fields_ref[: 2 * per * depth, :])
+        got = nt(jnp.concatenate(beside, axis=0), fields_ref[: 2 * LANES, :])
         row = lax.broadcasted_iota(jnp.int32, (receivers * 8, LANES), 0) % 8
         got = jnp.where(row < 2, got[:, :LANES], got[:, LANES:]).reshape(receivers, 8, LANES)
         block_ref[:, count * width // per :, :] = got.astype(jnp.bfloat16)
-    chunks = 2
-    some = receivers // chunks
-    copies = []
-    for c in range(chunks):
-        mine = slice(c * some, (c + 1) * some)
-        blocks = some * width // LANES
-        table = table_rows(table_ref, c * blocks, (c + 1) * blocks)
-        for first in range(0, full, 2):
-            here = min(2, full - first)
-            got = nt(table, fields_ref[first * LANES : (first + here) * LANES, :])
-            got = got.astype(jnp.bfloat16)
-            for j in range(here):
-                block = got[:, j * LANES : (j + 1) * LANES].reshape(some, width, LANES)
-                block_ref[mine, (first + j) * width : (first + j + 1) * width, :] = block
-        if count % per:
-            last = fields_ref[full * LANES : count * depth, :]
-            got = nt(table, jnp.concatenate([last, last], axis=0))
-            got = got.reshape(some, width, LANES)
-            half = width // 2
-            lane = lax.broadcasted_iota(jnp.int32, (some, half, LANES), 2)
-            block = jnp.where(lane < depth, got[:, :half, :], got[:, half:, :])
-            at = full * width
-            block_ref[mine, at : at + half, :] = block.astype(jnp.bfloat16)
-        copies.append(pltpu.make_async_copy(block_ref.at[mine], out_ref.at[mine], sem.at[c]))
-        copies[-1].start()
+    if tail < block_ref.shape[1]:
+        send(tail, block_ref.shape[1])
     for copy in copies:
         copy.wait()
 
@@ -115,14 +125,24 @@
     lines_ref[at : at + rows.shape[0], t * LANES : (t + 1) * LANES] = rows.astype(jnp.bfloat16)
 
 
-def products_kernel(table_ref, velocity_ref, out_ref, fields_ref, block_ref, sem):
+def products_kernel(
+    table_ref, velocity_far, out_ref, velocity_ref, fields_ref, block_ref, velocity_sem, sem
+):
     depth = velocity_ref.shape[1]
-    parts = [velocity_ref[a] for a in range(3)]
+    arrivals = []
     for a in range(3):
-        fields_ref[a * depth : (a + 1) * depth, :] = parts[a].astype(jnp.bfloat16)
-    for p, (a, b) in enumerate(index_pairs):
-        at = (3 + p) * depth
-        fields_ref[at : at + depth, :] = (parts[a] * parts[b]).astype(jnp.bfloat16)
+        arrivals.append(
+            pltpu.make_async_copy(velocity_far.at[a], velocity_ref.at[a], velocity_sem.at[a])
+        )
+        arrivals[-1].start()
+    for a in range(3):
+        arrivals[a].wait()
+        fields_ref[a * depth : (a + 1) * depth, :] = velocity_ref[a].astype(jnp.bfloat16)
+        for p, pair in enumerate(index_pairs):
+            if max(pair) == a:
+                at = (3 + p) * depth
+                product = velocity_ref[pair[0]] * velocity_ref[pair[1]]
+                fields_ref[at : at + depth, :] = product.astype(jnp.bfloat16)
     send_blocks(table_ref, fields_ref, block_ref, out_ref, sem, 9, depth, True)
 
 
@@ -144,14 +164,16 @@
 
 
 def strain_kernel(
-    table_ref, velocity_ref, one_ref, two_ref, sense_ref, first_ref, last_ref, out_ref, magnitude_ref,
+    table_ref, velocity_ref, one_ref, two_ref, sense_ref, within_ref, across_ref, out_ref, magnitude_ref,
     fields_ref, block_ref, sem,
 ):
     depth = velocity_ref.shape[1]
-    gradients = [
-        slopes(velocity_ref[a], one_ref[a], two_ref[a], sense_ref[...], first_ref[a], last_ref[a])
-        for a in range(3)
-    ]
+    sense = sense_ref[...]
+    gradients = []
+    for a in range(3):
+        first = jnp.where(sense > 0.0, across_ref[a], within_ref[a])
+        last = jnp.where(sense > 0.0, within_ref[a], across_ref[a])
+        gradients.append(slopes(velocity_ref[a], one_ref[a], two_ref[a], sense, first, last))
     strain_parts, magnitude = strain(gradients)
     magnitude_ref[...] = magnitude
     for p, part_value in enumerate(strain_parts):
@@ -170,7 +192,7 @@
         place(lines_ref, 2 * width, t, one)
         one, two = sorted_lines(recv_ref, t, 9 * width // 2, 8)
         place(lines_ref, 3 * width, t, jnp.concatenate([one, two], axis=0))
-    got = nt(lines_ref[...], table_rows(table_ref, 0, length // LANES)).astype(jnp.bfloat16)
+    got = nt(lines_ref[...], table_rows(table_ref)).astype(jnp.bfloat16)
     for a in range(3):
         smooth_ref[a] = got[a * width : (a + 1) * width, :]
     edges_ref[...] = got[3 * width :, :].astype(jnp.float32)
@@ -189,7 +211,7 @@
         one, two = sorted_lines(recv_ref, t, 4 * width, half)
         place(lines_ref, 5 * width, t, one)
         place(lines_ref, 5 * width + half, t, two)
-    got = nt(lines_ref[...], table_rows(table_ref, 0, length // LANES)).astype(jnp.bfloat16)
+    got = nt(lines_ref[...], table_rows(table_ref)).astype(jnp.bfloat16)
     for p in range(6):
         squares_ref[p] = got[p * width : (p + 1) * width, :]
 
@@ -206,26 +228,15 @@
         model_ref[p] = 4.0 * magnitude * part_value
 
 
-def sums_kernel(
-    table_ref, recv_far, smooth_ref, squares_ref, model_ref, out_ref, recv_ref, lines_ref, sem
-):
+def sums_kernel(table_ref, recv_ref, smooth_ref, squares_ref, model_ref, out_ref, lines_ref):
     senders = recv_ref.shape[0]
     _, width, length = model_ref.shape
-    groups = sem.shape[0]
-    some = senders // groups
-    arrivals = []
-    for g in range(groups):
-        mine = slice(g * some, (g + 1) * some)
-        arrivals.append(pltpu.make_async_copy(recv_far.at[mine], recv_ref.at[mine], sem.at[g]))
-        arrivals[-1].start()
-    for g in range(groups):
-        arrivals[g].wait()
-        for t in range(g * some // 2, (g + 1) * some // 2):
-            for j in range(3):
-                one, two = sorted_lines(recv_ref, t, j * width, width)
-                place(lines_ref, 2 * j * width, t, one)
-                place(lines_ref, (2 * j + 1) * width, t, two)
-    got = nt(lines_ref[...], table_rows(table_ref, 0, length // LANES)).astype(jnp.bfloat16)
+    for t in range(senders // 2):
+        for j in range(3):
+            one, two = sorted_lines(recv_ref, t, j * width, width)
+            place(lines_ref, 2 * j * width, t, one)
+            place(lines_ref, (2 * j + 1) * width, t, two)
+    got = nt(lines_ref[...], table_rows(table_ref)).astype(jnp.bfloat16)
     smooth = [smooth_ref[a].astype(jnp.float32) for a in range(3)]
     numerator = jnp.zeros((8, length), jnp.float32)
     denominator = jnp.zeros((8, length), jnp.float32)
@@ -270,9 +281,8 @@
     beside = np.zeros((2, 8, nx), bf16)
     for r in range(2):
         beside[r, :4] = table_x[[r * width - 1, (r + 1) * width] * 2]
-    lanes_x = jnp.asarray(np.concatenate([table_x[:LANES], beside.reshape(16, nx)]))
-    same = np.array_equal(table_x[:LANES], table_z[:LANES])
-    lanes_z = lanes_x if same else jnp.asarray(table_z[:LANES])
+    lanes_x = jnp.asarray(np.concatenate([table_x[:BAND], beside.reshape(16, nx)]))
+    lanes_z = jnp.asarray(table_z[:BAND])
     outward, inward = [], []
     for i in range(rows - 1):
         for j in range(parts):
@@ -280,25 +290,30 @@
             (inward if j % 2 else outward).append(pair)
             (outward if j % 2 else inward).append(pair[::-1])
     sense = (0.5 - (lax.axis_index("pz") % 2).astype(f32)).reshape(1, 1)
-    around = [(i, (i + 1) % parts) for i in range(parts)]
-    back = [(b, a) for a, b in around]
+    inside = [(j, j ^ 1) for j in range(parts)]
+    outside = [(j, (j + 1 if j % 2 else j - 1) % parts) for j in range(parts)]
     velocity = velocity.reshape(3, depth, nx)
     vmem, dma = pltpu.VMEM, pltpu.SemaphoreType.DMA
 
-    first = lax.ppermute(velocity[:, -1:], "pz", around)
-    last = lax.ppermute(velocity[:, :1], "pz", back)
+    low, high = velocity[:, :1], velocity[:, -1:]
+    even = lax.axis_index("pz") % 2 == 0
+    within = lax.ppermute(jnp.where(even, high, low), "pz", inside)
+    across = lax.ppermute(jnp.where(even, low, high), "pz", outside)
     send_shape = (parts, 9 * width // 2 + 8, LANES)
     send = call(
         products_kernel,
         jax.ShapeDtypeStruct(send_shape, bf16),
         2 * 9 * depth * nx * nx,
         12 * depth * nx + 2 * nx * nx,
-        [vmem((9 * depth, nx), bf16), vmem(send_shape, bf16), dma((2,))],
+        [
+            vmem(velocity.shape, f32), vmem((9 * depth, nx), bf16), vmem(send_shape, bf16),
+            dma((3,)), dma((3,)),
+        ],
         "products",
-        (2,),
+        (1, 2),
         58,
     )(lanes_x, velocity)
-    send, first, last = lax.optimization_barrier((send, first, last))
+    send, within, across = lax.optimization_barrier((send, within, across))
     received = lax.all_to_all(send, "pz", 0, 0, tiled=True)
 
     one = lax.ppermute(velocity, ("py", "pz"), outward)
@@ -312,7 +327,7 @@
         [vmem((6 * depth, nx), bf16), vmem(strain_shape, bf16), dma((2,))],
         "strain",
         (7,),
-    )(lanes_x, velocity, one, two, sense, first, last)
+    )(lanes_x, velocity, one, two, sense, within, across)
     received_strain = lax.all_to_all(send_strain, "pz", 0, 0, tiled=True)
 
     smooth, edges = call(
@@ -346,9 +361,8 @@
         jax.ShapeDtypeStruct((parts, 1, LANES), f32),
         2 * 6 * width * nz * nz,
         48 * width * nz,
-        [vmem(strain_shape, bf16), vmem((6 * width, nz), bf16), dma((4,))],
+        [vmem((6 * width, nz), bf16)],
         "sums",
-        (1,),
     )(lanes_z, received_strain, smooth, squares, model)
     totals = lax.all_to_all(sums, "pz", 0, 0, tiled=True)
     cells = nx * nz
@@ -359,6 +373,7 @@
         8 * depth * nx,
         (),
         "viscosity",
+        aliases={1: 0},
     )(totals, magnitude)
     filtered_velocity = jnp.transpose(smooth, (0, 2, 1))
     return (nu_t[None], filtered_velocity[:, None])

time: 95.7 us -> 99.2 us (1.037)
  starting transfers between devices: 33.3 us -> 39.5 us
  waiting for transfers between devices: 31.3 us -> 28.1 us
  local copies, waits for them, and re-layouts: 2.64 us -> 0.86 us
  Pallas kernels: 15 us -> 16.1 us
    ppermute x2, starting transfers between devices: 2.69 us -> 13 us  [the longest x1 8.41 us: body(): within = lax.ppermute(jnp.where(even, high, low), 'pz', inside)]
    all_to_all x1, starting transfers between devices: 7.86 us -> 3.74 us  [body(): received = lax.all_to_all(send, 'pz', 0, 0, tiled=True)]
    ppermute x2, waiting for transfers between devices: 3.02 us -> 0.01 us  [the longest x1 0.01 us: body(): within = lax.ppermute(jnp.where(even, high, low), 'pz', inside)]
    pallas_call x7, Pallas kernels: 15 us -> 16.1 us  [run(): pl.pallas_call(kernel, out_shape=out_shape, in_specs=[space(i) for i in r...]
  transfers between devices with their start and end apart: 8 -> 8, of which waited for: 7 -> 6; matrix products, arithmetic and copies ran while one was open for 0% -> 0% of each run, Pallas kernels for 12% -> 13%
where the time goes in v5:
time: 99.2 us; the launch traced here: 98.6 us
  starting transfers between devices  39.5 us (40%)
  waiting for transfers between devices  28.1 us (28%)
  Pallas kernels  16.1 us (16%)
  blocking collectives  12.2 us (12%)
    pallas_call x7, Pallas kernels, run(): pl.pallas_call(kernel, out_shape=out_shape, in_specs=[space(i) for i in r...  16.1 us
    all_to_all x1, blocking collectives, body(): totals = lax.all_to_all(sums, 'pz', 0, 0, tiled=True)  12.2 us
    ppermute x1, waiting for transfers between devices, body(): two = lax.ppermute(velocity, ('py', 'pz'), inward)  11.1 us
    ppermute x1, starting transfers between devices, body(): within = lax.ppermute(jnp.where(even, high, low), 'pz', inside)  8.41 us
    ppermute x1, starting transfers between devices, body(): smooth_one = lax.ppermute(smooth, ('py', 'pz'), outward)  6.68 us
    ppermute x1, starting transfers between devices, body(): one = lax.ppermute(velocity, ('py', 'pz'), outward)  5.49 us
    all_to_all x1, waiting for transfers between devices, body(): received_strain = lax.all_to_all(send_strain, 'pz', 0, 0, tiled=True)  5.48 us
    all_to_all x1, starting transfers between devices, body(): received_strain = lax.all_to_all(send_strain, 'pz', 0, 0, tiled=True)  5.44 us
  transfers between devices with their start and end apart: 8, of which 6 were waited for; matrix products, arithmetic and copies ran while one was open for 0% of the time, Pallas kernels for 13%

profile of v5, /device:TPU:33, one launch (start us, length us, event | category | flops | bytes accessed | tf_op | source)
XLA Modules:
  0.0 98.6 jit_solution(8406928256755257719)
XLA Ops:
  0.6 1.0 broadcast_select_fusion
  1.6 4.6 %collective-permute-start.3 = (f32[3,1,1024]{2,1,0:T(1,128)S(1)}, f32[3,1,1024]{2,1,0:T(1,128)S(1)}, u32[]{:S(2)}, u32[]{:S(2)}) collective-permute-start(f32[3,1,1024]{2,1,0:T(1,128)S(1)} %get-tuple-element.18), channel_id=1, source_target_pairs={{0,15},{1,2},{2,1},{3,4},{4,3},{5,6},{6,5},{7,8},{8,7},{9,10},{10,... | collective-permute-start | bytes 36872 | tf_op jit(solution)/shard_map/ppermute | solution.py:301
  6.2 8.4 %collective-permute-start.2 = (f32[3,1,1024]{2,1,0:T(1,128)S(1)}, f32[3,1,1024]{2,1,0:T(1,128)S(1)}, u32[]{:S(2)}, u32[]{:S(2)}) collective-permute-start(f32[3,1,1024]{2,1,0:T(1,128)S(1)} %get-tuple-element.19), channel_id=1, source_target_pairs={{0,1},{1,0},{2,3},{3,2},{4,5},{5,4},{6,7},{7,6},{8,9},{9,8},{10,11... | collective-permute-start | bytes 36872 | tf_op jit(solution)/shard_map/ppermute | solution.py:300
  14.6 4.7 %products.1 = bf16[16,296,128]{2,1,0:T(8,128)(2,1)} custom-call(bf16[48,1024]{1,0:T(8,128)(2,1)} %constant.26.clone.table_ref, f32[3,64,1024]{2,1,0:T(8,128)} %bitcast.10), custom_call_target="tpu_custom_call" | custom-call | flops 1207959552 | bytes 2883584 | tf_op jit(solution)/shard_map/products/pallas_call | solution.py:36
  19.3 0.0 copy-start.3
  19.3 0.0 copy-start.4
  19.3 0.0 collective-permute-done.3.across_ref
  19.3 0.0 collective-permute-done.2.within_ref
  19.3 3.7 %all-to-all-start.1 = ((bf16[16,296,128]{2,1,0:T(8,128)(2,1)}), bf16[16,296,128]{2,1,0:T(8,128)(2,1)S(1)}, u32[]{:S(2)}, u32[]{:S(2)}) async-start(bf16[16,296,128]{2,1,0:T(8,128)(2,1)} %products.1), calls=%async_computation.1 | async-start | bytes 2424832 | tf_op jit(solution)/shard_map/all_to_all | solution.py:317
  23.1 0.0 copy-done.3
  23.1 3.1 %collective-permute-start.1 = (f32[3,64,1024]{2,1,0:T(8,128)S(1)}, f32[3,64,1024]{2,1,0:T(8,128)S(1)}, u32[]{:S(2)}, u32[]{:S(2)}) collective-permute-start(f32[3,64,1024]{2,1,0:T(8,128)S(1)} %bitcast.11), channel_id=1, source_target_pairs={{16,0},{1,17},{18,2},{3,19},{20,4},{5,21},{22,6},{7,23},{24,8},{9,... | collective-permute-start | bytes 2359304 | tf_op jit(solution)/shard_map/ppermute | solution.py:320
  26.2 5.5 %collective-permute-start = (f32[3,64,1024]{2,1,0:T(8,128)S(1)}, f32[3,64,1024]{2,1,0:T(8,128)}, u32[]{:S(2)}, u32[]{:S(2)}) collective-permute-start(f32[3,64,1024]{2,1,0:T(8,128)S(1)} %bitcast.12), channel_id=1, source_target_pairs={{0,16},{17,1},{2,18},{19,3},{4,20},{21,5},{6,22},{23,7},{8,24},{25... | collective-permute-start | bytes 2359304 | tf_op jit(solution)/shard_map/ppermute | solution.py:319
  31.7 11.1 %collective-permute-done.1.two_ref = f32[3,64,1024]{2,1,0:T(8,128)S(1)} collective-permute-done((f32[3,64,1024]{2,1,0:T(8,128)S(1)}, f32[3,64,1024]{2,1,0:T(8,128)S(1)}, u32[]{:S(2)}, u32[]{:S(2)}) %collective-permute-start.1) | collective-permute-done | bytes 786464 | tf_op jit(solution)/shard_map/ppermute | solution.py:320
  42.8 2.5 %collective-permute-done.one_ref = f32[3,64,1024]{2,1,0:T(8,128)} collective-permute-done((f32[3,64,1024]{2,1,0:T(8,128)S(1)}, f32[3,64,1024]{2,1,0:T(8,128)}, u32[]{:S(2)}, u32[]{:S(2)}) %collective-permute-start) | collective-permute-done | bytes 786464 | tf_op jit(solution)/shard_map/ppermute | solution.py:319
  45.3 0.0 copy-done.4
  45.3 4.5 %strain.1 = (bf16[16,192,128]{2,1,0:T(8,128)(2,1)}, f32[64,1024]{1,0:T(8,128)}) custom-call(bf16[48,1024]{1,0:T(8,128)(2,1)S(1)} %copy-done.4, f32[3,64,1024]{2,1,0:T(8,128)S(1)} %bitcast.13, f32[3,64,1024]{2,1,0:T(8,128)} %collective-permute-done.one_ref, f32[3,64,1024]{2,1,0:T(8,128)S(1)} %collective-permute-done.1.two_ref, f32[1,1]{1,0:T(1,128)} %bitcast.1.sense_ref, ...), custom_call_target="tpu_custom_call" | custom-call | flops 805306368 | bytes 4456448 | tf_op jit(solution)/shard_map/strain/pallas_call | solution.py:36
  49.8 0.0 copy-start.1
  49.8 4.5 %all-to-all-done.1.recv_ref = bf16[16,296,128]{2,1,0:T(8,128)(2,1)S(1)} async-done(((bf16[16,296,128]{2,1,0:T(8,128)(2,1)}), bf16[16,296,128]{2,1,0:T(8,128)(2,1)S(1)}, u32[]{:S(2)}, u32[]{:S(2)}) %all-to-all-start.1) | async-done | bytes 1212448 | tf_op jit(solution)/shard_map/all_to_all | solution.py:317
  54.2 5.4 %all-to-all-start = ((bf16[16,192,128]{2,1,0:T(8,128)(2,1)}), bf16[16,192,128]{2,1,0:T(8,128)(2,1)S(1)}, u32[]{:S(2)}, u32[]{:S(2)}) async-start(bf16[16,192,128]{2,1,0:T(8,128)(2,1)} %get-tuple-element.11), calls=%async_computation | async-start | bytes 1572864 | tf_op jit(solution)/shard_map/all_to_all | solution.py:331
  59.7 0.0 copy-done.1
  59.7 1.7 %smooth.1 = (bf16[3,64,1024]{2,1,0:T(8,128)(2,1)}, f32[16,1024]{1,0:T(8,128)S(1)}) custom-call(bf16[32,1024]{1,0:T(8,128)(2,1)S(1)} %copy-done.1, bf16[16,296,128]{2,1,0:T(8,128)(2,1)S(1)} %all-to-all-done.1.recv_ref), custom_call_target="tpu_custom_call" | custom-call | flops 536870912 | bytes 2097152 | tf_op jit(solution)/shard_map/smooth/pallas_call | solution.py:36
  61.4 0.0 copy-start
  61.4 2.0 %collective-permute-start.5 = (bf16[3,64,1024]{2,1,0:T(8,128)(2,1)}, bf16[3,64,1024]{2,1,0:T(8,128)(2,1)S(1)}, u32[]{:S(2)}, u32[]{:S(2)}) collective-permute-start(bf16[3,64,1024]{2,1,0:T(8,128)(2,1)} %get-tuple-element.13.smooth_ref), channel_id=1, source_target_pairs={{16,0},{1,17},{18,2},{3,19},{20,4},{5,21},{22,6},{7,23},{24,8},{9,... | collective-permute-start | bytes 1179656 | tf_op jit(solution)/shard_map/ppermute | solution.py:342
  63.4 6.7 %collective-permute-start.4 = (bf16[3,64,1024]{2,1,0:T(8,128)(2,1)}, bf16[3,64,1024]{2,1,0:T(8,128)(2,1)S(1)}, u32[]{:S(2)}, u32[]{:S(2)}) collective-permute-start(bf16[3,64,1024]{2,1,0:T(8,128)(2,1)} %get-tuple-element.13.smooth_ref), channel_id=1, source_target_pairs={{0,16},{17,1},{2,18},{19,3},{4,20},{21,5},{6,22},{23,7},{8,24},{25... | collective-permute-start | bytes 1179656 | tf_op jit(solution)/shard_map/ppermute | solution.py:341
  70.1 1.1 %squares.1.squares_ref = bf16[6,64,1024]{2,1,0:T(8,128)(2,1)S(1)} custom-call(bf16[32,1024]{1,0:T(8,128)(2,1)S(1)} %copy-done.1, bf16[16,296,128]{2,1,0:T(8,128)(2,1)S(1)} %all-to-all-done.1.recv_ref), custom_call_target="tpu_custom_call" | custom-call | flops 805306368 | bytes 1572864 | tf_op jit(solution)/shard_map/squares/pallas_call | solution.py:36
  71.2 2.6 %collective-permute-done.5.two_ref = bf16[3,64,1024]{2,1,0:T(8,128)(2,1)S(1)} collective-permute-done((bf16[3,64,1024]{2,1,0:T(8,128)(2,1)}, bf16[3,64,1024]{2,1,0:T(8,128)(2,1)S(1)}, u32[]{:S(2)}, u32[]{:S(2)}) %collective-permute-start.5) | collective-permute-done | bytes 393248 | tf_op jit(solution)/shard_map/ppermute | solution.py:342
  73.8 2.0 %collective-permute-done.4.one_ref = bf16[3,64,1024]{2,1,0:T(8,128)(2,1)S(1)} collective-permute-done((bf16[3,64,1024]{2,1,0:T(8,128)(2,1)}, bf16[3,64,1024]{2,1,0:T(8,128)(2,1)S(1)}, u32[]{:S(2)}, u32[]{:S(2)}) %collective-permute-start.4) | collective-permute-done | bytes 393248 | tf_op jit(solution)/shard_map/ppermute | solution.py:341
  75.8 0.0 copy-done
  75.8 1.1 %model.1.model_ref = f32[6,64,1024]{2,1,0:T(8,128)S(1)} custom-call(bf16[3,64,1024]{2,1,0:T(8,128)(2,1)S(1)} %copy-done, bf16[3,64,1024]{2,1,0:T(8,128)(2,1)S(1)} %collective-permute-done.4.one_ref, bf16[3,64,1024]{2,1,0:T(8,128)(2,1)S(1)} %collective-permute-done.5.two_ref, f32[1,1]{1,0:T(1,128)} %bitcast.1.sense_ref, ...), custom_call_target="tpu_custom_call" | custom-call | flops 6553600 | bytes 1572864 | tf_op jit(solution)/shard_map/model/pallas_call | solution.py:36
  76.9 5.5 %all-to-all-done.recv_ref = bf16[16,192,128]{2,1,0:T(8,128)(2,1)S(1)} async-done(((bf16[16,192,128]{2,1,0:T(8,128)(2,1)}), bf16[16,192,128]{2,1,0:T(8,128)(2,1)S(1)}, u32[]{:S(2)}, u32[]{:S(2)}) %all-to-all-start) | async-done | bytes 786464 | tf_op jit(solution)/shard_map/all_to_all | solution.py:331
  82.3 0.0 copy-start.2
  82.3 0.8 copy-done.2
  83.2 1.3 %sums.1 = f32[16,1,128]{2,1,0:T(1,128)S(1)} custom-call(bf16[32,1024]{1,0:T(8,128)(2,1)S(1)} %copy-done.2, bf16[16,192,128]{2,1,0:T(8,128)(2,1)S(1)} %all-to-all-done.recv_ref, bf16[3,64,1024]{2,1,0:T(8,128)(2,1)S(1)} %copy-done, bf16[6,64,1024]{2,1,0:T(8,128)(2,1)S(1)} %squares.1.squares_ref, f32[6,64,1024]{2,1,0:T(8,128)S(1)} %model.1.model_ref), custom_call_target="tpu_custom_call" | custom-call | flops 805306368 | bytes 3145728 | tf_op jit(solution)/shard_map/sums/pallas_call | solution.py:36
  84.5 12.2 %all_to_all.15.refs_0_ = f32[16,1,128]{2,1,0:T(1,128)S(1)} all-to-all(f32[16,1,128]{2,1,0:T(1,128)S(1)} %sums.1), channel_id=1, replica_groups=mesh['py'=32,'pz'=16] {'pz'}, dimensions={0} | all-to-all | bytes 16384 | tf_op jit(solution)/shard_map/all_to_all | solution.py:367
  96.8 1.8 %viscosity.1 = f32[64,1024]{1,0:T(8,128)} custom-call(f32[16,1,128]{2,1,0:T(1,128)S(1)} %all_to_all.15.refs_0_, f32[64,1024]{1,0:T(8,128)} %get-tuple-element.15.refs_1_), custom_call_target="tpu_custom_call", output_to_operand_aliasing={{}: (1, {})} | custom-call | flops 131072 | bytes 524288 | tf_op jit(solution)/shard_map/viscosity/pallas_call | solution.py:36
Async XLA Ops:
  1.6 17.7 %collective-permute-start.3 = (f32[3,1,1024]{2,1,0:T(1,128)S(1)}, f32[3,1,1024]{2,1,0:T(1,128)S(1)}, u32[]{:S(2)}, u32[]{:S(2)}) collective-permute-start(f32[3,1,1024]{2,1,0:T(1,128)S(1)} %get-tuple-element.18), channel_id=1, source_target_pairs={{0,15},{1,2},{2,1},{3,4},{4,3},{5,6},{6,5},{7,8},{8,7},{9,10},{10,... | collective-permute-start | bytes 36872 | tf_op jit(solution)/shard_map/ppermute | solution.py:301
  6.2 13.2 %collective-permute-start.2 = (f32[3,1,1024]{2,1,0:T(1,128)S(1)}, f32[3,1,1024]{2,1,0:T(1,128)S(1)}, u32[]{:S(2)}, u32[]{:S(2)}) collective-permute-start(f32[3,1,1024]{2,1,0:T(1,128)S(1)} %get-tuple-element.19), channel_id=1, source_target_pairs={{0,1},{1,0},{2,3},{3,2},{4,5},{5,4},{6,7},{7,6},{8,9},{9,8},{10,11... | collective-permute-start | bytes 36872 | tf_op jit(solution)/shard_map/ppermute | solution.py:300
  19.3 3.8 %copy-start.3 = (f32[3,1,64,1024]{3,2,1,0:T(8,128)S(1)}, f32[3,1,64,1024]{3,2,1,0:T(8,128)}, u32[]{:S(2)}) copy-start(f32[3,1,64,1024]{3,2,1,0:T(8,128)} %param.3) | copy-start | bytes 2359300
  19.3 26.0 %copy-start.4 = (bf16[48,1024]{1,0:T(8,128)(2,1)S(1)}, bf16[48,1024]{1,0:T(8,128)(2,1)}, u32[]{:S(2)}) copy-start(bf16[48,1024]{1,0:T(8,128)(2,1)} %constant.26.clone.table_ref) | copy-start | bytes 294916
  19.3 34.9 %all-to-all-start.1 = ((bf16[16,296,128]{2,1,0:T(8,128)(2,1)}), bf16[16,296,128]{2,1,0:T(8,128)(2,1)S(1)}, u32[]{:S(2)}, u32[]{:S(2)}) async-start(bf16[16,296,128]{2,1,0:T(8,128)(2,1)} %products.1), calls=%async_computation.1 | async-start | bytes 2424832 | tf_op jit(solution)/shard_map/all_to_all | solution.py:317
  23.1 19.7 %collective-permute-start.1 = (f32[3,64,1024]{2,1,0:T(8,128)S(1)}, f32[3,64,1024]{2,1,0:T(8,128)S(1)}, u32[]{:S(2)}, u32[]{:S(2)}) collective-permute-start(f32[3,64,1024]{2,1,0:T(8,128)S(1)} %bitcast.11), channel_id=1, source_target_pairs={{16,0},{1,17},{18,2},{3,19},{20,4},{5,21},{22,6},{7,23},{24,8},{9,... | collective-permute-start | bytes 2359304 | tf_op jit(solution)/shard_map/ppermute | solution.py:320
  26.2 19.1 %collective-permute-start = (f32[3,64,1024]{2,1,0:T(8,128)S(1)}, f32[3,64,1024]{2,1,0:T(8,128)}, u32[]{:S(2)}, u32[]{:S(2)}) collective-permute-start(f32[3,64,1024]{2,1,0:T(8,128)S(1)} %bitcast.12), channel_id=1, source_target_pairs={{0,16},{17,1},{2,18},{19,3},{4,20},{21,5},{6,22},{23,7},{8,24},{25... | collective-permute-start | bytes 2359304 | tf_op jit(solution)/shard_map/ppermute | solution.py:319
  49.8 9.9 %copy-start.1 = (bf16[32,1024]{1,0:T(8,128)(2,1)S(1)}, bf16[32,1024]{1,0:T(8,128)(2,1)}, u32[]{:S(2)}) copy-start(bf16[32,1024]{1,0:T(8,128)(2,1)} %constant.27.clone.table_ref) | copy-start | bytes 196612
  54.2 28.1 %all-to-all-start = ((bf16[16,192,128]{2,1,0:T(8,128)(2,1)}), bf16[16,192,128]{2,1,0:T(8,128)(2,1)S(1)}, u32[]{:S(2)}, u32[]{:S(2)}) async-start(bf16[16,192,128]{2,1,0:T(8,128)(2,1)} %get-tuple-element.11), calls=%async_computation | async-start | bytes 1572864 | tf_op jit(solution)/shard_map/all_to_all | solution.py:331
  61.4 14.4 %copy-start = (bf16[3,64,1024]{2,1,0:T(8,128)(2,1)S(1)}, bf16[3,64,1024]{2,1,0:T(8,128)(2,1)}, u32[]{:S(2)}) copy-start(bf16[3,64,1024]{2,1,0:T(8,128)(2,1)} %get-tuple-element.13.smooth_ref) | copy-start | bytes 1179652
  61.4 12.5 %collective-permute-start.5 = (bf16[3,64,1024]{2,1,0:T(8,128)(2,1)}, bf16[3,64,1024]{2,1,0:T(8,128)(2,1)S(1)}, u32[]{:S(2)}, u32[]{:S(2)}) collective-permute-start(bf16[3,64,1024]{2,1,0:T(8,128)(2,1)} %get-tuple-element.13.smooth_ref), channel_id=1, source_target_pairs={{16,0},{1,17},{18,2},{3,19},{20,4},{5,21},{22,6},{7,23},{24,8},{9,... | collective-permute-start | bytes 1179656 | tf_op jit(solution)/shard_map/ppermute | solution.py:342
  63.4 12.4 %collective-permute-start.4 = (bf16[3,64,1024]{2,1,0:T(8,128)(2,1)}, bf16[3,64,1024]{2,1,0:T(8,128)(2,1)S(1)}, u32[]{:S(2)}, u32[]{:S(2)}) collective-permute-start(bf16[3,64,1024]{2,1,0:T(8,128)(2,1)} %get-tuple-element.13.smooth_ref), channel_id=1, source_target_pairs={{0,16},{17,1},{2,18},{19,3},{4,20},{21,5},{6,22},{23,7},{8,24},{25... | collective-permute-start | bytes 1179656 | tf_op jit(solution)/shard_map/ppermute | solution.py:341
  82.3 0.8 copy-start.2

commit v6 on v4

--- a/solution.py
+++ b/solution.py
@@ -12,6 +12,7 @@
 pair_weights = (1.0, 1.0, 1.0, 2.0, 2.0, 2.0)
 epsilon = 1e-06
 LANES = 128
+BAND = 32
 
 
 def filter_table(length):
@@ -58,6 +59,13 @@
 def table_rows(band_ref, first, last):
     band = band_ref[:LANES, :]
     return jnp.concatenate([turned(band, a) for a in range(first, last)], axis=0)
+
+
+def table_of(band):
+    band = band.astype(jnp.float32)
+    rows = [band] + [pltpu.roll(band, at, 1) for at in range(BAND, LANES, BAND)]
+    tile = jnp.concatenate(rows, axis=0).astype(jnp.bfloat16)
+    return jnp.concatenate([turned(tile, a) for a in range(band.shape[1] // LANES)], axis=0)
 
 
 def send_blocks(table_ref, fields_ref, block_ref, out_ref, sem, count, depth, edges):
@@ -170,7 +178,7 @@
         place(lines_ref, 2 * width, t, one)
         one, two = sorted_lines(recv_ref, t, 9 * width // 2, 8)
         place(lines_ref, 3 * width, t, jnp.concatenate([one, two], axis=0))
-    got = nt(lines_ref[...], table_rows(table_ref, 0, length // LANES)).astype(jnp.bfloat16)
+    got = nt(lines_ref[...], table_of(table_ref[...])).astype(jnp.bfloat16)
     for a in range(3):
         smooth_ref[a] = got[a * width : (a + 1) * width, :]
     edges_ref[...] = got[3 * width :, :].astype(jnp.float32)
@@ -189,7 +197,7 @@
         one, two = sorted_lines(recv_ref, t, 4 * width, half)
         place(lines_ref, 5 * width, t, one)
         place(lines_ref, 5 * width + half, t, two)
-    got = nt(lines_ref[...], table_rows(table_ref, 0, length // LANES)).astype(jnp.bfloat16)
+    got = nt(lines_ref[...], table_of(table_ref[...])).astype(jnp.bfloat16)
     for p in range(6):
         squares_ref[p] = got[p * width : (p + 1) * width, :]
 
@@ -206,26 +214,15 @@
         model_ref[p] = 4.0 * magnitude * part_value
 
 
-def sums_kernel(
-    table_ref, recv_far, smooth_ref, squares_ref, model_ref, out_ref, recv_ref, lines_ref, sem
-):
+def sums_kernel(table_ref, recv_ref, smooth_ref, squares_ref, model_ref, out_ref, lines_ref):
     senders = recv_ref.shape[0]
     _, width, length = model_ref.shape
-    groups = sem.shape[0]
-    some = senders // groups
-    arrivals = []
-    for g in range(groups):
-        mine = slice(g * some, (g + 1) * some)
-        arrivals.append(pltpu.make_async_copy(recv_far.at[mine], recv_ref.at[mine], sem.at[g]))
-        arrivals[-1].start()
-    for g in range(groups):
-        arrivals[g].wait()
-        for t in range(g * some // 2, (g + 1) * some // 2):
-            for j in range(3):
-                one, two = sorted_lines(recv_ref, t, j * width, width)
-                place(lines_ref, 2 * j * width, t, one)
-                place(lines_ref, (2 * j + 1) * width, t, two)
-    got = nt(lines_ref[...], table_rows(table_ref, 0, length // LANES)).astype(jnp.bfloat16)
+    for t in range(senders // 2):
+        for j in range(3):
+            one, two = sorted_lines(recv_ref, t, j * width, width)
+            place(lines_ref, 2 * j * width, t, one)
+            place(lines_ref, (2 * j + 1) * width, t, two)
+    got = nt(lines_ref[...], table_of(table_ref[...])).astype(jnp.bfloat16)
     smooth = [smooth_ref[a].astype(jnp.float32) for a in range(3)]
     numerator = jnp.zeros((8, length), jnp.float32)
     denominator = jnp.zeros((8, length), jnp.float32)
@@ -271,8 +268,7 @@
     for r in range(2):
         beside[r, :4] = table_x[[r * width - 1, (r + 1) * width] * 2]
     lanes_x = jnp.asarray(np.concatenate([table_x[:LANES], beside.reshape(16, nx)]))
-    same = np.array_equal(table_x[:LANES], table_z[:LANES])
-    lanes_z = lanes_x if same else jnp.asarray(table_z[:LANES])
+    lanes_z = jnp.asarray(table_z[:BAND])
     outward, inward = [], []
     for i in range(rows - 1):
         for j in range(parts):
@@ -317,7 +313,10 @@
 
     smooth, edges = call(
         smooth_kernel,
-        (jax.ShapeDtypeStruct((3, width, nz), bf16), jax.ShapeDtypeStruct((16, nz), f32)),
+        (
+            jax.ShapeDtypeStruct((3, width, nz), bf16),
+            jax.ShapeDtypeStruct((16, nz), f32),
+        ),
         2 * 4 * width * nz * nz,
         2 * nz * nz,
         [vmem((3 * width + 16, nz), bf16)],
@@ -346,9 +345,8 @@
         jax.ShapeDtypeStruct((parts, 1, LANES), f32),
         2 * 6 * width * nz * nz,
         48 * width * nz,
-        [vmem(strain_shape, bf16), vmem((6 * width, nz), bf16), dma((4,))],
+        [vmem((6 * width, nz), bf16)],
         "sums",
-        (1,),
     )(lanes_z, received_strain, smooth, squares, model)
     totals = lax.all_to_all(sums, "pz", 0, 0, tiled=True)
     cells = nx * nz

time: 95.7 us -> 94.6 us (0.989)
  Pallas kernels: 15 us -> 13.9 us
    pallas_call x7, Pallas kernels: 15 us -> 13.9 us  [run(): pl.pallas_call(kernel, out_shape=out_shape, in_specs=[space(i) for i in r...]
  transfers between devices with their start and end apart: 8 -> 8, of which waited for: 7 -> 7; matrix products, arithmetic and copies ran while one was open for 0% -> 0% of each run, Pallas kernels for 12% -> 13%
where the time goes in v6:
time: 94.6 us; the launch traced here: 94 us
  starting transfers between devices  33.4 us (35%)
  waiting for transfers between devices  31.1 us (33%)
  Pallas kernels  13.9 us (15%)
  blocking collectives  12.3 us (13%)
  local copies, waits for them, and re-layouts  2.52 us (3%)
    pallas_call x7, Pallas kernels, run(): pl.pallas_call(kernel, out_shape=out_shape, in_specs=[space(i) for i in r...  13.9 us
    all_to_all x1, blocking collectives, body(): totals = lax.all_to_all(sums, 'pz', 0, 0, tiled=True)  12.3 us
    ppermute x1, waiting for transfers between devices, body(): two = lax.ppermute(velocity, ('py', 'pz'), inward)  11.1 us
    all_to_all x1, starting transfers between devices, body(): received = lax.all_to_all(send, 'pz', 0, 0, tiled=True)  7.86 us
    ppermute x1, starting transfers between devices, body(): smooth_one = lax.ppermute(smooth, ('py', 'pz'), outward)  6.68 us
    all_to_all x1, starting transfers between devices, body(): received_strain = lax.all_to_all(send_strain, 'pz', 0, 0, tiled=True)  5.57 us
    ppermute x1, starting transfers between devices, body(): one = lax.ppermute(velocity, ('py', 'pz'), outward)  5.48 us
    all_to_all x1, waiting for transfers between devices, body(): received_strain = lax.all_to_all(send_strain, 'pz', 0, 0, tiled=True)  5.47 us
  transfers between devices with their start and end apart: 8, of which 7 were waited for; matrix products, arithmetic and copies ran while one was open for 0% of the time, Pallas kernels for 13%

profile of v6, /device:TPU:33, one launch (start us, length us, event | category | flops | bytes accessed | tf_op | source)
XLA Modules:
  0.0 94.0 jit_solution(6874769022940697005)
XLA Ops:
  0.6 1.0 %fusion = (f32[3,1,1024]{2,1,0:T(1,128)S(1)}, f32[3,1,1024]{2,1,0:T(1,128)S(1)}) fusion(f32[3,64,1024]{2,1,0:T(8,128)} %bitcast.9), kind=kLoop, calls=%fused_computation | loop fusion | bytes 49152 | tf_op jit(solution)/shard_map/slice | solution.py:285
  1.6 0.7 collective-permute-start.3
  2.3 2.0 %collective-permute-start.2 = (f32[3,1,1024]{2,1,0:T(1,128)S(1)}, f32[3,1,1024]{2,1,0:T(1,128)S(1)}, u32[]{:S(2)}, u32[]{:S(2)}) collective-permute-start(f32[3,1,1024]{2,1,0:T(1,128)S(1)} %get-tuple-element.19), channel_id=1, source_target_pairs={{0,1},{1,2},{2,3},{3,4},{4,5},{5,6},{6,7},{7,8},{8,9},{9,10},{10,1... | collective-permute-start | bytes 36872 | tf_op jit(solution)/shard_map/ppermute | solution.py:284
  4.3 4.1 %products.1 = bf16[16,296,128]{2,1,0:T(8,128)(2,1)} custom-call(bf16[144,1024]{1,0:T(8,128)(2,1)} %constant.23.clone.table_ref, f32[3,64,1024]{2,1,0:T(8,128)} %bitcast.10), custom_call_target="tpu_custom_call" | custom-call | flops 1207959552 | bytes 2883584 | tf_op jit(solution)/shard_map/products/pallas_call | solution.py:36
  8.4 0.0 copy-start.5
  8.4 0.0 copy-start.6
  8.4 0.0 collective-permute-done.3.last_ref
  8.4 3.0 %collective-permute-done.2.first_ref = f32[3,1,1024]{2,1,0:T(1,128)S(1)} collective-permute-done((f32[3,1,1024]{2,1,0:T(1,128)S(1)}, f32[3,1,1024]{2,1,0:T(1,128)S(1)}, u32[]{:S(2)}, u32[]{:S(2)}) %collective-permute-start.2) | collective-permute-done | bytes 12320 | tf_op jit(solution)/shard_map/ppermute | solution.py:284
  11.4 7.9 %all-to-all-start.1 = ((bf16[16,296,128]{2,1,0:T(8,128)(2,1)}), bf16[16,296,128]{2,1,0:T(8,128)(2,1)S(1)}, u32[]{:S(2)}, u32[]{:S(2)}) async-start(bf16[16,296,128]{2,1,0:T(8,128)(2,1)} %products.1), calls=%async_computation.1 | async-start | bytes 2424832 | tf_op jit(solution)/shard_map/all_to_all | solution.py:298
  19.3 0.0 copy-done.5
  19.3 3.1 %collective-permute-start.1 = (f32[3,64,1024]{2,1,0:T(8,128)S(1)}, f32[3,64,1024]{2,1,0:T(8,128)S(1)}, u32[]{:S(2)}, u32[]{:S(2)}) collective-permute-start(f32[3,64,1024]{2,1,0:T(8,128)S(1)} %bitcast.11), channel_id=1, source_target_pairs={{16,0},{1,17},{18,2},{3,19},{20,4},{5,21},{22,6},{7,23},{24,8},{9,... | collective-permute-start | bytes 2359304 | tf_op jit(solution)/shard_map/ppermute | solution.py:301
  22.4 5.5 %collective-permute-start = (f32[3,64,1024]{2,1,0:T(8,128)S(1)}, f32[3,64,1024]{2,1,0:T(8,128)}, u32[]{:S(2)}, u32[]{:S(2)}) collective-permute-start(f32[3,64,1024]{2,1,0:T(8,128)S(1)} %bitcast.12), channel_id=1, source_target_pairs={{0,16},{17,1},{2,18},{19,3},{4,20},{21,5},{6,22},{23,7},{8,24},{25... | collective-permute-start | bytes 2359304 | tf_op jit(solution)/shard_map/ppermute | solution.py:300
  27.9 11.1 %collective-permute-done.1.two_ref = f32[3,64,1024]{2,1,0:T(8,128)S(1)} collective-permute-done((f32[3,64,1024]{2,1,0:T(8,128)S(1)}, f32[3,64,1024]{2,1,0:T(8,128)S(1)}, u32[]{:S(2)}, u32[]{:S(2)}) %collective-permute-start.1) | collective-permute-done | bytes 786464 | tf_op jit(solution)/shard_map/ppermute | solution.py:301
  39.0 2.5 %collective-permute-done.one_ref = f32[3,64,1024]{2,1,0:T(8,128)} collective-permute-done((f32[3,64,1024]{2,1,0:T(8,128)S(1)}, f32[3,64,1024]{2,1,0:T(8,128)}, u32[]{:S(2)}, u32[]{:S(2)}) %collective-permute-start) | collective-permute-done | bytes 786464 | tf_op jit(solution)/shard_map/ppermute | solution.py:300
  41.5 0.0 copy-done.6
  41.5 3.8 %strain.1 = (bf16[16,192,128]{2,1,0:T(8,128)(2,1)}, f32[64,1024]{1,0:T(8,128)S(1)}) custom-call(bf16[144,1024]{1,0:T(8,128)(2,1)S(1)} %copy-done.6, f32[3,64,1024]{2,1,0:T(8,128)S(1)} %bitcast.13, f32[3,64,1024]{2,1,0:T(8,128)} %collective-permute-done.one_ref, f32[3,64,1024]{2,1,0:T(8,128)S(1)} %collective-permute-done.1.two_ref, f32[1,1]{1,0:T(1,128)} %bitcast.1.sense_ref, ...), custom_call_target="tpu_custom_call" | custom-call | flops 805306368 | bytes 4456448 | tf_op jit(solution)/shard_map/strain/pallas_call | solution.py:36
  45.3 0.0 copy-start.1
  45.3 0.7 copy-done.1
  46.0 0.0 copy-start.3
  46.0 4.5 %all-to-all-done.1.recv_ref = bf16[16,296,128]{2,1,0:T(8,128)(2,1)S(1)} async-done(((bf16[16,296,128]{2,1,0:T(8,128)(2,1)}), bf16[16,296,128]{2,1,0:T(8,128)(2,1)S(1)}, u32[]{:S(2)}, u32[]{:S(2)}) %all-to-all-start.1) | async-done | bytes 1212448 | tf_op jit(solution)/shard_map/all_to_all | solution.py:298
  50.5 5.6 %all-to-all-start = ((bf16[16,192,128]{2,1,0:T(8,128)(2,1)}), bf16[16,192,128]{2,1,0:T(8,128)(2,1)S(1)}, u32[]{:S(2)}, u32[]{:S(2)}) async-start(bf16[16,192,128]{2,1,0:T(8,128)(2,1)} %get-tuple-element.11), calls=%async_computation | async-start | bytes 1572864 | tf_op jit(solution)/shard_map/all_to_all | solution.py:312
  56.1 0.0 copy-done.3
  56.1 1.7 %smooth.1 = (bf16[3,64,1024]{2,1,0:T(8,128)(2,1)}, f32[16,1024]{1,0:T(8,128)S(1)}) custom-call(bf16[32,1024]{1,0:T(8,128)(2,1)S(1)} %copy-done.3, bf16[16,296,128]{2,1,0:T(8,128)(2,1)S(1)} %all-to-all-done.1.recv_ref), custom_call_target="tpu_custom_call" | custom-call | flops 536870912 | bytes 2097152 | tf_op jit(solution)/shard_map/smooth/pallas_call | solution.py:36
  57.8 0.0 copy-start
  57.8 2.0 %collective-permute-start.5 = (bf16[3,64,1024]{2,1,0:T(8,128)(2,1)}, bf16[3,64,1024]{2,1,0:T(8,128)(2,1)S(1)}, u32[]{:S(2)}, u32[]{:S(2)}) collective-permute-start(bf16[3,64,1024]{2,1,0:T(8,128)(2,1)} %get-tuple-element.13.smooth_ref), channel_id=1, source_target_pairs={{16,0},{1,17},{18,2},{3,19},{20,4},{5,21},{22,6},{7,23},{24,8},{9,... | collective-permute-start | bytes 1179656 | tf_op jit(solution)/shard_map/ppermute | solution.py:326
  59.8 6.7 %collective-permute-start.4 = (bf16[3,64,1024]{2,1,0:T(8,128)(2,1)}, bf16[3,64,1024]{2,1,0:T(8,128)(2,1)S(1)}, u32[]{:S(2)}, u32[]{:S(2)}) collective-permute-start(bf16[3,64,1024]{2,1,0:T(8,128)(2,1)} %get-tuple-element.13.smooth_ref), channel_id=1, source_target_pairs={{0,16},{17,1},{2,18},{19,3},{4,20},{21,5},{6,22},{23,7},{8,24},{25... | collective-permute-start | bytes 1179656 | tf_op jit(solution)/shard_map/ppermute | solution.py:325
  66.5 1.1 %squares.1.squares_ref = bf16[6,64,1024]{2,1,0:T(8,128)(2,1)S(1)} custom-call(bf16[32,1024]{1,0:T(8,128)(2,1)S(1)} %copy-done.3, bf16[16,296,128]{2,1,0:T(8,128)(2,1)S(1)} %all-to-all-done.1.recv_ref), custom_call_target="tpu_custom_call" | custom-call | flops 805306368 | bytes 1572864 | tf_op jit(solution)/shard_map/squares/pallas_call | solution.py:36
  67.7 2.6 %collective-permute-done.5.two_ref = bf16[3,64,1024]{2,1,0:T(8,128)(2,1)S(1)} collective-permute-done((bf16[3,64,1024]{2,1,0:T(8,128)(2,1)}, bf16[3,64,1024]{2,1,0:T(8,128)(2,1)S(1)}, u32[]{:S(2)}, u32[]{:S(2)}) %collective-permute-start.5) | collective-permute-done | bytes 393248 | tf_op jit(solution)/shard_map/ppermute | solution.py:326
  70.2 2.0 %collective-permute-done.4.one_ref = bf16[3,64,1024]{2,1,0:T(8,128)(2,1)S(1)} collective-permute-done((bf16[3,64,1024]{2,1,0:T(8,128)(2,1)}, bf16[3,64,1024]{2,1,0:T(8,128)(2,1)S(1)}, u32[]{:S(2)}, u32[]{:S(2)}) %collective-permute-start.4) | collective-permute-done | bytes 393248 | tf_op jit(solution)/shard_map/ppermute | solution.py:325
  72.2 0.0 copy-done
  72.2 1.1 %model.1.model_ref = f32[6,64,1024]{2,1,0:T(8,128)S(1)} custom-call(bf16[3,64,1024]{2,1,0:T(8,128)(2,1)S(1)} %copy-done, bf16[3,64,1024]{2,1,0:T(8,128)(2,1)S(1)} %collective-permute-done.4.one_ref, bf16[3,64,1024]{2,1,0:T(8,128)(2,1)S(1)} %collective-permute-done.5.two_ref, f32[1,1]{1,0:T(1,128)} %bitcast.1.sense_ref, ...), custom_call_target="tpu_custom_call" | custom-call | flops 6553600 | bytes 1572864 | tf_op jit(solution)/shard_map/model/pallas_call | solution.py:36
  73.3 5.5 %all-to-all-done.recv_ref = bf16[16,192,128]{2,1,0:T(8,128)(2,1)S(1)} async-done(((bf16[16,192,128]{2,1,0:T(8,128)(2,1)}), bf16[16,192,128]{2,1,0:T(8,128)(2,1)S(1)}, u32[]{:S(2)}, u32[]{:S(2)}) %all-to-all-start) | async-done | bytes 786464 | tf_op jit(solution)/shard_map/all_to_all | solution.py:312
  78.8 0.0 copy-start.4
  78.8 0.8 copy-done.4
  79.6 0.0 copy-start.2
  79.6 1.3 %sums.1 = f32[16,1,128]{2,1,0:T(1,128)S(1)} custom-call(bf16[32,1024]{1,0:T(8,128)(2,1)S(1)} %copy-done.4, bf16[16,192,128]{2,1,0:T(8,128)(2,1)S(1)} %all-to-all-done.recv_ref, bf16[3,64,1024]{2,1,0:T(8,128)(2,1)S(1)} %copy-done, bf16[6,64,1024]{2,1,0:T(8,128)(2,1)S(1)} %squares.1.squares_ref, f32[6,64,1024]{2,1,0:T(8,128)S(1)} %model.1.model_ref), custom_call_target="tpu_custom_call" | custom-call | flops 805306368 | bytes 3145728 | tf_op jit(solution)/shard_map/sums/pallas_call | solution.py:36
  80.9 12.3 %all_to_all.15.refs_0_ = f32[16,1,128]{2,1,0:T(1,128)S(1)} all-to-all(f32[16,1,128]{2,1,0:T(1,128)S(1)} %sums.1), channel_id=1, replica_groups=mesh['py'=32,'pz'=16] {'pz'}, dimensions={0} | all-to-all | bytes 16384 | tf_op jit(solution)/shard_map/all_to_all | solution.py:351
  93.2 0.0 copy-done.2
  93.2 0.8 viscosity.1
Async XLA Ops:
  1.6 6.8 %collective-permute-start.3 = (f32[3,1,1024]{2,1,0:T(1,128)S(1)}, f32[3,1,1024]{2,1,0:T(1,128)S(1)}, u32[]{:S(2)}, u32[]{:S(2)}) collective-permute-start(f32[3,1,1024]{2,1,0:T(1,128)S(1)} %get-tuple-element.18), channel_id=1, source_target_pairs={{1,0},{2,1},{3,2},{4,3},{5,4},{6,5},{7,6},{8,7},{9,8},{10,9},{11,1... | collective-permute-start | bytes 36872 | tf_op jit(solution)/shard_map/ppermute | solution.py:285
  2.3 9.2 %collective-permute-start.2 = (f32[3,1,1024]{2,1,0:T(1,128)S(1)}, f32[3,1,1024]{2,1,0:T(1,128)S(1)}, u32[]{:S(2)}, u32[]{:S(2)}) collective-permute-start(f32[3,1,1024]{2,1,0:T(1,128)S(1)} %get-tuple-element.19), channel_id=1, source_target_pairs={{0,1},{1,2},{2,3},{3,4},{4,5},{5,6},{6,7},{7,8},{8,9},{9,10},{10,1... | collective-permute-start | bytes 36872 | tf_op jit(solution)/shard_map/ppermute | solution.py:284
  8.4 10.9 %copy-start.5 = (f32[3,1,64,1024]{3,2,1,0:T(8,128)S(1)}, f32[3,1,64,1024]{3,2,1,0:T(8,128)}, u32[]{:S(2)}) copy-start(f32[3,1,64,1024]{3,2,1,0:T(8,128)} %param.3) | copy-start | bytes 2359300
  8.4 33.1 %copy-start.6 = (bf16[144,1024]{1,0:T(8,128)(2,1)S(1)}, bf16[144,1024]{1,0:T(8,128)(2,1)}, u32[]{:S(2)}) copy-start(bf16[144,1024]{1,0:T(8,128)(2,1)} %constant.23.clone.table_ref) | copy-start | bytes 884740
  11.4 39.1 %all-to-all-start.1 = ((bf16[16,296,128]{2,1,0:T(8,128)(2,1)}), bf16[16,296,128]{2,1,0:T(8,128)(2,1)S(1)}, u32[]{:S(2)}, u32[]{:S(2)}) async-start(bf16[16,296,128]{2,1,0:T(8,128)(2,1)} %products.1), calls=%async_computation.1 | async-start | bytes 2424832 | tf_op jit(solution)/shard_map/all_to_all | solution.py:298
  19.3 19.7 %collective-permute-start.1 = (f32[3,64,1024]{2,1,0:T(8,128)S(1)}, f32[3,64,1024]{2,1,0:T(8,128)S(1)}, u32[]{:S(2)}, u32[]{:S(2)}) collective-permute-start(f32[3,64,1024]{2,1,0:T(8,128)S(1)} %bitcast.11), channel_id=1, source_target_pairs={{16,0},{1,17},{18,2},{3,19},{20,4},{5,21},{22,6},{7,23},{24,8},{9,... | collective-permute-start | bytes 2359304 | tf_op jit(solution)/shard_map/ppermute | solution.py:301
  22.4 19.1 %collective-permute-start = (f32[3,64,1024]{2,1,0:T(8,128)S(1)}, f32[3,64,1024]{2,1,0:T(8,128)}, u32[]{:S(2)}, u32[]{:S(2)}) collective-permute-start(f32[3,64,1024]{2,1,0:T(8,128)S(1)} %bitcast.12), channel_id=1, source_target_pairs={{0,16},{17,1},{2,18},{19,3},{4,20},{21,5},{6,22},{23,7},{8,24},{25... | collective-permute-start | bytes 2359304 | tf_op jit(solution)/shard_map/ppermute | solution.py:300
  45.3 0.7 copy-start.1
  46.0 10.1 %copy-start.3 = (bf16[32,1024]{1,0:T(8,128)(2,1)S(1)}, bf16[32,1024]{1,0:T(8,128)(2,1)}, u32[]{:S(2)}) copy-start(bf16[32,1024]{1,0:T(8,128)(2,1)} %constant.24.clone.table_ref) | copy-start | bytes 196612
  50.5 28.2 %all-to-all-start = ((bf16[16,192,128]{2,1,0:T(8,128)(2,1)}), bf16[16,192,128]{2,1,0:T(8,128)(2,1)S(1)}, u32[]{:S(2)}, u32[]{:S(2)}) async-start(bf16[16,192,128]{2,1,0:T(8,128)(2,1)} %get-tuple-element.11), calls=%async_computation | async-start | bytes 1572864 | tf_op jit(solution)/shard_map/all_to_all | solution.py:312
  57.8 14.4 %copy-start = (bf16[3,64,1024]{2,1,0:T(8,128)(2,1)S(1)}, bf16[3,64,1024]{2,1,0:T(8,128)(2,1)}, u32[]{:S(2)}) copy-start(bf16[3,64,1024]{2,1,0:T(8,128)(2,1)} %get-tuple-element.13.smooth_ref) | copy-start | bytes 1179652
  57.8 12.5 %collective-permute-start.5 = (bf16[3,64,1024]{2,1,0:T(8,128)(2,1)}, bf16[3,64,1024]{2,1,0:T(8,128)(2,1)S(1)}, u32[]{:S(2)}, u32[]{:S(2)}) collective-permute-start(bf16[3,64,1024]{2,1,0:T(8,128)(2,1)} %get-tuple-element.13.smooth_ref), channel_id=1, source_target_pairs={{16,0},{1,17},{18,2},{3,19},{20,4},{5,21},{22,6},{7,23},{24,8},{9,... | collective-permute-start | bytes 1179656 | tf_op jit(solution)/shard_map/ppermute | solution.py:326
  59.8 12.4 %collective-permute-start.4 = (bf16[3,64,1024]{2,1,0:T(8,128)(2,1)}, bf16[3,64,1024]{2,1,0:T(8,128)(2,1)S(1)}, u32[]{:S(2)}, u32[]{:S(2)}) collective-permute-start(bf16[3,64,1024]{2,1,0:T(8,128)(2,1)} %get-tuple-element.13.smooth_ref), channel_id=1, source_target_pairs={{0,16},{17,1},{2,18},{19,3},{4,20},{21,5},{6,22},{23,7},{8,24},{25... | collective-permute-start | bytes 1179656 | tf_op jit(solution)/shard_map/ppermute | solution.py:325
  78.8 0.8 copy-start.4
  79.6 13.6 %copy-start.2 = (f32[64,1024]{1,0:T(8,128)S(1)}, f32[64,1024]{1,0:T(8,128)}, u32[]{:S(2)}) copy-start(f32[64,1024]{1,0:T(8,128)} %copy-done.1) | copy-start | bytes 786436

commit v7 on v6

--- a/solution.py
+++ b/solution.py
@@ -12,7 +12,7 @@
 pair_weights = (1.0, 1.0, 1.0, 2.0, 2.0, 2.0)
 epsilon = 1e-06
 LANES = 128
-BAND = 32
+BAND = 8
 
 
 def filter_table(length):
@@ -167,7 +167,7 @@
     send_blocks(table_ref, fields_ref, block_ref, out_ref, sem, 6, depth, False)
 
 
-def smooth_kernel(table_ref, recv_ref, smooth_ref, edges_ref, lines_ref):
+def smooth_kernel(table_ref, recv_ref, smooth_ref, edges_ref, band_ref, lines_ref):
     senders = recv_ref.shape[0]
     _, width, length = smooth_ref.shape
     for t in range(senders // 2):
@@ -182,6 +182,7 @@
     for a in range(3):
         smooth_ref[a] = got[a * width : (a + 1) * width, :]
     edges_ref[...] = got[3 * width :, :].astype(jnp.float32)
+    band_ref[...] = table_ref[...]
 
 
 def squares_kernel(table_ref, recv_ref, squares_ref, lines_ref):
@@ -311,11 +312,12 @@
     )(lanes_x, velocity, one, two, sense, first, last)
     received_strain = lax.all_to_all(send_strain, "pz", 0, 0, tiled=True)
 
-    smooth, edges = call(
+    smooth, edges, band = call(
         smooth_kernel,
         (
             jax.ShapeDtypeStruct((3, width, nz), bf16),
             jax.ShapeDtypeStruct((16, nz), f32),
+            jax.ShapeDtypeStruct((BAND, nz), bf16),
         ),
         2 * 4 * width * nz * nz,
         2 * nz * nz,
@@ -347,7 +349,7 @@
         48 * width * nz,
         [vmem((6 * width, nz), bf16)],
         "sums",
-    )(lanes_z, received_strain, smooth, squares, model)
+    )(band, received_strain, smooth, squares, model)
     totals = lax.all_to_all(sums, "pz", 0, 0, tiled=True)
     cells = nx * nz
     nu_t = call(

time: 94.6 us -> 93.7 us (level)
  no operation moved by 1% of the time
where the time goes in v7:
time: 93.7 us; the launch traced here: 93.2 us
  starting transfers between devices  33.4 us (36%)
  waiting for transfers between devices  31.1 us (33%)
  Pallas kernels  13.9 us (15%)
  blocking collectives  12.3 us (13%)
  local copies, waits for them, and re-layouts  1.68 us (2%)
    pallas_call x7, Pallas kernels, run(): pl.pallas_call(kernel, out_shape=out_shape, in_specs=[space(i) for i in r...  13.9 us
    all_to_all x1, blocking collectives, body(): totals = lax.all_to_all(sums, 'pz', 0, 0, tiled=True)  12.3 us
    ppermute x1, waiting for transfers between devices, body(): two = lax.ppermute(velocity, ('py', 'pz'), inward)  11.1 us
    all_to_all x1, starting transfers between devices, body(): received = lax.all_to_all(send, 'pz', 0, 0, tiled=True)  7.86 us
    ppermute x1, starting transfers between devices, body(): smooth_one = lax.ppermute(smooth, ('py', 'pz'), outward)  6.68 us
    all_to_all x1, starting transfers between devices, body(): received_strain = lax.all_to_all(send_strain, 'pz', 0, 0, tiled=True)  5.57 us
    ppermute x1, starting transfers between devices, body(): one = lax.ppermute(velocity, ('py', 'pz'), outward)  5.48 us
    all_to_all x1, waiting for transfers between devices, body(): received_strain = lax.all_to_all(send_strain, 'pz', 0, 0, tiled=True)  5.48 us
  transfers between devices with their start and end apart: 8, of which 7 were waited for; matrix products, arithmetic and copies ran while one was open for 0% of the time, Pallas kernels for 13%

profile of v7, /device:TPU:33, one launch (start us, length us, event | category | flops | bytes accessed | tf_op | source)
XLA Modules:
  0.0 93.2 jit_solution(11892093086305910713)
XLA Ops:
  0.6 1.0 %fusion = (f32[3,1,1024]{2,1,0:T(1,128)S(1)}, f32[3,1,1024]{2,1,0:T(1,128)S(1)}) fusion(f32[3,64,1024]{2,1,0:T(8,128)} %bitcast.9), kind=kLoop, calls=%fused_computation | loop fusion | bytes 49152 | tf_op jit(solution)/shard_map/slice | solution.py:286
  1.6 0.7 collective-permute-start.1
  2.3 2.0 %collective-permute-start = (f32[3,1,1024]{2,1,0:T(1,128)S(1)}, f32[3,1,1024]{2,1,0:T(1,128)S(1)}, u32[]{:S(2)}, u32[]{:S(2)}) collective-permute-start(f32[3,1,1024]{2,1,0:T(1,128)S(1)} %get-tuple-element.21), channel_id=1, source_target_pairs={{0,1},{1,2},{2,3},{3,4},{4,5},{5,6},{6,7},{7,8},{8,9},{9,10},{10,1... | collective-permute-start | bytes 36872 | tf_op jit(solution)/shard_map/ppermute | solution.py:285
  4.3 4.1 %products.1 = bf16[16,296,128]{2,1,0:T(8,128)(2,1)} custom-call(bf16[144,1024]{1,0:T(8,128)(2,1)} %constant.23.clone.table_ref, f32[3,64,1024]{2,1,0:T(8,128)} %bitcast.10), custom_call_target="tpu_custom_call" | custom-call | flops 1207959552 | bytes 2883584 | tf_op jit(solution)/shard_map/products/pallas_call | solution.py:36
  8.4 0.0 copy-start.3
  8.4 0.0 copy-start.4
  8.4 0.0 collective-permute-done.1.last_ref
  8.4 3.0 %collective-permute-done.first_ref = f32[3,1,1024]{2,1,0:T(1,128)S(1)} collective-permute-done((f32[3,1,1024]{2,1,0:T(1,128)S(1)}, f32[3,1,1024]{2,1,0:T(1,128)S(1)}, u32[]{:S(2)}, u32[]{:S(2)}) %collective-permute-start) | collective-permute-done | bytes 12320 | tf_op jit(solution)/shard_map/ppermute | solution.py:285
  11.4 7.9 %all-to-all-start = ((bf16[16,296,128]{2,1,0:T(8,128)(2,1)}), bf16[16,296,128]{2,1,0:T(8,128)(2,1)S(1)}, u32[]{:S(2)}, u32[]{:S(2)}) async-start(bf16[16,296,128]{2,1,0:T(8,128)(2,1)} %products.1), calls=%async_computation | async-start | bytes 2424832 | tf_op jit(solution)/shard_map/all_to_all | solution.py:299
  19.3 0.0 copy-done.3
  19.3 3.1 %collective-permute-start.3 = (f32[3,64,1024]{2,1,0:T(8,128)S(1)}, f32[3,64,1024]{2,1,0:T(8,128)S(1)}, u32[]{:S(2)}, u32[]{:S(2)}) collective-permute-start(f32[3,64,1024]{2,1,0:T(8,128)S(1)} %bitcast.11), channel_id=1, source_target_pairs={{16,0},{1,17},{18,2},{3,19},{20,4},{5,21},{22,6},{7,23},{24,8},{9,... | collective-permute-start | bytes 2359304 | tf_op jit(solution)/shard_map/ppermute | solution.py:302
  22.4 5.5 %collective-permute-start.2 = (f32[3,64,1024]{2,1,0:T(8,128)S(1)}, f32[3,64,1024]{2,1,0:T(8,128)}, u32[]{:S(2)}, u32[]{:S(2)}) collective-permute-start(f32[3,64,1024]{2,1,0:T(8,128)S(1)} %bitcast.12), channel_id=1, source_target_pairs={{0,16},{17,1},{2,18},{19,3},{4,20},{21,5},{6,22},{23,7},{8,24},{25... | collective-permute-start | bytes 2359304 | tf_op jit(solution)/shard_map/ppermute | solution.py:301
  27.9 11.1 %collective-permute-done.3.two_ref = f32[3,64,1024]{2,1,0:T(8,128)S(1)} collective-permute-done((f32[3,64,1024]{2,1,0:T(8,128)S(1)}, f32[3,64,1024]{2,1,0:T(8,128)S(1)}, u32[]{:S(2)}, u32[]{:S(2)}) %collective-permute-start.3) | collective-permute-done | bytes 786464 | tf_op jit(solution)/shard_map/ppermute | solution.py:302
  39.0 2.5 %collective-permute-done.2.one_ref = f32[3,64,1024]{2,1,0:T(8,128)} collective-permute-done((f32[3,64,1024]{2,1,0:T(8,128)S(1)}, f32[3,64,1024]{2,1,0:T(8,128)}, u32[]{:S(2)}, u32[]{:S(2)}) %collective-permute-start.2) | collective-permute-done | bytes 786464 | tf_op jit(solution)/shard_map/ppermute | solution.py:301
  41.5 0.0 copy-done.4
  41.5 3.8 %strain.1 = (bf16[16,192,128]{2,1,0:T(8,128)(2,1)}, f32[64,1024]{1,0:T(8,128)S(1)}) custom-call(bf16[144,1024]{1,0:T(8,128)(2,1)S(1)} %copy-done.4, f32[3,64,1024]{2,1,0:T(8,128)S(1)} %bitcast.13, f32[3,64,1024]{2,1,0:T(8,128)} %collective-permute-done.2.one_ref, f32[3,64,1024]{2,1,0:T(8,128)S(1)} %collective-permute-done.3.two_ref, ...), custom_call_target="tpu_custom_call" | custom-call | flops 805306368 | bytes 4456448 | tf_op jit(solution)/shard_map/strain/pallas_call | solution.py:36
  45.3 0.0 copy-start.1
  45.3 0.7 copy-done.1
  46.0 0.0 copy-start.5
  46.0 4.5 %all-to-all-done.recv_ref = bf16[16,296,128]{2,1,0:T(8,128)(2,1)S(1)} async-done(((bf16[16,296,128]{2,1,0:T(8,128)(2,1)}), bf16[16,296,128]{2,1,0:T(8,128)(2,1)S(1)}, u32[]{:S(2)}, u32[]{:S(2)}) %all-to-all-start) | async-done | bytes 1212448 | tf_op jit(solution)/shard_map/all_to_all | solution.py:299
  50.5 5.6 %all-to-all-start.1 = ((bf16[16,192,128]{2,1,0:T(8,128)(2,1)}), bf16[16,192,128]{2,1,0:T(8,128)(2,1)S(1)}, u32[]{:S(2)}, u32[]{:S(2)}) async-start(bf16[16,192,128]{2,1,0:T(8,128)(2,1)} %get-tuple-element.14), calls=%async_computation.1 | async-start | bytes 1572864 | tf_op jit(solution)/shard_map/all_to_all | solution.py:313
  56.1 0.0 copy-done.5
  56.1 1.7 %smooth.1 = (bf16[3,64,1024]{2,1,0:T(8,128)(2,1)}, f32[16,1024]{1,0:T(8,128)S(1)}, bf16[8,1024]{1,0:T(8,128)(2,1)S(1)}) custom-call(bf16[8,1024]{1,0:T(8,128)(2,1)S(1)} %copy-done.5, bf16[16,296,128]{2,1,0:T(8,128)(2,1)S(1)} %all-to-all-done.recv_ref), custom_call_target="tpu_custom_call" | custom-call | flops 536870912 | bytes 2097152 | tf_op jit(solution)/shard_map/smooth/pallas_call | solution.py:36
  57.8 0.0 copy-start
  57.8 2.0 %collective-permute-start.5 = (bf16[3,64,1024]{2,1,0:T(8,128)(2,1)}, bf16[3,64,1024]{2,1,0:T(8,128)(2,1)S(1)}, u32[]{:S(2)}, u32[]{:S(2)}) collective-permute-start(bf16[3,64,1024]{2,1,0:T(8,128)(2,1)} %get-tuple-element.15.smooth_ref), channel_id=1, source_target_pairs={{16,0},{1,17},{18,2},{3,19},{20,4},{5,21},{22,6},{7,23},{24,8},{9,... | collective-permute-start | bytes 1179656 | tf_op jit(solution)/shard_map/ppermute | solution.py:328
  59.8 6.7 %collective-permute-start.4 = (bf16[3,64,1024]{2,1,0:T(8,128)(2,1)}, bf16[3,64,1024]{2,1,0:T(8,128)(2,1)S(1)}, u32[]{:S(2)}, u32[]{:S(2)}) collective-permute-start(bf16[3,64,1024]{2,1,0:T(8,128)(2,1)} %get-tuple-element.15.smooth_ref), channel_id=1, source_target_pairs={{0,16},{17,1},{2,18},{19,3},{4,20},{21,5},{6,22},{23,7},{8,24},{25... | collective-permute-start | bytes 1179656 | tf_op jit(solution)/shard_map/ppermute | solution.py:327
  66.5 1.1 %squares.1.squares_ref = bf16[6,64,1024]{2,1,0:T(8,128)(2,1)S(1)} custom-call(bf16[8,1024]{1,0:T(8,128)(2,1)S(1)} %copy-done.5, bf16[16,296,128]{2,1,0:T(8,128)(2,1)S(1)} %all-to-all-done.recv_ref), custom_call_target="tpu_custom_call" | custom-call | flops 805306368 | bytes 1572864 | tf_op jit(solution)/shard_map/squares/pallas_call | solution.py:36
  67.7 2.6 %collective-permute-done.5.two_ref = bf16[3,64,1024]{2,1,0:T(8,128)(2,1)S(1)} collective-permute-done((bf16[3,64,1024]{2,1,0:T(8,128)(2,1)}, bf16[3,64,1024]{2,1,0:T(8,128)(2,1)S(1)}, u32[]{:S(2)}, u32[]{:S(2)}) %collective-permute-start.5) | collective-permute-done | bytes 393248 | tf_op jit(solution)/shard_map/ppermute | solution.py:328
  70.2 2.0 %collective-permute-done.4.one_ref = bf16[3,64,1024]{2,1,0:T(8,128)(2,1)S(1)} collective-permute-done((bf16[3,64,1024]{2,1,0:T(8,128)(2,1)}, bf16[3,64,1024]{2,1,0:T(8,128)(2,1)S(1)}, u32[]{:S(2)}, u32[]{:S(2)}) %collective-permute-start.4) | collective-permute-done | bytes 393248 | tf_op jit(solution)/shard_map/ppermute | solution.py:327
  72.2 0.0 copy-done
  72.2 1.1 %model.1.model_ref = f32[6,64,1024]{2,1,0:T(8,128)S(1)} custom-call(bf16[3,64,1024]{2,1,0:T(8,128)(2,1)S(1)} %copy-done, bf16[3,64,1024]{2,1,0:T(8,128)(2,1)S(1)} %collective-permute-done.4.one_ref, bf16[3,64,1024]{2,1,0:T(8,128)(2,1)S(1)} %collective-permute-done.5.two_ref, f32[1,1]{1,0:T(1,128)} %bitcast.1.sense_ref, ...), custom_call_target="tpu_custom_call" | custom-call | flops 6553600 | bytes 1572864 | tf_op jit(solution)/shard_map/model/pallas_call | solution.py:36
  73.3 5.5 %all-to-all-done.1.recv_ref = bf16[16,192,128]{2,1,0:T(8,128)(2,1)S(1)} async-done(((bf16[16,192,128]{2,1,0:T(8,128)(2,1)}), bf16[16,192,128]{2,1,0:T(8,128)(2,1)S(1)}, u32[]{:S(2)}, u32[]{:S(2)}) %all-to-all-start.1) | async-done | bytes 786464 | tf_op jit(solution)/shard_map/all_to_all | solution.py:313
  78.8 0.0 copy-start.2
  78.8 1.3 %sums.1 = f32[16,1,128]{2,1,0:T(1,128)S(1)} custom-call(bf16[8,1024]{1,0:T(8,128)(2,1)S(1)} %get-tuple-element.11.table_ref, bf16[16,192,128]{2,1,0:T(8,128)(2,1)S(1)} %all-to-all-done.1.recv_ref, bf16[3,64,1024]{2,1,0:T(8,128)(2,1)S(1)} %copy-done, bf16[6,64,1024]{2,1,0:T(8,128)(2,1)S(1)} %squares.1.squares_ref, f32[6,64,1024]{2,1,0:T(8,128)S(1)} %model.1.model_ref), custom_call_target="tpu_custom_call" | custom-call | flops 805306368 | bytes 3145728 | tf_op jit(solution)/shard_map/sums/pallas_call | solution.py:36
  80.1 12.3 %all_to_all.15.refs_0_ = f32[16,1,128]{2,1,0:T(1,128)S(1)} all-to-all(f32[16,1,128]{2,1,0:T(1,128)S(1)} %sums.1), channel_id=1, replica_groups=mesh['py'=32,'pz'=16] {'pz'}, dimensions={0} | all-to-all | bytes 16384 | tf_op jit(solution)/shard_map/all_to_all | solution.py:353
  92.4 0.0 copy-done.2
  92.4 0.8 viscosity.1
Async XLA Ops:
  1.6 6.8 %collective-permute-start.1 = (f32[3,1,1024]{2,1,0:T(1,128)S(1)}, f32[3,1,1024]{2,1,0:T(1,128)S(1)}, u32[]{:S(2)}, u32[]{:S(2)}) collective-permute-start(f32[3,1,1024]{2,1,0:T(1,128)S(1)} %get-tuple-element.20), channel_id=1, source_target_pairs={{1,0},{2,1},{3,2},{4,3},{5,4},{6,5},{7,6},{8,7},{9,8},{10,9},{11,1... | collective-permute-start | bytes 36872 | tf_op jit(solution)/shard_map/ppermute | solution.py:286
  2.3 9.2 %collective-permute-start = (f32[3,1,1024]{2,1,0:T(1,128)S(1)}, f32[3,1,1024]{2,1,0:T(1,128)S(1)}, u32[]{:S(2)}, u32[]{:S(2)}) collective-permute-start(f32[3,1,1024]{2,1,0:T(1,128)S(1)} %get-tuple-element.21), channel_id=1, source_target_pairs={{0,1},{1,2},{2,3},{3,4},{4,5},{5,6},{6,7},{7,8},{8,9},{9,10},{10,1... | collective-permute-start | bytes 36872 | tf_op jit(solution)/shard_map/ppermute | solution.py:285
  8.4 10.9 %copy-start.3 = (f32[3,1,64,1024]{3,2,1,0:T(8,128)S(1)}, f32[3,1,64,1024]{3,2,1,0:T(8,128)}, u32[]{:S(2)}) copy-start(f32[3,1,64,1024]{3,2,1,0:T(8,128)} %param.3) | copy-start | bytes 2359300
  8.4 33.1 %copy-start.4 = (bf16[144,1024]{1,0:T(8,128)(2,1)S(1)}, bf16[144,1024]{1,0:T(8,128)(2,1)}, u32[]{:S(2)}) copy-start(bf16[144,1024]{1,0:T(8,128)(2,1)} %constant.23.clone.table_ref) | copy-start | bytes 884740
  11.4 39.1 %all-to-all-start = ((bf16[16,296,128]{2,1,0:T(8,128)(2,1)}), bf16[16,296,128]{2,1,0:T(8,128)(2,1)S(1)}, u32[]{:S(2)}, u32[]{:S(2)}) async-start(bf16[16,296,128]{2,1,0:T(8,128)(2,1)} %products.1), calls=%async_computation | async-start | bytes 2424832 | tf_op jit(solution)/shard_map/all_to_all | solution.py:299
  19.3 19.7 %collective-permute-start.3 = (f32[3,64,1024]{2,1,0:T(8,128)S(1)}, f32[3,64,1024]{2,1,0:T(8,128)S(1)}, u32[]{:S(2)}, u32[]{:S(2)}) collective-permute-start(f32[3,64,1024]{2,1,0:T(8,128)S(1)} %bitcast.11), channel_id=1, source_target_pairs={{16,0},{1,17},{18,2},{3,19},{20,4},{5,21},{22,6},{7,23},{24,8},{9,... | collective-permute-start | bytes 2359304 | tf_op jit(solution)/shard_map/ppermute | solution.py:302
  22.4 19.1 %collective-permute-start.2 = (f32[3,64,1024]{2,1,0:T(8,128)S(1)}, f32[3,64,1024]{2,1,0:T(8,128)}, u32[]{:S(2)}, u32[]{:S(2)}) collective-permute-start(f32[3,64,1024]{2,1,0:T(8,128)S(1)} %bitcast.12), channel_id=1, source_target_pairs={{0,16},{17,1},{2,18},{19,3},{4,20},{21,5},{6,22},{23,7},{8,24},{25... | collective-permute-start | bytes 2359304 | tf_op jit(solution)/shard_map/ppermute | solution.py:301
  45.3 0.7 copy-start.1
  46.0 10.1 %copy-start.5 = (bf16[8,1024]{1,0:T(8,128)(2,1)S(1)}, bf16[8,1024]{1,0:T(8,128)(2,1)}, u32[]{:S(2)}) copy-start(bf16[8,1024]{1,0:T(8,128)(2,1)} %constant.24.clone.table_ref) | copy-start | bytes 49156
  50.5 28.2 %all-to-all-start.1 = ((bf16[16,192,128]{2,1,0:T(8,128)(2,1)}), bf16[16,192,128]{2,1,0:T(8,128)(2,1)S(1)}, u32[]{:S(2)}, u32[]{:S(2)}) async-start(bf16[16,192,128]{2,1,0:T(8,128)(2,1)} %get-tuple-element.14), calls=%async_computation.1 | async-start | bytes 1572864 | tf_op jit(solution)/shard_map/all_to_all | solution.py:313
  57.8 14.4 %copy-start = (bf16[3,64,1024]{2,1,0:T(8,128)(2,1)S(1)}, bf16[3,64,1024]{2,1,0:T(8,128)(2,1)}, u32[]{:S(2)}) copy-start(bf16[3,64,1024]{2,1,0:T(8,128)(2,1)} %get-tuple-element.15.smooth_ref) | copy-start | bytes 1179652
  57.8 12.5 %collective-permute-start.5 = (bf16[3,64,1024]{2,1,0:T(8,128)(2,1)}, bf16[3,64,1024]{2,1,0:T(8,128)(2,1)S(1)}, u32[]{:S(2)}, u32[]{:S(2)}) collective-permute-start(bf16[3,64,1024]{2,1,0:T(8,128)(2,1)} %get-tuple-element.15.smooth_ref), channel_id=1, source_target_pairs={{16,0},{1,17},{18,2},{3,19},{20,4},{5,21},{22,6},{7,23},{24,8},{9,... | collective-permute-start | bytes 1179656 | tf_op jit(solution)/shard_map/ppermute | solution.py:328
  59.8 12.4 %collective-permute-start.4 = (bf16[3,64,1024]{2,1,0:T(8,128)(2,1)}, bf16[3,64,1024]{2,1,0:T(8,128)(2,1)S(1)}, u32[]{:S(2)}, u32[]{:S(2)}) collective-permute-start(bf16[3,64,1024]{2,1,0:T(8,128)(2,1)} %get-tuple-element.15.smooth_ref), channel_id=1, source_target_pairs={{0,16},{17,1},{2,18},{19,3},{4,20},{21,5},{6,22},{23,7},{8,24},{25... | collective-permute-start | bytes 1179656 | tf_op jit(solution)/shard_map/ppermute | solution.py:327
  78.8 13.6 %copy-start.2 = (f32[64,1024]{1,0:T(8,128)S(1)}, f32[64,1024]{1,0:T(8,128)}, u32[]{:S(2)}) copy-start(f32[64,1024]{1,0:T(8,128)} %copy-done.1) | copy-start | bytes 786436

commit v8 on v7

--- a/solution.py
+++ b/solution.py
@@ -56,38 +56,40 @@
     return rows if blocks == 0 else jnp.concatenate([rows[:, at:], rows[:, :at]], axis=1)
 
 
-def table_rows(band_ref, first, last):
-    band = band_ref[:LANES, :]
-    return jnp.concatenate([turned(band, a) for a in range(first, last)], axis=0)
-
-
-def table_of(band):
+def tile_of(band):
     band = band.astype(jnp.float32)
     rows = [band] + [pltpu.roll(band, at, 1) for at in range(BAND, LANES, BAND)]
-    tile = jnp.concatenate(rows, axis=0).astype(jnp.bfloat16)
-    return jnp.concatenate([turned(tile, a) for a in range(band.shape[1] // LANES)], axis=0)
-
-
-def send_blocks(table_ref, fields_ref, block_ref, out_ref, sem, count, depth, edges):
+    return jnp.concatenate(rows, axis=0).astype(jnp.bfloat16)
+
+
+def table_rows(tile, first, last):
+    return jnp.concatenate([turned(tile, a) for a in range(first, last)], axis=0)
+
+
+def table_of(band):
+    tile = tile_of(band)
+    return table_rows(tile, 0, tile.shape[1] // LANES)
+
+
+def send_blocks(tile, seed, fields_ref, block_ref, out_ref, sem, count, depth):
     receivers = block_ref.shape[0]
     width = fields_ref.shape[1] // receivers
     per = LANES // depth
     full = count // per
-    if edges:
-        seed = table_ref[LANES:, :]
+    if seed is not None:
         beside = [turned(seed, q) for q in range(receivers * width // LANES)]
         beside = jnp.concatenate(beside, axis=0)
         got = nt(beside, fields_ref[: 2 * per * depth, :])
         row = lax.broadcasted_iota(jnp.int32, (receivers * 8, LANES), 0) % 8
         got = jnp.where(row < 2, got[:, :LANES], got[:, LANES:]).reshape(receivers, 8, LANES)
         block_ref[:, count * width // per :, :] = got.astype(jnp.bfloat16)
-    chunks = 2
+    chunks = sem.shape[0]
     some = receivers // chunks
     copies = []
     for c in range(chunks):
         mine = slice(c * some, (c + 1) * some)
         blocks = some * width // LANES
-        table = table_rows(table_ref, c * blocks, (c + 1) * blocks)
+        table = table_rows(tile, c * blocks, (c + 1) * blocks)
         for first in range(0, full, 2):
             here = min(2, full - first)
             got = nt(table, fields_ref[first * LANES : (first + here) * LANES, :])
@@ -131,7 +133,8 @@
     for p, (a, b) in enumerate(index_pairs):
         at = (3 + p) * depth
         fields_ref[at : at + depth, :] = (parts[a] * parts[b]).astype(jnp.bfloat16)
-    send_blocks(table_ref, fields_ref, block_ref, out_ref, sem, 9, depth, True)
+    tile, seed = table_ref[:LANES, :], table_ref[LANES:, :]
+    send_blocks(tile, seed, fields_ref, block_ref, out_ref, sem, 9, depth)
 
 
 def strain(gradients):
@@ -164,7 +167,8 @@
     magnitude_ref[...] = magnitude
     for p, part_value in enumerate(strain_parts):
         fields_ref[p * depth : (p + 1) * depth, :] = (magnitude * part_value).astype(jnp.bfloat16)
-    send_blocks(table_ref, fields_ref, block_ref, out_ref, sem, 6, depth, False)
+    tile = tile_of(table_ref[...])
+    send_blocks(tile, None, fields_ref, block_ref, out_ref, sem, 6, depth)
 
 
 def smooth_kernel(table_ref, recv_ref, smooth_ref, edges_ref, band_ref, lines_ref):
@@ -269,7 +273,9 @@
     for r in range(2):
         beside[r, :4] = table_x[[r * width - 1, (r + 1) * width] * 2]
     lanes_x = jnp.asarray(np.concatenate([table_x[:LANES], beside.reshape(16, nx)]))
-    lanes_z = jnp.asarray(table_z[:BAND])
+    short_x = jnp.asarray(table_x[:BAND])
+    same = np.array_equal(table_x[:BAND], table_z[:BAND])
+    lanes_z = short_x if same else jnp.asarray(table_z[:BAND])
     outward, inward = [], []
     for i in range(rows - 1):
         for j in range(parts):
@@ -282,20 +288,20 @@
     velocity = velocity.reshape(3, depth, nx)
     vmem, dma = pltpu.VMEM, pltpu.SemaphoreType.DMA
 
+    last = lax.ppermute(velocity[:, :1], "pz", back)
     first = lax.ppermute(velocity[:, -1:], "pz", around)
-    last = lax.ppermute(velocity[:, :1], "pz", back)
     send_shape = (parts, 9 * width // 2 + 8, LANES)
     send = call(
         products_kernel,
         jax.ShapeDtypeStruct(send_shape, bf16),
         2 * 9 * depth * nx * nx,
         12 * depth * nx + 2 * nx * nx,
-        [vmem((9 * depth, nx), bf16), vmem(send_shape, bf16), dma((2,))],
+        [vmem((9 * depth, nx), bf16), vmem(send_shape, bf16), dma((4,))],
         "products",
         (2,),
         58,
     )(lanes_x, velocity)
-    send, first, last = lax.optimization_barrier((send, first, last))
+    send, last, first = lax.optimization_barrier((send, last, first))
     received = lax.all_to_all(send, "pz", 0, 0, tiled=True)
 
     one = lax.ppermute(velocity, ("py", "pz"), outward)
@@ -309,7 +315,7 @@
         [vmem((6 * depth, nx), bf16), vmem(strain_shape, bf16), dma((2,))],
         "strain",
         (7,),
-    )(lanes_x, velocity, one, two, sense, first, last)
+    )(short_x, velocity, one, two, sense, first, last)
     received_strain = lax.all_to_all(send_strain, "pz", 0, 0, tiled=True)
 
     smooth, edges, band = call(

time: 93.7 us -> 94 us (level)
  starting transfers between devices: 33.4 us -> 36.8 us
  waiting for transfers between devices: 31.1 us -> 28.1 us
    all_to_all x1, starting transfers between devices: 7.86 us -> 11.4 us  [body(): received = lax.all_to_all(send, 'pz', 0, 0, tiled=True)]
    ppermute x1, waiting for transfers between devices: 3.01 us -> 0.01 us  [body(): first = lax.ppermute(velocity[:, -1:], 'pz', around)]
  transfers between devices with their start and end apart: 8 -> 8, of which waited for: 7 -> 6; matrix products, arithmetic and copies ran while one was open for 0% -> 0% of each run, Pallas kernels for 13% -> 12%
where the time goes in v8:
time: 94 us; the launch traced here: 93.5 us
  starting transfers between devices  36.8 us (39%)
  waiting for transfers between devices  28.1 us (30%)
  Pallas kernels  13.8 us (15%)
  blocking collectives  12.3 us (13%)
  local copies, waits for them, and re-layouts  1.69 us (2%)
    pallas_call x7, Pallas kernels, run(): pl.pallas_call(kernel, out_shape=out_shape, in_specs=[space(i) for i in r...  13.8 us
    all_to_all x1, blocking collectives, body(): totals = lax.all_to_all(sums, 'pz', 0, 0, tiled=True)  12.3 us
    all_to_all x1, starting transfers between devices, body(): received = lax.all_to_all(send, 'pz', 0, 0, tiled=True)  11.4 us
    ppermute x1, waiting for transfers between devices, body(): two = lax.ppermute(velocity, ('py', 'pz'), inward)  11.1 us
    ppermute x1, starting transfers between devices, body(): smooth_one = lax.ppermute(smooth, ('py', 'pz'), outward)  6.68 us
    ppermute x1, starting transfers between devices, body(): one = lax.ppermute(velocity, ('py', 'pz'), outward)  5.49 us
    all_to_all x1, waiting for transfers between devices, body(): received_strain = lax.all_to_all(send_strain, 'pz', 0, 0, tiled=True)  5.47 us
    all_to_all x1, starting transfers between devices, body(): received_strain = lax.all_to_all(send_strain, 'pz', 0, 0, tiled=True)  5.43 us
  transfers between devices with their start and end apart: 8, of which 6 were waited for; matrix products, arithmetic and copies ran while one was open for 0% of the time, Pallas kernels for 12%

profile of v8, /device:TPU:33, one launch (start us, length us, event | category | flops | bytes accessed | tf_op | source)
XLA Modules:
  0.0 93.5 jit_solution(7099018306604613471)
XLA Ops:
  0.6 1.0 %fusion = (f32[3,1,1024]{2,1,0:T(1,128)S(1)}, f32[3,1,1024]{2,1,0:T(1,128)S(1)}) fusion(f32[3,64,1024]{2,1,0:T(8,128)} %bitcast.9), kind=kLoop, calls=%fused_computation | loop fusion | bytes 49152 | tf_op jit(solution)/shard_map/slice | solution.py:292
  1.6 2.7 %collective-permute-start.1 = (f32[3,1,1024]{2,1,0:T(1,128)S(1)}, f32[3,1,1024]{2,1,0:T(1,128)S(1)}, u32[]{:S(2)}, u32[]{:S(2)}) collective-permute-start(f32[3,1,1024]{2,1,0:T(1,128)S(1)} %get-tuple-element.20), channel_id=1, source_target_pairs={{0,1},{1,2},{2,3},{3,4},{4,5},{5,6},{6,7},{7,8},{8,9},{9,10},{10,1... | collective-permute-start | bytes 36872 | tf_op jit(solution)/shard_map/ppermute | solution.py:292
  4.3 0.0 collective-permute-start
  4.3 4.0 %products.1 = bf16[16,296,128]{2,1,0:T(8,128)(2,1)} custom-call(bf16[144,1024]{1,0:T(8,128)(2,1)} %constant.23.clone.table_ref, f32[3,64,1024]{2,1,0:T(8,128)} %bitcast.10), custom_call_target="tpu_custom_call" | custom-call | flops 1207959552 | bytes 2883584 | tf_op jit(solution)/shard_map/products/pallas_call | solution.py:36
  8.3 0.0 copy-start.3
  8.3 0.0 copy-start.4
  8.3 0.0 collective-permute-done.1.first_ref
  8.3 0.0 collective-permute-done.last_ref
  8.3 11.4 %all-to-all-start = ((bf16[16,296,128]{2,1,0:T(8,128)(2,1)}), bf16[16,296,128]{2,1,0:T(8,128)(2,1)S(1)}, u32[]{:S(2)}, u32[]{:S(2)}) async-start(bf16[16,296,128]{2,1,0:T(8,128)(2,1)} %products.1), calls=%async_computation | async-start | bytes 2424832 | tf_op jit(solution)/shard_map/all_to_all | solution.py:305
  19.7 0.0 copy-done.3
  19.8 3.1 %collective-permute-start.3 = (f32[3,64,1024]{2,1,0:T(8,128)S(1)}, f32[3,64,1024]{2,1,0:T(8,128)S(1)}, u32[]{:S(2)}, u32[]{:S(2)}) collective-permute-start(f32[3,64,1024]{2,1,0:T(8,128)S(1)} %bitcast.11), channel_id=1, source_target_pairs={{16,0},{1,17},{18,2},{3,19},{20,4},{5,21},{22,6},{7,23},{24,8},{9,... | collective-permute-start | bytes 2359304 | tf_op jit(solution)/shard_map/ppermute | solution.py:308
  22.9 5.5 %collective-permute-start.2 = (f32[3,64,1024]{2,1,0:T(8,128)S(1)}, f32[3,64,1024]{2,1,0:T(8,128)}, u32[]{:S(2)}, u32[]{:S(2)}) collective-permute-start(f32[3,64,1024]{2,1,0:T(8,128)S(1)} %bitcast.12), channel_id=1, source_target_pairs={{0,16},{17,1},{2,18},{19,3},{4,20},{21,5},{6,22},{23,7},{8,24},{25... | collective-permute-start | bytes 2359304 | tf_op jit(solution)/shard_map/ppermute | solution.py:307
  28.4 11.1 %collective-permute-done.3.two_ref = f32[3,64,1024]{2,1,0:T(8,128)S(1)} collective-permute-done((f32[3,64,1024]{2,1,0:T(8,128)S(1)}, f32[3,64,1024]{2,1,0:T(8,128)S(1)}, u32[]{:S(2)}, u32[]{:S(2)}) %collective-permute-start.3) | collective-permute-done | bytes 786464 | tf_op jit(solution)/shard_map/ppermute | solution.py:308
  39.4 2.5 %collective-permute-done.2.one_ref = f32[3,64,1024]{2,1,0:T(8,128)} collective-permute-done((f32[3,64,1024]{2,1,0:T(8,128)S(1)}, f32[3,64,1024]{2,1,0:T(8,128)}, u32[]{:S(2)}, u32[]{:S(2)}) %collective-permute-start.2) | collective-permute-done | bytes 786464 | tf_op jit(solution)/shard_map/ppermute | solution.py:307
  41.9 0.0 copy-done.4
  41.9 3.8 %strain.1 = (bf16[16,192,128]{2,1,0:T(8,128)(2,1)}, f32[64,1024]{1,0:T(8,128)S(1)}) custom-call(bf16[8,1024]{1,0:T(8,128)(2,1)S(1)} %copy-done.4, f32[3,64,1024]{2,1,0:T(8,128)S(1)} %bitcast.13, f32[3,64,1024]{2,1,0:T(8,128)} %collective-permute-done.2.one_ref, f32[3,64,1024]{2,1,0:T(8,128)S(1)} %collective-permute-done.3.two_ref, f32[1,1]{1,0:T(1,128)} %bitcast.1.sense_ref, ...), custom_call_target="tpu_custom_call" | custom-call | flops 805306368 | bytes 4456448 | tf_op jit(solution)/shard_map/strain/pallas_call | solution.py:36
  45.7 0.0 copy-start.1
  45.8 0.7 copy-done.1
  46.4 4.5 %all-to-all-done.recv_ref = bf16[16,296,128]{2,1,0:T(8,128)(2,1)S(1)} async-done(((bf16[16,296,128]{2,1,0:T(8,128)(2,1)}), bf16[16,296,128]{2,1,0:T(8,128)(2,1)S(1)}, u32[]{:S(2)}, u32[]{:S(2)}) %all-to-all-start) | async-done | bytes 1212448 | tf_op jit(solution)/shard_map/all_to_all | solution.py:305
  51.0 5.4 %all-to-all-start.1 = ((bf16[16,192,128]{2,1,0:T(8,128)(2,1)}), bf16[16,192,128]{2,1,0:T(8,128)(2,1)S(1)}, u32[]{:S(2)}, u32[]{:S(2)}) async-start(bf16[16,192,128]{2,1,0:T(8,128)(2,1)} %get-tuple-element.14), calls=%async_computation.1 | async-start | bytes 1572864 | tf_op jit(solution)/shard_map/all_to_all | solution.py:319
  56.4 0.0 copy-start.5
  56.4 1.7 %smooth.1 = (bf16[3,64,1024]{2,1,0:T(8,128)(2,1)}, f32[16,1024]{1,0:T(8,128)S(1)}, bf16[8,1024]{1,0:T(8,128)(2,1)S(1)}) custom-call(bf16[8,1024]{1,0:T(8,128)(2,1)S(1)} %copy-done.4, bf16[16,296,128]{2,1,0:T(8,128)(2,1)S(1)} %all-to-all-done.recv_ref), custom_call_target="tpu_custom_call" | custom-call | flops 536870912 | bytes 2097152 | tf_op jit(solution)/shard_map/smooth/pallas_call | solution.py:36
  58.1 0.0 copy-start
  58.1 2.0 %collective-permute-start.5 = (bf16[3,64,1024]{2,1,0:T(8,128)(2,1)}, bf16[3,64,1024]{2,1,0:T(8,128)(2,1)S(1)}, u32[]{:S(2)}, u32[]{:S(2)}) collective-permute-start(bf16[3,64,1024]{2,1,0:T(8,128)(2,1)} %get-tuple-element.15.smooth_ref), channel_id=1, source_target_pairs={{16,0},{1,17},{18,2},{3,19},{20,4},{5,21},{22,6},{7,23},{24,8},{9,... | collective-permute-start | bytes 1179656 | tf_op jit(solution)/shard_map/ppermute | solution.py:334
  60.1 6.7 %collective-permute-start.4 = (bf16[3,64,1024]{2,1,0:T(8,128)(2,1)}, bf16[3,64,1024]{2,1,0:T(8,128)(2,1)S(1)}, u32[]{:S(2)}, u32[]{:S(2)}) collective-permute-start(bf16[3,64,1024]{2,1,0:T(8,128)(2,1)} %get-tuple-element.15.smooth_ref), channel_id=1, source_target_pairs={{0,16},{17,1},{2,18},{19,3},{4,20},{21,5},{6,22},{23,7},{8,24},{25... | collective-permute-start | bytes 1179656 | tf_op jit(solution)/shard_map/ppermute | solution.py:333
  66.8 0.0 copy-done.5
  66.8 1.1 %squares.1.squares_ref = bf16[6,64,1024]{2,1,0:T(8,128)(2,1)S(1)} custom-call(bf16[8,1024]{1,0:T(8,128)(2,1)S(1)} %copy-done.5, bf16[16,296,128]{2,1,0:T(8,128)(2,1)S(1)} %all-to-all-done.recv_ref), custom_call_target="tpu_custom_call" | custom-call | flops 805306368 | bytes 1572864 | tf_op jit(solution)/shard_map/squares/pallas_call | solution.py:36
  68.0 2.6 %collective-permute-done.5.two_ref = bf16[3,64,1024]{2,1,0:T(8,128)(2,1)S(1)} collective-permute-done((bf16[3,64,1024]{2,1,0:T(8,128)(2,1)}, bf16[3,64,1024]{2,1,0:T(8,128)(2,1)S(1)}, u32[]{:S(2)}, u32[]{:S(2)}) %collective-permute-start.5) | collective-permute-done | bytes 393248 | tf_op jit(solution)/shard_map/ppermute | solution.py:334
  70.6 2.0 %collective-permute-done.4.one_ref = bf16[3,64,1024]{2,1,0:T(8,128)(2,1)S(1)} collective-permute-done((bf16[3,64,1024]{2,1,0:T(8,128)(2,1)}, bf16[3,64,1024]{2,1,0:T(8,128)(2,1)S(1)}, u32[]{:S(2)}, u32[]{:S(2)}) %collective-permute-start.4) | collective-permute-done | bytes 393248 | tf_op jit(solution)/shard_map/ppermute | solution.py:333
  72.5 0.0 copy-done
  72.5 1.1 %model.1.model_ref = f32[6,64,1024]{2,1,0:T(8,128)S(1)} custom-call(bf16[3,64,1024]{2,1,0:T(8,128)(2,1)S(1)} %copy-done, bf16[3,64,1024]{2,1,0:T(8,128)(2,1)S(1)} %collective-permute-done.4.one_ref, bf16[3,64,1024]{2,1,0:T(8,128)(2,1)S(1)} %collective-permute-done.5.two_ref, f32[1,1]{1,0:T(1,128)} %bitcast.1.sense_ref, ...), custom_call_target="tpu_custom_call" | custom-call | flops 6553600 | bytes 1572864 | tf_op jit(solution)/shard_map/model/pallas_call | solution.py:36
  73.6 5.5 %all-to-all-done.1.recv_ref = bf16[16,192,128]{2,1,0:T(8,128)(2,1)S(1)} async-done(((bf16[16,192,128]{2,1,0:T(8,128)(2,1)}), bf16[16,192,128]{2,1,0:T(8,128)(2,1)S(1)}, u32[]{:S(2)}, u32[]{:S(2)}) %all-to-all-start.1) | async-done | bytes 786464 | tf_op jit(solution)/shard_map/all_to_all | solution.py:319
  79.1 0.0 copy-start.2
  79.1 1.3 %sums.1 = f32[16,1,128]{2,1,0:T(1,128)S(1)} custom-call(bf16[8,1024]{1,0:T(8,128)(2,1)S(1)} %get-tuple-element.11.table_ref, bf16[16,192,128]{2,1,0:T(8,128)(2,1)S(1)} %all-to-all-done.1.recv_ref, bf16[3,64,1024]{2,1,0:T(8,128)(2,1)S(1)} %copy-done, bf16[6,64,1024]{2,1,0:T(8,128)(2,1)S(1)} %squares.1.squares_ref, f32[6,64,1024]{2,1,0:T(8,128)S(1)} %model.1.model_ref), custom_call_target="tpu_custom_call" | custom-call | flops 805306368 | bytes 3145728 | tf_op jit(solution)/shard_map/sums/pallas_call | solution.py:36
  80.4 12.3 %all_to_all.15.refs_0_ = f32[16,1,128]{2,1,0:T(1,128)S(1)} all-to-all(f32[16,1,128]{2,1,0:T(1,128)S(1)} %sums.1), channel_id=1, replica_groups=mesh['py'=32,'pz'=16] {'pz'}, dimensions={0} | all-to-all | bytes 16384 | tf_op jit(solution)/shard_map/all_to_all | solution.py:359
  92.7 0.0 copy-done.2
  92.7 0.8 viscosity.1
Async XLA Ops:
  1.6 6.7 %collective-permute-start.1 = (f32[3,1,1024]{2,1,0:T(1,128)S(1)}, f32[3,1,1024]{2,1,0:T(1,128)S(1)}, u32[]{:S(2)}, u32[]{:S(2)}) collective-permute-start(f32[3,1,1024]{2,1,0:T(1,128)S(1)} %get-tuple-element.20), channel_id=1, source_target_pairs={{0,1},{1,2},{2,3},{3,4},{4,5},{5,6},{6,7},{7,8},{8,9},{9,10},{10,1... | collective-permute-start | bytes 36872 | tf_op jit(solution)/shard_map/ppermute | solution.py:292
  4.3 4.1 %collective-permute-start = (f32[3,1,1024]{2,1,0:T(1,128)S(1)}, f32[3,1,1024]{2,1,0:T(1,128)S(1)}, u32[]{:S(2)}, u32[]{:S(2)}) collective-permute-start(f32[3,1,1024]{2,1,0:T(1,128)S(1)} %get-tuple-element.21), channel_id=1, source_target_pairs={{1,0},{2,1},{3,2},{4,3},{5,4},{6,5},{7,6},{8,7},{9,8},{10,9},{11,1... | collective-permute-start | bytes 36872 | tf_op jit(solution)/shard_map/ppermute | solution.py:291
  8.3 11.5 %copy-start.3 = (f32[3,1,64,1024]{3,2,1,0:T(8,128)S(1)}, f32[3,1,64,1024]{3,2,1,0:T(8,128)}, u32[]{:S(2)}) copy-start(f32[3,1,64,1024]{3,2,1,0:T(8,128)} %param.3) | copy-start | bytes 2359300
  8.3 33.6 %copy-start.4 = (bf16[8,1024]{1,0:T(8,128)(2,1)S(1)}, bf16[8,1024]{1,0:T(8,128)(2,1)}, u32[]{:S(2)}) copy-start(bf16[8,1024]{1,0:T(8,128)(2,1)} %constant.24.clone.table_ref) | copy-start | bytes 49156
  8.3 42.6 %all-to-all-start = ((bf16[16,296,128]{2,1,0:T(8,128)(2,1)}), bf16[16,296,128]{2,1,0:T(8,128)(2,1)S(1)}, u32[]{:S(2)}, u32[]{:S(2)}) async-start(bf16[16,296,128]{2,1,0:T(8,128)(2,1)} %products.1), calls=%async_computation | async-start | bytes 2424832 | tf_op jit(solution)/shard_map/all_to_all | solution.py:305
  19.8 19.7 %collective-permute-start.3 = (f32[3,64,1024]{2,1,0:T(8,128)S(1)}, f32[3,64,1024]{2,1,0:T(8,128)S(1)}, u32[]{:S(2)}, u32[]{:S(2)}) collective-permute-start(f32[3,64,1024]{2,1,0:T(8,128)S(1)} %bitcast.11), channel_id=1, source_target_pairs={{16,0},{1,17},{18,2},{3,19},{20,4},{5,21},{22,6},{7,23},{24,8},{9,... | collective-permute-start | bytes 2359304 | tf_op jit(solution)/shard_map/ppermute | solution.py:308
  22.9 19.1 %collective-permute-start.2 = (f32[3,64,1024]{2,1,0:T(8,128)S(1)}, f32[3,64,1024]{2,1,0:T(8,128)}, u32[]{:S(2)}, u32[]{:S(2)}) collective-permute-start(f32[3,64,1024]{2,1,0:T(8,128)S(1)} %bitcast.12), channel_id=1, source_target_pairs={{0,16},{17,1},{2,18},{19,3},{4,20},{21,5},{6,22},{23,7},{8,24},{25... | collective-permute-start | bytes 2359304 | tf_op jit(solution)/shard_map/ppermute | solution.py:307
  45.7 0.7 copy-start.1
  51.0 28.1 %all-to-all-start.1 = ((bf16[16,192,128]{2,1,0:T(8,128)(2,1)}), bf16[16,192,128]{2,1,0:T(8,128)(2,1)S(1)}, u32[]{:S(2)}, u32[]{:S(2)}) async-start(bf16[16,192,128]{2,1,0:T(8,128)(2,1)} %get-tuple-element.14), calls=%async_computation.1 | async-start | bytes 1572864 | tf_op jit(solution)/shard_map/all_to_all | solution.py:319
  56.4 10.4 %copy-start.5 = (bf16[8,1024]{1,0:T(8,128)(2,1)S(1)}, bf16[8,1024]{1,0:T(8,128)(2,1)}, u32[]{:S(2)}) copy-start(bf16[8,1024]{1,0:T(8,128)(2,1)} %constant.24.clone.table_ref) | copy-start | bytes 49156
  58.1 14.4 %copy-start = (bf16[3,64,1024]{2,1,0:T(8,128)(2,1)S(1)}, bf16[3,64,1024]{2,1,0:T(8,128)(2,1)}, u32[]{:S(2)}) copy-start(bf16[3,64,1024]{2,1,0:T(8,128)(2,1)} %get-tuple-element.15.smooth_ref) | copy-start | bytes 1179652
  58.1 12.5 %collective-permute-start.5 = (bf16[3,64,1024]{2,1,0:T(8,128)(2,1)}, bf16[3,64,1024]{2,1,0:T(8,128)(2,1)S(1)}, u32[]{:S(2)}, u32[]{:S(2)}) collective-permute-start(bf16[3,64,1024]{2,1,0:T(8,128)(2,1)} %get-tuple-element.15.smooth_ref), channel_id=1, source_target_pairs={{16,0},{1,17},{18,2},{3,19},{20,4},{5,21},{22,6},{7,23},{24,8},{9,... | collective-permute-start | bytes 1179656 | tf_op jit(solution)/shard_map/ppermute | solution.py:334
  60.1 12.4 %collective-permute-start.4 = (bf16[3,64,1024]{2,1,0:T(8,128)(2,1)}, bf16[3,64,1024]{2,1,0:T(8,128)(2,1)S(1)}, u32[]{:S(2)}, u32[]{:S(2)}) collective-permute-start(bf16[3,64,1024]{2,1,0:T(8,128)(2,1)} %get-tuple-element.15.smooth_ref), channel_id=1, source_target_pairs={{0,16},{17,1},{2,18},{19,3},{4,20},{21,5},{6,22},{23,7},{8,24},{25... | collective-permute-start | bytes 1179656 | tf_op jit(solution)/shard_map/ppermute | solution.py:333
  79.1 13.6 %copy-start.2 = (f32[64,1024]{1,0:T(8,128)S(1)}, f32[64,1024]{1,0:T(8,128)}, u32[]{:S(2)}) copy-start(f32[64,1024]{1,0:T(8,128)} %copy-done.1) | copy-start | bytes 786436

commit v9 on v8

--- a/solution.py
+++ b/solution.py
@@ -315,6 +315,7 @@
         [vmem((6 * depth, nx), bf16), vmem(strain_shape, bf16), dma((2,))],
         "strain",
         (7,),
+        54,
     )(short_x, velocity, one, two, sense, first, last)
     received_strain = lax.all_to_all(send_strain, "pz", 0, 0, tiled=True)
 

time: 94 us -> 95 us (1.011)
  Pallas kernels: 13.8 us -> 15 us
    pallas_call x7, Pallas kernels: 13.8 us -> 15 us  [run(): pl.pallas_call(kernel, out_shape=out_shape, in_specs=[space(i) for i in r...]
  transfers between devices with their start and end apart: 8 -> 8, of which waited for: 6 -> 6; matrix products, arithmetic and copies ran while one was open for 0% -> 0% of each run, Pallas kernels for 12% -> 14%
where the time goes in v9:
time: 95 us; the launch traced here: 94.4 us
  starting transfers between devices  37.2 us (39%)
  waiting for transfers between devices  27.6 us (29%)
  Pallas kernels  15 us (16%)
  blocking collectives  12.3 us (13%)
  local copies, waits for them, and re-layouts  1.58 us (2%)
    pallas_call x7, Pallas kernels, run(): pl.pallas_call(kernel, out_shape=out_shape, in_specs=[space(i) for i in r...  15 us
    all_to_all x1, blocking collectives, body(): totals = lax.all_to_all(sums, 'pz', 0, 0, tiled=True)  12.3 us
    all_to_all x1, starting transfers between devices, body(): received = lax.all_to_all(send, 'pz', 0, 0, tiled=True)  11.3 us
    ppermute x1, waiting for transfers between devices, body(): two = lax.ppermute(velocity, ('py', 'pz'), inward)  11.1 us
    ppermute x1, starting transfers between devices, body(): smooth_one = lax.ppermute(smooth, ('py', 'pz'), outward)  6.68 us
    all_to_all x1, starting transfers between devices, body(): received_strain = lax.all_to_all(send_strain, 'pz', 0, 0, tiled=True)  5.93 us
    ppermute x1, starting transfers between devices, body(): one = lax.ppermute(velocity, ('py', 'pz'), outward)  5.49 us
    all_to_all x1, waiting for transfers between devices, body(): received_strain = lax.all_to_all(send_strain, 'pz', 0, 0, tiled=True)  5.48 us
  transfers between devices with their start and end apart: 8, of which 6 were waited for; matrix products, arithmetic and copies ran while one was open for 0% of the time, Pallas kernels for 14%

profile of v9, /device:TPU:33, one launch (start us, length us, event | category | flops | bytes accessed | tf_op | source)
XLA Modules:
  0.0 94.4 jit_solution(5231632115459208336)
XLA Ops:
  0.6 1.0 %fusion = (f32[3,1,1024]{2,1,0:T(1,128)S(1)}, f32[3,1,1024]{2,1,0:T(1,128)S(1)}) fusion(f32[3,64,1024]{2,1,0:T(8,128)} %bitcast.10), kind=kLoop, calls=%fused_computation | loop fusion | bytes 49152 | tf_op jit(solution)/shard_map/slice | solution.py:292
  1.6 2.7 %collective-permute-start.1 = (f32[3,1,1024]{2,1,0:T(1,128)S(1)}, f32[3,1,1024]{2,1,0:T(1,128)S(1)}, u32[]{:S(2)}, u32[]{:S(2)}) collective-permute-start(f32[3,1,1024]{2,1,0:T(1,128)S(1)} %get-tuple-element.20), channel_id=1, source_target_pairs={{0,1},{1,2},{2,3},{3,4},{4,5},{5,6},{6,7},{7,8},{8,9},{9,10},{10,1... | collective-permute-start | bytes 36872 | tf_op jit(solution)/shard_map/ppermute | solution.py:292
  4.3 0.0 collective-permute-start
  4.3 4.0 %products.1 = bf16[16,296,128]{2,1,0:T(8,128)(2,1)} custom-call(bf16[144,1024]{1,0:T(8,128)(2,1)} %constant.23.clone.table_ref, f32[3,64,1024]{2,1,0:T(8,128)} %bitcast.11), custom_call_target="tpu_custom_call" | custom-call | flops 1207959552 | bytes 2883584 | tf_op jit(solution)/shard_map/products/pallas_call | solution.py:36
  8.3 0.0 copy-start.3
  8.3 0.0 collective-permute-done.1.first_ref
  8.3 0.0 copy-start.5
  8.3 0.0 collective-permute-done.last_ref
  8.3 0.0 copy-start.6
  8.3 0.6 copy-done.5
  8.9 0.0 copy-done.6
  8.9 11.3 %all-to-all-start = ((bf16[16,296,128]{2,1,0:T(8,128)(2,1)}), bf16[16,296,128]{2,1,0:T(8,128)(2,1)S(1)}, u32[]{:S(2)}, u32[]{:S(2)}) async-start(bf16[16,296,128]{2,1,0:T(8,128)(2,1)} %products.1), calls=%async_computation | async-start | bytes 2424832 | tf_op jit(solution)/shard_map/all_to_all | solution.py:305
  20.2 0.0 copy-done.3
  20.2 3.1 %collective-permute-start.3 = (f32[3,64,1024]{2,1,0:T(8,128)S(1)}, f32[3,64,1024]{2,1,0:T(8,128)S(1)}, u32[]{:S(2)}, u32[]{:S(2)}) collective-permute-start(f32[3,64,1024]{2,1,0:T(8,128)S(1)} %bitcast.13), channel_id=1, source_target_pairs={{16,0},{1,17},{18,2},{3,19},{20,4},{5,21},{22,6},{7,23},{24,8},{9,... | collective-permute-start | bytes 2359304 | tf_op jit(solution)/shard_map/ppermute | solution.py:308
  23.3 5.5 %collective-permute-start.2 = (f32[3,64,1024]{2,1,0:T(8,128)S(1)}, f32[3,64,1024]{2,1,0:T(8,128)}, u32[]{:S(2)}, u32[]{:S(2)}) collective-permute-start(f32[3,64,1024]{2,1,0:T(8,128)S(1)} %bitcast.14), channel_id=1, source_target_pairs={{0,16},{17,1},{2,18},{19,3},{4,20},{21,5},{6,22},{23,7},{8,24},{25... | collective-permute-start | bytes 2359304 | tf_op jit(solution)/shard_map/ppermute | solution.py:307
  28.8 11.1 %collective-permute-done.3.two_ref = f32[3,64,1024]{2,1,0:T(8,128)S(1)} collective-permute-done((f32[3,64,1024]{2,1,0:T(8,128)S(1)}, f32[3,64,1024]{2,1,0:T(8,128)S(1)}, u32[]{:S(2)}, u32[]{:S(2)}) %collective-permute-start.3) | collective-permute-done | bytes 786464 | tf_op jit(solution)/shard_map/ppermute | solution.py:308
  39.9 0.0 copy-start.4
  39.9 2.5 %collective-permute-done.2.one_ref = f32[3,64,1024]{2,1,0:T(8,128)} collective-permute-done((f32[3,64,1024]{2,1,0:T(8,128)S(1)}, f32[3,64,1024]{2,1,0:T(8,128)}, u32[]{:S(2)}, u32[]{:S(2)}) %collective-permute-start.2) | collective-permute-done | bytes 786464 | tf_op jit(solution)/shard_map/ppermute | solution.py:307
  42.4 0.0 copy-done.4
  42.4 5.0 %strain.1 = (bf16[16,192,128]{2,1,0:T(8,128)(2,1)}, f32[64,1024]{1,0:T(8,128)}) custom-call(bf16[8,1024]{1,0:T(8,128)(2,1)} %constant.24.clone.table_ref, f32[3,64,1024]{2,1,0:T(8,128)} %bitcast.12, f32[3,64,1024]{2,1,0:T(8,128)} %collective-permute-done.2.one_ref, f32[3,64,1024]{2,1,0:T(8,128)} %copy-done.4, f32[1,1]{1,0:T(1,128)} %bitcast.1.sense_ref, ...), custom_call_target="tpu_custom_call" | custom-call | flops 805306368 | bytes 4456448 | tf_op jit(solution)/shard_map/strain/pallas_call | solution.py:36
  47.4 0.0 copy-start.2
  47.4 4.1 %all-to-all-done.recv_ref = bf16[16,296,128]{2,1,0:T(8,128)(2,1)S(1)} async-done(((bf16[16,296,128]{2,1,0:T(8,128)(2,1)}), bf16[16,296,128]{2,1,0:T(8,128)(2,1)S(1)}, u32[]{:S(2)}, u32[]{:S(2)}) %all-to-all-start) | async-done | bytes 1212448 | tf_op jit(solution)/shard_map/all_to_all | solution.py:305
  51.4 5.9 %all-to-all-start.1 = ((bf16[16,192,128]{2,1,0:T(8,128)(2,1)}), bf16[16,192,128]{2,1,0:T(8,128)(2,1)S(1)}, u32[]{:S(2)}, u32[]{:S(2)}) async-start(bf16[16,192,128]{2,1,0:T(8,128)(2,1)} %get-tuple-element.14), calls=%async_computation.1 | async-start | bytes 1572864 | tf_op jit(solution)/shard_map/all_to_all | solution.py:320
  57.3 0.0 copy-done.2
  57.3 1.7 %smooth.1 = (bf16[3,64,1024]{2,1,0:T(8,128)(2,1)}, f32[16,1024]{1,0:T(8,128)S(1)}, bf16[8,1024]{1,0:T(8,128)(2,1)S(1)}) custom-call(bf16[8,1024]{1,0:T(8,128)(2,1)S(1)} %copy-done.2, bf16[16,296,128]{2,1,0:T(8,128)(2,1)S(1)} %all-to-all-done.recv_ref), custom_call_target="tpu_custom_call" | custom-call | flops 536870912 | bytes 2097152 | tf_op jit(solution)/shard_map/smooth/pallas_call | solution.py:36
  59.0 0.0 copy-start
  59.0 2.0 %collective-permute-start.5 = (bf16[3,64,1024]{2,1,0:T(8,128)(2,1)}, bf16[3,64,1024]{2,1,0:T(8,128)(2,1)S(1)}, u32[]{:S(2)}, u32[]{:S(2)}) collective-permute-start(bf16[3,64,1024]{2,1,0:T(8,128)(2,1)} %get-tuple-element.15.smooth_ref), channel_id=1, source_target_pairs={{16,0},{1,17},{18,2},{3,19},{20,4},{5,21},{22,6},{7,23},{24,8},{9,... | collective-permute-start | bytes 1179656 | tf_op jit(solution)/shard_map/ppermute | solution.py:335
  61.1 6.7 %collective-permute-start.4 = (bf16[3,64,1024]{2,1,0:T(8,128)(2,1)}, bf16[3,64,1024]{2,1,0:T(8,128)(2,1)S(1)}, u32[]{:S(2)}, u32[]{:S(2)}) collective-permute-start(bf16[3,64,1024]{2,1,0:T(8,128)(2,1)} %get-tuple-element.15.smooth_ref), channel_id=1, source_target_pairs={{0,16},{17,1},{2,18},{19,3},{4,20},{21,5},{6,22},{23,7},{8,24},{25... | collective-permute-start | bytes 1179656 | tf_op jit(solution)/shard_map/ppermute | solution.py:334
  67.8 1.1 %squares.1.squares_ref = bf16[6,64,1024]{2,1,0:T(8,128)(2,1)S(1)} custom-call(bf16[8,1024]{1,0:T(8,128)(2,1)S(1)} %copy-done.2, bf16[16,296,128]{2,1,0:T(8,128)(2,1)S(1)} %all-to-all-done.recv_ref), custom_call_target="tpu_custom_call" | custom-call | flops 805306368 | bytes 1572864 | tf_op jit(solution)/shard_map/squares/pallas_call | solution.py:36
  68.9 2.6 %collective-permute-done.5.two_ref = bf16[3,64,1024]{2,1,0:T(8,128)(2,1)S(1)} collective-permute-done((bf16[3,64,1024]{2,1,0:T(8,128)(2,1)}, bf16[3,64,1024]{2,1,0:T(8,128)(2,1)S(1)}, u32[]{:S(2)}, u32[]{:S(2)}) %collective-permute-start.5) | collective-permute-done | bytes 393248 | tf_op jit(solution)/shard_map/ppermute | solution.py:335
  71.5 2.0 %collective-permute-done.4.one_ref = bf16[3,64,1024]{2,1,0:T(8,128)(2,1)S(1)} collective-permute-done((bf16[3,64,1024]{2,1,0:T(8,128)(2,1)}, bf16[3,64,1024]{2,1,0:T(8,128)(2,1)S(1)}, u32[]{:S(2)}, u32[]{:S(2)}) %collective-permute-start.4) | collective-permute-done | bytes 393248 | tf_op jit(solution)/shard_map/ppermute | solution.py:334
  73.5 0.0 copy-done
  73.5 1.1 %model.1.model_ref = f32[6,64,1024]{2,1,0:T(8,128)S(1)} custom-call(bf16[3,64,1024]{2,1,0:T(8,128)(2,1)S(1)} %copy-done, bf16[3,64,1024]{2,1,0:T(8,128)(2,1)S(1)} %collective-permute-done.4.one_ref, bf16[3,64,1024]{2,1,0:T(8,128)(2,1)S(1)} %collective-permute-done.5.two_ref, f32[1,1]{1,0:T(1,128)} %bitcast.1.sense_ref, ...), custom_call_target="tpu_custom_call" | custom-call | flops 6553600 | bytes 1572864 | tf_op jit(solution)/shard_map/model/pallas_call | solution.py:36
  74.5 5.5 %all-to-all-done.1.recv_ref = bf16[16,192,128]{2,1,0:T(8,128)(2,1)S(1)} async-done(((bf16[16,192,128]{2,1,0:T(8,128)(2,1)}), bf16[16,192,128]{2,1,0:T(8,128)(2,1)S(1)}, u32[]{:S(2)}, u32[]{:S(2)}) %all-to-all-start.1) | async-done | bytes 786464 | tf_op jit(solution)/shard_map/all_to_all | solution.py:320
  80.0 0.0 copy-start.1
  80.0 1.3 %sums.1 = f32[16,1,128]{2,1,0:T(1,128)S(1)} custom-call(bf16[8,1024]{1,0:T(8,128)(2,1)S(1)} %get-tuple-element.11.table_ref, bf16[16,192,128]{2,1,0:T(8,128)(2,1)S(1)} %all-to-all-done.1.recv_ref, bf16[3,64,1024]{2,1,0:T(8,128)(2,1)S(1)} %copy-done, bf16[6,64,1024]{2,1,0:T(8,128)(2,1)S(1)} %squares.1.squares_ref, f32[6,64,1024]{2,1,0:T(8,128)S(1)} %model.1.model_ref), custom_call_target="tpu_custom_call" | custom-call | flops 805306368 | bytes 3145728 | tf_op jit(solution)/shard_map/sums/pallas_call | solution.py:36
  81.3 12.3 %all_to_all.15.refs_0_ = f32[16,1,128]{2,1,0:T(1,128)S(1)} all-to-all(f32[16,1,128]{2,1,0:T(1,128)S(1)} %sums.1), channel_id=1, replica_groups=mesh['py'=32,'pz'=16] {'pz'}, dimensions={0} | all-to-all | bytes 16384 | tf_op jit(solution)/shard_map/all_to_all | solution.py:360
  93.6 0.0 copy-done.1
  93.6 0.8 viscosity.1
Async XLA Ops:
  1.6 6.7 %collective-permute-start.1 = (f32[3,1,1024]{2,1,0:T(1,128)S(1)}, f32[3,1,1024]{2,1,0:T(1,128)S(1)}, u32[]{:S(2)}, u32[]{:S(2)}) collective-permute-start(f32[3,1,1024]{2,1,0:T(1,128)S(1)} %get-tuple-element.20), channel_id=1, source_target_pairs={{0,1},{1,2},{2,3},{3,4},{4,5},{5,6},{6,7},{7,8},{8,9},{9,10},{10,1... | collective-permute-start | bytes 36872 | tf_op jit(solution)/shard_map/ppermute | solution.py:292
  4.3 4.1 %collective-permute-start = (f32[3,1,1024]{2,1,0:T(1,128)S(1)}, f32[3,1,1024]{2,1,0:T(1,128)S(1)}, u32[]{:S(2)}, u32[]{:S(2)}) collective-permute-start(f32[3,1,1024]{2,1,0:T(1,128)S(1)} %get-tuple-element.21), channel_id=1, source_target_pairs={{1,0},{2,1},{3,2},{4,3},{5,4},{6,5},{7,6},{8,7},{9,8},{10,9},{11,1... | collective-permute-start | bytes 36872 | tf_op jit(solution)/shard_map/ppermute | solution.py:291
  8.3 11.9 %copy-start.3 = (f32[3,1,64,1024]{3,2,1,0:T(8,128)S(1)}, f32[3,1,64,1024]{3,2,1,0:T(8,128)}, u32[]{:S(2)}) copy-start(f32[3,1,64,1024]{3,2,1,0:T(8,128)} %param.3) | copy-start | bytes 2359300
  8.3 0.6 copy-start.5
  8.3 0.6 copy-start.6
  8.9 42.5 %all-to-all-start = ((bf16[16,296,128]{2,1,0:T(8,128)(2,1)}), bf16[16,296,128]{2,1,0:T(8,128)(2,1)S(1)}, u32[]{:S(2)}, u32[]{:S(2)}) async-start(bf16[16,296,128]{2,1,0:T(8,128)(2,1)} %products.1), calls=%async_computation | async-start | bytes 2424832 | tf_op jit(solution)/shard_map/all_to_all | solution.py:305
  20.2 19.7 %collective-permute-start.3 = (f32[3,64,1024]{2,1,0:T(8,128)S(1)}, f32[3,64,1024]{2,1,0:T(8,128)S(1)}, u32[]{:S(2)}, u32[]{:S(2)}) collective-permute-start(f32[3,64,1024]{2,1,0:T(8,128)S(1)} %bitcast.13), channel_id=1, source_target_pairs={{16,0},{1,17},{18,2},{3,19},{20,4},{5,21},{22,6},{7,23},{24,8},{9,... | collective-permute-start | bytes 2359304 | tf_op jit(solution)/shard_map/ppermute | solution.py:308
  23.3 19.1 %collective-permute-start.2 = (f32[3,64,1024]{2,1,0:T(8,128)S(1)}, f32[3,64,1024]{2,1,0:T(8,128)}, u32[]{:S(2)}, u32[]{:S(2)}) collective-permute-start(f32[3,64,1024]{2,1,0:T(8,128)S(1)} %bitcast.14), channel_id=1, source_target_pairs={{0,16},{17,1},{2,18},{19,3},{4,20},{21,5},{6,22},{23,7},{8,24},{25... | collective-permute-start | bytes 2359304 | tf_op jit(solution)/shard_map/ppermute | solution.py:307
  39.9 2.5 %copy-start.4 = (f32[3,64,1024]{2,1,0:T(8,128)}, f32[3,64,1024]{2,1,0:T(8,128)S(1)}, u32[]{:S(2)}) copy-start(f32[3,64,1024]{2,1,0:T(8,128)S(1)} %collective-permute-done.3.two_ref) | copy-start | bytes 2359300
  47.4 10.0 %copy-start.2 = (bf16[8,1024]{1,0:T(8,128)(2,1)S(1)}, bf16[8,1024]{1,0:T(8,128)(2,1)}, u32[]{:S(2)}) copy-start(bf16[8,1024]{1,0:T(8,128)(2,1)} %constant.24.clone.table_ref) | copy-start | bytes 49156
  51.4 28.6 %all-to-all-start.1 = ((bf16[16,192,128]{2,1,0:T(8,128)(2,1)}), bf16[16,192,128]{2,1,0:T(8,128)(2,1)S(1)}, u32[]{:S(2)}, u32[]{:S(2)}) async-start(bf16[16,192,128]{2,1,0:T(8,128)(2,1)} %get-tuple-element.14), calls=%async_computation.1 | async-start | bytes 1572864 | tf_op jit(solution)/shard_map/all_to_all | solution.py:320
  59.0 14.4 %copy-start = (bf16[3,64,1024]{2,1,0:T(8,128)(2,1)S(1)}, bf16[3,64,1024]{2,1,0:T(8,128)(2,1)}, u32[]{:S(2)}) copy-start(bf16[3,64,1024]{2,1,0:T(8,128)(2,1)} %get-tuple-element.15.smooth_ref) | copy-start | bytes 1179652
  59.0 12.5 %collective-permute-start.5 = (bf16[3,64,1024]{2,1,0:T(8,128)(2,1)}, bf16[3,64,1024]{2,1,0:T(8,128)(2,1)S(1)}, u32[]{:S(2)}, u32[]{:S(2)}) collective-permute-start(bf16[3,64,1024]{2,1,0:T(8,128)(2,1)} %get-tuple-element.15.smooth_ref), channel_id=1, source_target_pairs={{16,0},{1,17},{18,2},{3,19},{20,4},{5,21},{22,6},{7,23},{24,8},{9,... | collective-permute-start | bytes 1179656 | tf_op jit(solution)/shard_map/ppermute | solution.py:335
  61.1 12.4 %collective-permute-start.4 = (bf16[3,64,1024]{2,1,0:T(8,128)(2,1)}, bf16[3,64,1024]{2,1,0:T(8,128)(2,1)S(1)}, u32[]{:S(2)}, u32[]{:S(2)}) collective-permute-start(bf16[3,64,1024]{2,1,0:T(8,128)(2,1)} %get-tuple-element.15.smooth_ref), channel_id=1, source_target_pairs={{0,16},{17,1},{2,18},{19,3},{4,20},{21,5},{6,22},{23,7},{8,24},{25... | collective-permute-start | bytes 1179656 | tf_op jit(solution)/shard_map/ppermute | solution.py:334
  80.0 13.6 %copy-start.1 = (f32[64,1024]{1,0:T(8,128)S(1)}, f32[64,1024]{1,0:T(8,128)}, u32[]{:S(2)}) copy-start(f32[64,1024]{1,0:T(8,128)} %get-tuple-element.17.refs_1_) | copy-start | bytes 786436

commit v10 on v7

--- a/solution.py
+++ b/solution.py
@@ -81,7 +81,7 @@
         row = lax.broadcasted_iota(jnp.int32, (receivers * 8, LANES), 0) % 8
         got = jnp.where(row < 2, got[:, :LANES], got[:, LANES:]).reshape(receivers, 8, LANES)
         block_ref[:, count * width // per :, :] = got.astype(jnp.bfloat16)
-    chunks = 2
+    chunks = sem.shape[0]
     some = receivers // chunks
     copies = []
     for c in range(chunks):
@@ -178,11 +178,11 @@
         place(lines_ref, 2 * width, t, one)
         one, two = sorted_lines(recv_ref, t, 9 * width // 2, 8)
         place(lines_ref, 3 * width, t, jnp.concatenate([one, two], axis=0))
-    got = nt(lines_ref[...], table_of(table_ref[...])).astype(jnp.bfloat16)
+    got = nt(lines_ref[...], table_rows(table_ref, 0, length // LANES)).astype(jnp.bfloat16)
     for a in range(3):
         smooth_ref[a] = got[a * width : (a + 1) * width, :]
     edges_ref[...] = got[3 * width :, :].astype(jnp.float32)
-    band_ref[...] = table_ref[...]
+    band_ref[...] = table_ref[:BAND, :]
 
 
 def squares_kernel(table_ref, recv_ref, squares_ref, lines_ref):
@@ -198,7 +198,7 @@
         one, two = sorted_lines(recv_ref, t, 4 * width, half)
         place(lines_ref, 5 * width, t, one)
         place(lines_ref, 5 * width + half, t, two)
-    got = nt(lines_ref[...], table_of(table_ref[...])).astype(jnp.bfloat16)
+    got = nt(lines_ref[...], table_rows(table_ref, 0, length // LANES)).astype(jnp.bfloat16)
     for p in range(6):
         squares_ref[p] = got[p * width : (p + 1) * width, :]
 
@@ -269,7 +269,8 @@
     for r in range(2):
         beside[r, :4] = table_x[[r * width - 1, (r + 1) * width] * 2]
     lanes_x = jnp.asarray(np.concatenate([table_x[:LANES], beside.reshape(16, nx)]))
-    lanes_z = jnp.asarray(table_z[:BAND])
+    same = np.array_equal(table_x[:LANES], table_z[:LANES])
+    lanes_z = lanes_x if same else jnp.asarray(table_z[:LANES])
     outward, inward = [], []
     for i in range(rows - 1):
         for j in range(parts):
@@ -290,7 +291,7 @@
         jax.ShapeDtypeStruct(send_shape, bf16),
         2 * 9 * depth * nx * nx,
         12 * depth * nx + 2 * nx * nx,
-        [vmem((9 * depth, nx), bf16), vmem(send_shape, bf16), dma((2,))],
+        [vmem((9 * depth, nx), bf16), vmem(send_shape, bf16), dma((4,))],
         "products",
         (2,),
         58,

time: 93.7 us -> 93.4 us (level)
  transfers between devices with their start and end apart: 8 -> 8, of which waited for: 7 -> 7; matrix products, arithmetic and copies ran while one was open for 0% -> 0% of each run, Pallas kernels for 13% -> 12%
where the time goes in v10:
time: 93.4 us; the launch traced here: 92.9 us
  starting transfers between devices  33.3 us (36%)
  waiting for transfers between devices  31.3 us (34%)
  Pallas kernels  13.7 us (15%)
  blocking collectives  12.2 us (13%)
  local copies, waits for them, and re-layouts  1.68 us (2%)
    pallas_call x7, Pallas kernels, run(): pl.pallas_call(kernel, out_shape=out_shape, in_specs=[space(i) for i in r...  13.7 us
    all_to_all x1, blocking collectives, body(): totals = lax.all_to_all(sums, 'pz', 0, 0, tiled=True)  12.2 us
    ppermute x1, waiting for transfers between devices, body(): two = lax.ppermute(velocity, ('py', 'pz'), inward)  11.1 us
    all_to_all x1, starting transfers between devices, body(): received = lax.all_to_all(send, 'pz', 0, 0, tiled=True)  7.79 us
    ppermute x1, starting transfers between devices, body(): smooth_one = lax.ppermute(smooth, ('py', 'pz'), outward)  6.68 us
    all_to_all x1, waiting for transfers between devices, body(): received_strain = lax.all_to_all(send_strain, 'pz', 0, 0, tiled=True)  5.56 us
    ppermute x1, starting transfers between devices, body(): one = lax.ppermute(velocity, ('py', 'pz'), outward)  5.48 us
    all_to_all x1, starting transfers between devices, body(): received_strain = lax.all_to_all(send_strain, 'pz', 0, 0, tiled=True)  5.45 us
  transfers between devices with their start and end apart: 8, of which 7 were waited for; matrix products, arithmetic and copies ran while one was open for 0% of the time, Pallas kernels for 12%

profile of v10, /device:TPU:33, one launch (start us, length us, event | category | flops | bytes accessed | tf_op | source)
XLA Modules:
  0.0 92.9 jit_solution(15741608741514082268)
XLA Ops:
  0.6 1.0 %fusion = (f32[3,1,1024]{2,1,0:T(1,128)S(1)}, f32[3,1,1024]{2,1,0:T(1,128)S(1)}) fusion(f32[3,64,1024]{2,1,0:T(8,128)} %bitcast.9), kind=kLoop, calls=%fused_computation | loop fusion | bytes 49152 | tf_op jit(solution)/shard_map/slice | solution.py:287
  1.6 0.7 collective-permute-start.1
  2.3 2.0 %collective-permute-start = (f32[3,1,1024]{2,1,0:T(1,128)S(1)}, f32[3,1,1024]{2,1,0:T(1,128)S(1)}, u32[]{:S(2)}, u32[]{:S(2)}) collective-permute-start(f32[3,1,1024]{2,1,0:T(1,128)S(1)} %get-tuple-element.21), channel_id=1, source_target_pairs={{0,1},{1,2},{2,3},{3,4},{4,5},{5,6},{6,7},{7,8},{8,9},{9,10},{10,1... | collective-permute-start | bytes 36872 | tf_op jit(solution)/shard_map/ppermute | solution.py:286
  4.3 4.0 %products.1 = bf16[16,296,128]{2,1,0:T(8,128)(2,1)} custom-call(bf16[144,1024]{1,0:T(8,128)(2,1)} %constant.21.clone.table_ref, f32[3,64,1024]{2,1,0:T(8,128)} %bitcast.10), custom_call_target="tpu_custom_call" | custom-call | flops 1207959552 | bytes 2883584 | tf_op jit(solution)/shard_map/products/pallas_call | solution.py:36
  8.3 0.0 copy-start.3
  8.3 0.0 copy-start.4
  8.3 0.0 collective-permute-done.1.last_ref
  8.3 3.1 %collective-permute-done.first_ref = f32[3,1,1024]{2,1,0:T(1,128)S(1)} collective-permute-done((f32[3,1,1024]{2,1,0:T(1,128)S(1)}, f32[3,1,1024]{2,1,0:T(1,128)S(1)}, u32[]{:S(2)}, u32[]{:S(2)}) %collective-permute-start) | collective-permute-done | bytes 12320 | tf_op jit(solution)/shard_map/ppermute | solution.py:286
  11.4 7.8 %all-to-all-start = ((bf16[16,296,128]{2,1,0:T(8,128)(2,1)}), bf16[16,296,128]{2,1,0:T(8,128)(2,1)S(1)}, u32[]{:S(2)}, u32[]{:S(2)}) async-start(bf16[16,296,128]{2,1,0:T(8,128)(2,1)} %products.1), calls=%async_computation | async-start | bytes 2424832 | tf_op jit(solution)/shard_map/all_to_all | solution.py:300
  19.2 0.0 copy-done.3
  19.2 3.1 %collective-permute-start.3 = (f32[3,64,1024]{2,1,0:T(8,128)S(1)}, f32[3,64,1024]{2,1,0:T(8,128)S(1)}, u32[]{:S(2)}, u32[]{:S(2)}) collective-permute-start(f32[3,64,1024]{2,1,0:T(8,128)S(1)} %bitcast.11), channel_id=1, source_target_pairs={{16,0},{1,17},{18,2},{3,19},{20,4},{5,21},{22,6},{7,23},{24,8},{9,... | collective-permute-start | bytes 2359304 | tf_op jit(solution)/shard_map/ppermute | solution.py:303
  22.4 5.5 %collective-permute-start.2 = (f32[3,64,1024]{2,1,0:T(8,128)S(1)}, f32[3,64,1024]{2,1,0:T(8,128)}, u32[]{:S(2)}, u32[]{:S(2)}) collective-permute-start(f32[3,64,1024]{2,1,0:T(8,128)S(1)} %bitcast.12), channel_id=1, source_target_pairs={{0,16},{17,1},{2,18},{19,3},{4,20},{21,5},{6,22},{23,7},{8,24},{25... | collective-permute-start | bytes 2359304 | tf_op jit(solution)/shard_map/ppermute | solution.py:302
  27.9 11.1 %collective-permute-done.3.two_ref = f32[3,64,1024]{2,1,0:T(8,128)S(1)} collective-permute-done((f32[3,64,1024]{2,1,0:T(8,128)S(1)}, f32[3,64,1024]{2,1,0:T(8,128)S(1)}, u32[]{:S(2)}, u32[]{:S(2)}) %collective-permute-start.3) | collective-permute-done | bytes 786464 | tf_op jit(solution)/shard_map/ppermute | solution.py:303
  38.9 2.5 %collective-permute-done.2.one_ref = f32[3,64,1024]{2,1,0:T(8,128)} collective-permute-done((f32[3,64,1024]{2,1,0:T(8,128)S(1)}, f32[3,64,1024]{2,1,0:T(8,128)}, u32[]{:S(2)}, u32[]{:S(2)}) %collective-permute-start.2) | collective-permute-done | bytes 786464 | tf_op jit(solution)/shard_map/ppermute | solution.py:302
  41.4 0.0 copy-done.4
  41.4 3.8 %strain.1 = (bf16[16,192,128]{2,1,0:T(8,128)(2,1)}, f32[64,1024]{1,0:T(8,128)S(1)}) custom-call(bf16[144,1024]{1,0:T(8,128)(2,1)S(1)} %copy-done.4, f32[3,64,1024]{2,1,0:T(8,128)S(1)} %bitcast.13, f32[3,64,1024]{2,1,0:T(8,128)} %collective-permute-done.2.one_ref, f32[3,64,1024]{2,1,0:T(8,128)S(1)} %collective-permute-done.3.two_ref, ...), custom_call_target="tpu_custom_call" | custom-call | flops 805306368 | bytes 4456448 | tf_op jit(solution)/shard_map/strain/pallas_call | solution.py:36
  45.2 0.0 copy-start.1
  45.2 0.7 copy-done.1
  45.9 4.5 %all-to-all-done.recv_ref = bf16[16,296,128]{2,1,0:T(8,128)(2,1)S(1)} async-done(((bf16[16,296,128]{2,1,0:T(8,128)(2,1)}), bf16[16,296,128]{2,1,0:T(8,128)(2,1)S(1)}, u32[]{:S(2)}, u32[]{:S(2)}) %all-to-all-start) | async-done | bytes 1212448 | tf_op jit(solution)/shard_map/all_to_all | solution.py:300
  50.4 5.4 %all-to-all-start.1 = ((bf16[16,192,128]{2,1,0:T(8,128)(2,1)}), bf16[16,192,128]{2,1,0:T(8,128)(2,1)S(1)}, u32[]{:S(2)}, u32[]{:S(2)}) async-start(bf16[16,192,128]{2,1,0:T(8,128)(2,1)} %get-tuple-element.14), calls=%async_computation.1 | async-start | bytes 1572864 | tf_op jit(solution)/shard_map/all_to_all | solution.py:314
  55.9 0.0 copy-start.5
  55.9 1.6 %smooth.1 = (bf16[3,64,1024]{2,1,0:T(8,128)(2,1)}, f32[16,1024]{1,0:T(8,128)S(1)}, bf16[8,1024]{1,0:T(8,128)(2,1)S(1)}) custom-call(bf16[144,1024]{1,0:T(8,128)(2,1)S(1)} %copy-done.4, bf16[16,296,128]{2,1,0:T(8,128)(2,1)S(1)} %all-to-all-done.recv_ref), custom_call_target="tpu_custom_call" | custom-call | flops 536870912 | bytes 2097152 | tf_op jit(solution)/shard_map/smooth/pallas_call | solution.py:36
  57.5 0.0 copy-start
  57.5 2.0 %collective-permute-start.5 = (bf16[3,64,1024]{2,1,0:T(8,128)(2,1)}, bf16[3,64,1024]{2,1,0:T(8,128)(2,1)S(1)}, u32[]{:S(2)}, u32[]{:S(2)}) collective-permute-start(bf16[3,64,1024]{2,1,0:T(8,128)(2,1)} %get-tuple-element.15.smooth_ref), channel_id=1, source_target_pairs={{16,0},{1,17},{18,2},{3,19},{20,4},{5,21},{22,6},{7,23},{24,8},{9,... | collective-permute-start | bytes 1179656 | tf_op jit(solution)/shard_map/ppermute | solution.py:329
  59.6 6.7 %collective-permute-start.4 = (bf16[3,64,1024]{2,1,0:T(8,128)(2,1)}, bf16[3,64,1024]{2,1,0:T(8,128)(2,1)S(1)}, u32[]{:S(2)}, u32[]{:S(2)}) collective-permute-start(bf16[3,64,1024]{2,1,0:T(8,128)(2,1)} %get-tuple-element.15.smooth_ref), channel_id=1, source_target_pairs={{0,16},{17,1},{2,18},{19,3},{4,20},{21,5},{6,22},{23,7},{8,24},{25... | collective-permute-start | bytes 1179656 | tf_op jit(solution)/shard_map/ppermute | solution.py:328
  66.2 0.0 copy-done.5
  66.3 1.1 %squares.1.squares_ref = bf16[6,64,1024]{2,1,0:T(8,128)(2,1)S(1)} custom-call(bf16[144,1024]{1,0:T(8,128)(2,1)S(1)} %copy-done.5, bf16[16,296,128]{2,1,0:T(8,128)(2,1)S(1)} %all-to-all-done.recv_ref), custom_call_target="tpu_custom_call" | custom-call | flops 805306368 | bytes 1572864 | tf_op jit(solution)/shard_map/squares/pallas_call | solution.py:36
  67.3 2.6 %collective-permute-done.5.two_ref = bf16[3,64,1024]{2,1,0:T(8,128)(2,1)S(1)} collective-permute-done((bf16[3,64,1024]{2,1,0:T(8,128)(2,1)}, bf16[3,64,1024]{2,1,0:T(8,128)(2,1)S(1)}, u32[]{:S(2)}, u32[]{:S(2)}) %collective-permute-start.5) | collective-permute-done | bytes 393248 | tf_op jit(solution)/shard_map/ppermute | solution.py:329
  70.0 2.0 %collective-permute-done.4.one_ref = bf16[3,64,1024]{2,1,0:T(8,128)(2,1)S(1)} collective-permute-done((bf16[3,64,1024]{2,1,0:T(8,128)(2,1)}, bf16[3,64,1024]{2,1,0:T(8,128)(2,1)S(1)}, u32[]{:S(2)}, u32[]{:S(2)}) %collective-permute-start.4) | collective-permute-done | bytes 393248 | tf_op jit(solution)/shard_map/ppermute | solution.py:328
  71.9 0.0 copy-done
  71.9 1.1 %model.1.model_ref = f32[6,64,1024]{2,1,0:T(8,128)S(1)} custom-call(bf16[3,64,1024]{2,1,0:T(8,128)(2,1)S(1)} %copy-done, bf16[3,64,1024]{2,1,0:T(8,128)(2,1)S(1)} %collective-permute-done.4.one_ref, bf16[3,64,1024]{2,1,0:T(8,128)(2,1)S(1)} %collective-permute-done.5.two_ref, f32[1,1]{1,0:T(1,128)} %bitcast.1.sense_ref, ...), custom_call_target="tpu_custom_call" | custom-call | flops 6553600 | bytes 1572864 | tf_op jit(solution)/shard_map/model/pallas_call | solution.py:36
  73.0 5.6 %all-to-all-done.1.recv_ref = bf16[16,192,128]{2,1,0:T(8,128)(2,1)S(1)} async-done(((bf16[16,192,128]{2,1,0:T(8,128)(2,1)}), bf16[16,192,128]{2,1,0:T(8,128)(2,1)S(1)}, u32[]{:S(2)}, u32[]{:S(2)}) %all-to-all-start.1) | async-done | bytes 786464 | tf_op jit(solution)/shard_map/all_to_all | solution.py:314
  78.6 0.0 copy-start.2
  78.6 1.3 %sums.1 = f32[16,1,128]{2,1,0:T(1,128)S(1)} custom-call(bf16[8,1024]{1,0:T(8,128)(2,1)S(1)} %get-tuple-element.11.table_ref, bf16[16,192,128]{2,1,0:T(8,128)(2,1)S(1)} %all-to-all-done.1.recv_ref, bf16[3,64,1024]{2,1,0:T(8,128)(2,1)S(1)} %copy-done, bf16[6,64,1024]{2,1,0:T(8,128)(2,1)S(1)} %squares.1.squares_ref, f32[6,64,1024]{2,1,0:T(8,128)S(1)} %model.1.model_ref), custom_call_target="tpu_custom_call" | custom-call | flops 805306368 | bytes 3145728 | tf_op jit(solution)/shard_map/sums/pallas_call | solution.py:36
  79.9 12.2 %all_to_all.15.refs_0_ = f32[16,1,128]{2,1,0:T(1,128)S(1)} all-to-all(f32[16,1,128]{2,1,0:T(1,128)S(1)} %sums.1), channel_id=1, replica_groups=mesh['py'=32,'pz'=16] {'pz'}, dimensions={0} | all-to-all | bytes 16384 | tf_op jit(solution)/shard_map/all_to_all | solution.py:354
  92.1 0.0 copy-done.2
  92.1 0.8 viscosity.1
Async XLA Ops:
  1.6 6.7 %collective-permute-start.1 = (f32[3,1,1024]{2,1,0:T(1,128)S(1)}, f32[3,1,1024]{2,1,0:T(1,128)S(1)}, u32[]{:S(2)}, u32[]{:S(2)}) collective-permute-start(f32[3,1,1024]{2,1,0:T(1,128)S(1)} %get-tuple-element.20), channel_id=1, source_target_pairs={{1,0},{2,1},{3,2},{4,3},{5,4},{6,5},{7,6},{8,7},{9,8},{10,9},{11,1... | collective-permute-start | bytes 36872 | tf_op jit(solution)/shard_map/ppermute | solution.py:287
  2.3 9.2 %collective-permute-start = (f32[3,1,1024]{2,1,0:T(1,128)S(1)}, f32[3,1,1024]{2,1,0:T(1,128)S(1)}, u32[]{:S(2)}, u32[]{:S(2)}) collective-permute-start(f32[3,1,1024]{2,1,0:T(1,128)S(1)} %get-tuple-element.21), channel_id=1, source_target_pairs={{0,1},{1,2},{2,3},{3,4},{4,5},{5,6},{6,7},{7,8},{8,9},{9,10},{10,1... | collective-permute-start | bytes 36872 | tf_op jit(solution)/shard_map/ppermute | solution.py:286
  8.3 10.9 %copy-start.3 = (f32[3,1,64,1024]{3,2,1,0:T(8,128)S(1)}, f32[3,1,64,1024]{3,2,1,0:T(8,128)}, u32[]{:S(2)}) copy-start(f32[3,1,64,1024]{3,2,1,0:T(8,128)} %param.2) | copy-start | bytes 2359300
  8.3 33.1 %copy-start.4 = (bf16[144,1024]{1,0:T(8,128)(2,1)S(1)}, bf16[144,1024]{1,0:T(8,128)(2,1)}, u32[]{:S(2)}) copy-start(bf16[144,1024]{1,0:T(8,128)(2,1)} %constant.21.clone.table_ref) | copy-start | bytes 884740
  11.4 39.0 %all-to-all-start = ((bf16[16,296,128]{2,1,0:T(8,128)(2,1)}), bf16[16,296,128]{2,1,0:T(8,128)(2,1)S(1)}, u32[]{:S(2)}, u32[]{:S(2)}) async-start(bf16[16,296,128]{2,1,0:T(8,128)(2,1)} %products.1), calls=%async_computation | async-start | bytes 2424832 | tf_op jit(solution)/shard_map/all_to_all | solution.py:300
  19.2 19.7 %collective-permute-start.3 = (f32[3,64,1024]{2,1,0:T(8,128)S(1)}, f32[3,64,1024]{2,1,0:T(8,128)S(1)}, u32[]{:S(2)}, u32[]{:S(2)}) collective-permute-start(f32[3,64,1024]{2,1,0:T(8,128)S(1)} %bitcast.11), channel_id=1, source_target_pairs={{16,0},{1,17},{18,2},{3,19},{20,4},{5,21},{22,6},{7,23},{24,8},{9,... | collective-permute-start | bytes 2359304 | tf_op jit(solution)/shard_map/ppermute | solution.py:303
  22.4 19.1 %collective-permute-start.2 = (f32[3,64,1024]{2,1,0:T(8,128)S(1)}, f32[3,64,1024]{2,1,0:T(8,128)}, u32[]{:S(2)}, u32[]{:S(2)}) collective-permute-start(f32[3,64,1024]{2,1,0:T(8,128)S(1)} %bitcast.12), channel_id=1, source_target_pairs={{0,16},{17,1},{2,18},{19,3},{4,20},{21,5},{6,22},{23,7},{8,24},{25... | collective-permute-start | bytes 2359304 | tf_op jit(solution)/shard_map/ppermute | solution.py:302
  45.2 0.7 copy-start.1
  50.4 28.1 %all-to-all-start.1 = ((bf16[16,192,128]{2,1,0:T(8,128)(2,1)}), bf16[16,192,128]{2,1,0:T(8,128)(2,1)S(1)}, u32[]{:S(2)}, u32[]{:S(2)}) async-start(bf16[16,192,128]{2,1,0:T(8,128)(2,1)} %get-tuple-element.14), calls=%async_computation.1 | async-start | bytes 1572864 | tf_op jit(solution)/shard_map/all_to_all | solution.py:314
  55.9 10.3 %copy-start.5 = (bf16[144,1024]{1,0:T(8,128)(2,1)S(1)}, bf16[144,1024]{1,0:T(8,128)(2,1)}, u32[]{:S(2)}) copy-start(bf16[144,1024]{1,0:T(8,128)(2,1)} %constant.21.clone.table_ref) | copy-start | bytes 884740
  57.5 14.4 %copy-start = (bf16[3,64,1024]{2,1,0:T(8,128)(2,1)S(1)}, bf16[3,64,1024]{2,1,0:T(8,128)(2,1)}, u32[]{:S(2)}) copy-start(bf16[3,64,1024]{2,1,0:T(8,128)(2,1)} %get-tuple-element.15.smooth_ref) | copy-start | bytes 1179652
  57.5 12.5 %collective-permute-start.5 = (bf16[3,64,1024]{2,1,0:T(8,128)(2,1)}, bf16[3,64,1024]{2,1,0:T(8,128)(2,1)S(1)}, u32[]{:S(2)}, u32[]{:S(2)}) collective-permute-start(bf16[3,64,1024]{2,1,0:T(8,128)(2,1)} %get-tuple-element.15.smooth_ref), channel_id=1, source_target_pairs={{16,0},{1,17},{18,2},{3,19},{20,4},{5,21},{22,6},{7,23},{24,8},{9,... | collective-permute-start | bytes 1179656 | tf_op jit(solution)/shard_map/ppermute | solution.py:329
  59.6 12.4 %collective-permute-start.4 = (bf16[3,64,1024]{2,1,0:T(8,128)(2,1)}, bf16[3,64,1024]{2,1,0:T(8,128)(2,1)S(1)}, u32[]{:S(2)}, u32[]{:S(2)}) collective-permute-start(bf16[3,64,1024]{2,1,0:T(8,128)(2,1)} %get-tuple-element.15.smooth_ref), channel_id=1, source_target_pairs={{0,16},{17,1},{2,18},{19,3},{4,20},{21,5},{6,22},{23,7},{8,24},{25... | collective-permute-start | bytes 1179656 | tf_op jit(solution)/shard_map/ppermute | solution.py:328
  78.6 13.5 %copy-start.2 = (f32[64,1024]{1,0:T(8,128)S(1)}, f32[64,1024]{1,0:T(8,128)}, u32[]{:S(2)}) copy-start(f32[64,1024]{1,0:T(8,128)} %copy-done.1) | copy-start | bytes 786436

commit v11 on v10

--- a/solution.py
+++ b/solution.py
@@ -68,7 +68,7 @@
     return jnp.concatenate([turned(tile, a) for a in range(band.shape[1] // LANES)], axis=0)
 
 
-def send_blocks(table_ref, fields_ref, block_ref, out_ref, sem, count, depth, edges):
+def send_blocks(table_ref, fields_ref, block_ref, out_ref, sem, count, depth, edges, shares):
     receivers = block_ref.shape[0]
     width = fields_ref.shape[1] // receivers
     per = LANES // depth
@@ -81,13 +81,12 @@
         row = lax.broadcasted_iota(jnp.int32, (receivers * 8, LANES), 0) % 8
         got = jnp.where(row < 2, got[:, :LANES], got[:, LANES:]).reshape(receivers, 8, LANES)
         block_ref[:, count * width // per :, :] = got.astype(jnp.bfloat16)
-    chunks = sem.shape[0]
-    some = receivers // chunks
-    copies = []
-    for c in range(chunks):
-        mine = slice(c * some, (c + 1) * some)
-        blocks = some * width // LANES
-        table = table_rows(table_ref, c * blocks, (c + 1) * blocks)
+    copies, done = [], 0
+    for c, some in enumerate(shares):
+        mine = slice(done, done + some)
+        first_block, last_block = done * width // LANES, (done + some) * width // LANES
+        done += some
+        table = table_rows(table_ref, first_block, last_block)
         for first in range(0, full, 2):
             here = min(2, full - first)
             got = nt(table, fields_ref[first * LANES : (first + here) * LANES, :])
@@ -131,7 +130,7 @@
     for p, (a, b) in enumerate(index_pairs):
         at = (3 + p) * depth
         fields_ref[at : at + depth, :] = (parts[a] * parts[b]).astype(jnp.bfloat16)
-    send_blocks(table_ref, fields_ref, block_ref, out_ref, sem, 9, depth, True)
+    send_blocks(table_ref, fields_ref, block_ref, out_ref, sem, 9, depth, True, (8, 4, 4))
 
 
 def strain(gradients):
@@ -164,7 +163,7 @@
     magnitude_ref[...] = magnitude
     for p, part_value in enumerate(strain_parts):
         fields_ref[p * depth : (p + 1) * depth, :] = (magnitude * part_value).astype(jnp.bfloat16)
-    send_blocks(table_ref, fields_ref, block_ref, out_ref, sem, 6, depth, False)
+    send_blocks(table_ref, fields_ref, block_ref, out_ref, sem, 6, depth, False, (8, 8))
 
 
 def smooth_kernel(table_ref, recv_ref, smooth_ref, edges_ref, band_ref, lines_ref):
@@ -291,7 +290,7 @@
         jax.ShapeDtypeStruct(send_shape, bf16),
         2 * 9 * depth * nx * nx,
         12 * depth * nx + 2 * nx * nx,
-        [vmem((9 * depth, nx), bf16), vmem(send_shape, bf16), dma((4,))],
+        [vmem((9 * depth, nx), bf16), vmem(send_shape, bf16), dma((3,))],
         "products",
         (2,),
         58,

time: 93.4 us -> 93.4 us (level)
  no operation moved by 1% of the time
where the time goes in v11:
time: 93.4 us; the launch traced here: 92.9 us
  starting transfers between devices  33.2 us (36%)
  waiting for transfers between devices  31.4 us (34%)
  Pallas kernels  13.7 us (15%)
  blocking collectives  12.2 us (13%)
  local copies, waits for them, and re-layouts  1.68 us (2%)
    pallas_call x7, Pallas kernels, run(): pl.pallas_call(kernel, out_shape=out_shape, in_specs=[space(i) for i in r...  13.7 us
    all_to_all x1, blocking collectives, body(): totals = lax.all_to_all(sums, 'pz', 0, 0, tiled=True)  12.2 us
    ppermute x1, waiting for transfers between devices, body(): two = lax.ppermute(velocity, ('py', 'pz'), inward)  11.1 us
    all_to_all x1, starting transfers between devices, body(): received = lax.all_to_all(send, 'pz', 0, 0, tiled=True)  7.77 us
    ppermute x1, starting transfers between devices, body(): smooth_one = lax.ppermute(smooth, ('py', 'pz'), outward)  6.68 us
    all_to_all x1, waiting for transfers between devices, body(): received_strain = lax.all_to_all(send_strain, 'pz', 0, 0, tiled=True)  5.55 us
    ppermute x1, starting transfers between devices, body(): one = lax.ppermute(velocity, ('py', 'pz'), outward)  5.48 us
    all_to_all x1, starting transfers between devices, body(): received_strain = lax.all_to_all(send_strain, 'pz', 0, 0, tiled=True)  5.44 us
  transfers between devices with their start and end apart: 8, of which 7 were waited for; matrix products, arithmetic and copies ran while one was open for 0% of the time, Pallas kernels for 12%

profile of v11, /device:TPU:33, one launch (start us, length us, event | category | flops | bytes accessed | tf_op | source)
XLA Modules:
  0.0 92.9 jit_solution(6445319658534032175)
XLA Ops:
  0.6 1.0 %fusion = (f32[3,1,1024]{2,1,0:T(1,128)S(1)}, f32[3,1,1024]{2,1,0:T(1,128)S(1)}) fusion(f32[3,64,1024]{2,1,0:T(8,128)} %bitcast.9), kind=kLoop, calls=%fused_computation | loop fusion | bytes 49152 | tf_op jit(solution)/shard_map/slice | solution.py:286
  1.6 0.7 collective-permute-start.1
  2.3 2.0 %collective-permute-start = (f32[3,1,1024]{2,1,0:T(1,128)S(1)}, f32[3,1,1024]{2,1,0:T(1,128)S(1)}, u32[]{:S(2)}, u32[]{:S(2)}) collective-permute-start(f32[3,1,1024]{2,1,0:T(1,128)S(1)} %get-tuple-element.21), channel_id=1, source_target_pairs={{0,1},{1,2},{2,3},{3,4},{4,5},{5,6},{6,7},{7,8},{8,9},{9,10},{10,1... | collective-permute-start | bytes 36872 | tf_op jit(solution)/shard_map/ppermute | solution.py:285
  4.3 4.0 %products.1 = bf16[16,296,128]{2,1,0:T(8,128)(2,1)} custom-call(bf16[144,1024]{1,0:T(8,128)(2,1)} %constant.21.clone.table_ref, f32[3,64,1024]{2,1,0:T(8,128)} %bitcast.10), custom_call_target="tpu_custom_call" | custom-call | flops 1207959552 | bytes 2883584 | tf_op jit(solution)/shard_map/products/pallas_call | solution.py:36
  8.3 0.0 copy-start.3
  8.3 0.0 copy-start.4
  8.3 0.0 collective-permute-done.1.last_ref
  8.3 3.1 %collective-permute-done.first_ref = f32[3,1,1024]{2,1,0:T(1,128)S(1)} collective-permute-done((f32[3,1,1024]{2,1,0:T(1,128)S(1)}, f32[3,1,1024]{2,1,0:T(1,128)S(1)}, u32[]{:S(2)}, u32[]{:S(2)}) %collective-permute-start) | collective-permute-done | bytes 12320 | tf_op jit(solution)/shard_map/ppermute | solution.py:285
  11.4 7.8 %all-to-all-start = ((bf16[16,296,128]{2,1,0:T(8,128)(2,1)}), bf16[16,296,128]{2,1,0:T(8,128)(2,1)S(1)}, u32[]{:S(2)}, u32[]{:S(2)}) async-start(bf16[16,296,128]{2,1,0:T(8,128)(2,1)} %products.1), calls=%async_computation | async-start | bytes 2424832 | tf_op jit(solution)/shard_map/all_to_all | solution.py:299
  19.2 0.0 copy-done.3
  19.2 3.1 %collective-permute-start.3 = (f32[3,64,1024]{2,1,0:T(8,128)S(1)}, f32[3,64,1024]{2,1,0:T(8,128)S(1)}, u32[]{:S(2)}, u32[]{:S(2)}) collective-permute-start(f32[3,64,1024]{2,1,0:T(8,128)S(1)} %bitcast.11), channel_id=1, source_target_pairs={{16,0},{1,17},{18,2},{3,19},{20,4},{5,21},{22,6},{7,23},{24,8},{9,... | collective-permute-start | bytes 2359304 | tf_op jit(solution)/shard_map/ppermute | solution.py:302
  22.3 5.5 %collective-permute-start.2 = (f32[3,64,1024]{2,1,0:T(8,128)S(1)}, f32[3,64,1024]{2,1,0:T(8,128)}, u32[]{:S(2)}, u32[]{:S(2)}) collective-permute-start(f32[3,64,1024]{2,1,0:T(8,128)S(1)} %bitcast.12), channel_id=1, source_target_pairs={{0,16},{17,1},{2,18},{19,3},{4,20},{21,5},{6,22},{23,7},{8,24},{25... | collective-permute-start | bytes 2359304 | tf_op jit(solution)/shard_map/ppermute | solution.py:301
  27.8 11.1 %collective-permute-done.3.two_ref = f32[3,64,1024]{2,1,0:T(8,128)S(1)} collective-permute-done((f32[3,64,1024]{2,1,0:T(8,128)S(1)}, f32[3,64,1024]{2,1,0:T(8,128)S(1)}, u32[]{:S(2)}, u32[]{:S(2)}) %collective-permute-start.3) | collective-permute-done | bytes 786464 | tf_op jit(solution)/shard_map/ppermute | solution.py:302
  38.9 2.5 %collective-permute-done.2.one_ref = f32[3,64,1024]{2,1,0:T(8,128)} collective-permute-done((f32[3,64,1024]{2,1,0:T(8,128)S(1)}, f32[3,64,1024]{2,1,0:T(8,128)}, u32[]{:S(2)}, u32[]{:S(2)}) %collective-permute-start.2) | collective-permute-done | bytes 786464 | tf_op jit(solution)/shard_map/ppermute | solution.py:301
  41.4 0.0 copy-done.4
  41.4 3.8 %strain.1 = (bf16[16,192,128]{2,1,0:T(8,128)(2,1)}, f32[64,1024]{1,0:T(8,128)S(1)}) custom-call(bf16[144,1024]{1,0:T(8,128)(2,1)S(1)} %copy-done.4, f32[3,64,1024]{2,1,0:T(8,128)S(1)} %bitcast.13, f32[3,64,1024]{2,1,0:T(8,128)} %collective-permute-done.2.one_ref, f32[3,64,1024]{2,1,0:T(8,128)S(1)} %collective-permute-done.3.two_ref, ...), custom_call_target="tpu_custom_call" | custom-call | flops 805306368 | bytes 4456448 | tf_op jit(solution)/shard_map/strain/pallas_call | solution.py:36
  45.2 0.0 copy-start.1
  45.2 0.7 copy-done.1
  45.9 4.5 %all-to-all-done.recv_ref = bf16[16,296,128]{2,1,0:T(8,128)(2,1)S(1)} async-done(((bf16[16,296,128]{2,1,0:T(8,128)(2,1)}), bf16[16,296,128]{2,1,0:T(8,128)(2,1)S(1)}, u32[]{:S(2)}, u32[]{:S(2)}) %all-to-all-start) | async-done | bytes 1212448 | tf_op jit(solution)/shard_map/all_to_all | solution.py:299
  50.4 5.4 %all-to-all-start.1 = ((bf16[16,192,128]{2,1,0:T(8,128)(2,1)}), bf16[16,192,128]{2,1,0:T(8,128)(2,1)S(1)}, u32[]{:S(2)}, u32[]{:S(2)}) async-start(bf16[16,192,128]{2,1,0:T(8,128)(2,1)} %get-tuple-element.14), calls=%async_computation.1 | async-start | bytes 1572864 | tf_op jit(solution)/shard_map/all_to_all | solution.py:313
  55.9 0.0 copy-start.5
  55.9 1.6 %smooth.1 = (bf16[3,64,1024]{2,1,0:T(8,128)(2,1)}, f32[16,1024]{1,0:T(8,128)S(1)}, bf16[8,1024]{1,0:T(8,128)(2,1)S(1)}) custom-call(bf16[144,1024]{1,0:T(8,128)(2,1)S(1)} %copy-done.4, bf16[16,296,128]{2,1,0:T(8,128)(2,1)S(1)} %all-to-all-done.recv_ref), custom_call_target="tpu_custom_call" | custom-call | flops 536870912 | bytes 2097152 | tf_op jit(solution)/shard_map/smooth/pallas_call | solution.py:36
  57.5 0.0 copy-start
  57.5 2.0 %collective-permute-start.5 = (bf16[3,64,1024]{2,1,0:T(8,128)(2,1)}, bf16[3,64,1024]{2,1,0:T(8,128)(2,1)S(1)}, u32[]{:S(2)}, u32[]{:S(2)}) collective-permute-start(bf16[3,64,1024]{2,1,0:T(8,128)(2,1)} %get-tuple-element.15.smooth_ref), channel_id=1, source_target_pairs={{16,0},{1,17},{18,2},{3,19},{20,4},{5,21},{22,6},{7,23},{24,8},{9,... | collective-permute-start | bytes 1179656 | tf_op jit(solution)/shard_map/ppermute | solution.py:328
  59.5 6.7 %collective-permute-start.4 = (bf16[3,64,1024]{2,1,0:T(8,128)(2,1)}, bf16[3,64,1024]{2,1,0:T(8,128)(2,1)S(1)}, u32[]{:S(2)}, u32[]{:S(2)}) collective-permute-start(bf16[3,64,1024]{2,1,0:T(8,128)(2,1)} %get-tuple-element.15.smooth_ref), channel_id=1, source_target_pairs={{0,16},{17,1},{2,18},{19,3},{4,20},{21,5},{6,22},{23,7},{8,24},{25... | collective-permute-start | bytes 1179656 | tf_op jit(solution)/shard_map/ppermute | solution.py:327
  66.2 0.0 copy-done.5
  66.2 1.0 %squares.1.squares_ref = bf16[6,64,1024]{2,1,0:T(8,128)(2,1)S(1)} custom-call(bf16[144,1024]{1,0:T(8,128)(2,1)S(1)} %copy-done.5, bf16[16,296,128]{2,1,0:T(8,128)(2,1)S(1)} %all-to-all-done.recv_ref), custom_call_target="tpu_custom_call" | custom-call | flops 805306368 | bytes 1572864 | tf_op jit(solution)/shard_map/squares/pallas_call | solution.py:36
  67.3 2.7 %collective-permute-done.5.two_ref = bf16[3,64,1024]{2,1,0:T(8,128)(2,1)S(1)} collective-permute-done((bf16[3,64,1024]{2,1,0:T(8,128)(2,1)}, bf16[3,64,1024]{2,1,0:T(8,128)(2,1)S(1)}, u32[]{:S(2)}, u32[]{:S(2)}) %collective-permute-start.5) | collective-permute-done | bytes 393248 | tf_op jit(solution)/shard_map/ppermute | solution.py:328
  69.9 2.0 %collective-permute-done.4.one_ref = bf16[3,64,1024]{2,1,0:T(8,128)(2,1)S(1)} collective-permute-done((bf16[3,64,1024]{2,1,0:T(8,128)(2,1)}, bf16[3,64,1024]{2,1,0:T(8,128)(2,1)S(1)}, u32[]{:S(2)}, u32[]{:S(2)}) %collective-permute-start.4) | collective-permute-done | bytes 393248 | tf_op jit(solution)/shard_map/ppermute | solution.py:327
  71.9 0.0 copy-done
  71.9 1.1 %model.1.model_ref = f32[6,64,1024]{2,1,0:T(8,128)S(1)} custom-call(bf16[3,64,1024]{2,1,0:T(8,128)(2,1)S(1)} %copy-done, bf16[3,64,1024]{2,1,0:T(8,128)(2,1)S(1)} %collective-permute-done.4.one_ref, bf16[3,64,1024]{2,1,0:T(8,128)(2,1)S(1)} %collective-permute-done.5.two_ref, f32[1,1]{1,0:T(1,128)} %bitcast.1.sense_ref, ...), custom_call_target="tpu_custom_call" | custom-call | flops 6553600 | bytes 1572864 | tf_op jit(solution)/shard_map/model/pallas_call | solution.py:36
  73.0 5.6 %all-to-all-done.1.recv_ref = bf16[16,192,128]{2,1,0:T(8,128)(2,1)S(1)} async-done(((bf16[16,192,128]{2,1,0:T(8,128)(2,1)}), bf16[16,192,128]{2,1,0:T(8,128)(2,1)S(1)}, u32[]{:S(2)}, u32[]{:S(2)}) %all-to-all-start.1) | async-done | bytes 786464 | tf_op jit(solution)/shard_map/all_to_all | solution.py:313
  78.5 0.0 copy-start.2
  78.5 1.3 %sums.1 = f32[16,1,128]{2,1,0:T(1,128)S(1)} custom-call(bf16[8,1024]{1,0:T(8,128)(2,1)S(1)} %get-tuple-element.11.table_ref, bf16[16,192,128]{2,1,0:T(8,128)(2,1)S(1)} %all-to-all-done.1.recv_ref, bf16[3,64,1024]{2,1,0:T(8,128)(2,1)S(1)} %copy-done, bf16[6,64,1024]{2,1,0:T(8,128)(2,1)S(1)} %squares.1.squares_ref, f32[6,64,1024]{2,1,0:T(8,128)S(1)} %model.1.model_ref), custom_call_target="tpu_custom_call" | custom-call | flops 805306368 | bytes 3145728 | tf_op jit(solution)/shard_map/sums/pallas_call | solution.py:36
  79.9 12.2 %all_to_all.15.refs_0_ = f32[16,1,128]{2,1,0:T(1,128)S(1)} all-to-all(f32[16,1,128]{2,1,0:T(1,128)S(1)} %sums.1), channel_id=1, replica_groups=mesh['py'=32,'pz'=16] {'pz'}, dimensions={0} | all-to-all | bytes 16384 | tf_op jit(solution)/shard_map/all_to_all | solution.py:353
  92.1 0.0 copy-done.2
  92.1 0.8 viscosity.1
Async XLA Ops:
  1.6 6.7 %collective-permute-start.1 = (f32[3,1,1024]{2,1,0:T(1,128)S(1)}, f32[3,1,1024]{2,1,0:T(1,128)S(1)}, u32[]{:S(2)}, u32[]{:S(2)}) collective-permute-start(f32[3,1,1024]{2,1,0:T(1,128)S(1)} %get-tuple-element.20), channel_id=1, source_target_pairs={{1,0},{2,1},{3,2},{4,3},{5,4},{6,5},{7,6},{8,7},{9,8},{10,9},{11,1... | collective-permute-start | bytes 36872 | tf_op jit(solution)/shard_map/ppermute | solution.py:286
  2.3 9.2 %collective-permute-start = (f32[3,1,1024]{2,1,0:T(1,128)S(1)}, f32[3,1,1024]{2,1,0:T(1,128)S(1)}, u32[]{:S(2)}, u32[]{:S(2)}) collective-permute-start(f32[3,1,1024]{2,1,0:T(1,128)S(1)} %get-tuple-element.21), channel_id=1, source_target_pairs={{0,1},{1,2},{2,3},{3,4},{4,5},{5,6},{6,7},{7,8},{8,9},{9,10},{10,1... | collective-permute-start | bytes 36872 | tf_op jit(solution)/shard_map/ppermute | solution.py:285
  8.3 10.9 %copy-start.3 = (f32[3,1,64,1024]{3,2,1,0:T(8,128)S(1)}, f32[3,1,64,1024]{3,2,1,0:T(8,128)}, u32[]{:S(2)}) copy-start(f32[3,1,64,1024]{3,2,1,0:T(8,128)} %param.2) | copy-start | bytes 2359300
  8.3 33.1 %copy-start.4 = (bf16[144,1024]{1,0:T(8,128)(2,1)S(1)}, bf16[144,1024]{1,0:T(8,128)(2,1)}, u32[]{:S(2)}) copy-start(bf16[144,1024]{1,0:T(8,128)(2,1)} %constant.21.clone.table_ref) | copy-start | bytes 884740
  11.4 39.0 %all-to-all-start = ((bf16[16,296,128]{2,1,0:T(8,128)(2,1)}), bf16[16,296,128]{2,1,0:T(8,128)(2,1)S(1)}, u32[]{:S(2)}, u32[]{:S(2)}) async-start(bf16[16,296,128]{2,1,0:T(8,128)(2,1)} %products.1), calls=%async_computation | async-start | bytes 2424832 | tf_op jit(solution)/shard_map/all_to_all | solution.py:299
  19.2 19.7 %collective-permute-start.3 = (f32[3,64,1024]{2,1,0:T(8,128)S(1)}, f32[3,64,1024]{2,1,0:T(8,128)S(1)}, u32[]{:S(2)}, u32[]{:S(2)}) collective-permute-start(f32[3,64,1024]{2,1,0:T(8,128)S(1)} %bitcast.11), channel_id=1, source_target_pairs={{16,0},{1,17},{18,2},{3,19},{20,4},{5,21},{22,6},{7,23},{24,8},{9,... | collective-permute-start | bytes 2359304 | tf_op jit(solution)/shard_map/ppermute | solution.py:302
  22.3 19.1 %collective-permute-start.2 = (f32[3,64,1024]{2,1,0:T(8,128)S(1)}, f32[3,64,1024]{2,1,0:T(8,128)}, u32[]{:S(2)}, u32[]{:S(2)}) collective-permute-start(f32[3,64,1024]{2,1,0:T(8,128)S(1)} %bitcast.12), channel_id=1, source_target_pairs={{0,16},{17,1},{2,18},{19,3},{4,20},{21,5},{6,22},{23,7},{8,24},{25... | collective-permute-start | bytes 2359304 | tf_op jit(solution)/shard_map/ppermute | solution.py:301
  45.2 0.7 copy-start.1
  50.4 28.1 %all-to-all-start.1 = ((bf16[16,192,128]{2,1,0:T(8,128)(2,1)}), bf16[16,192,128]{2,1,0:T(8,128)(2,1)S(1)}, u32[]{:S(2)}, u32[]{:S(2)}) async-start(bf16[16,192,128]{2,1,0:T(8,128)(2,1)} %get-tuple-element.14), calls=%async_computation.1 | async-start | bytes 1572864 | tf_op jit(solution)/shard_map/all_to_all | solution.py:313
  55.9 10.4 %copy-start.5 = (bf16[144,1024]{1,0:T(8,128)(2,1)S(1)}, bf16[144,1024]{1,0:T(8,128)(2,1)}, u32[]{:S(2)}) copy-start(bf16[144,1024]{1,0:T(8,128)(2,1)} %constant.21.clone.table_ref) | copy-start | bytes 884740
  57.5 14.4 %copy-start = (bf16[3,64,1024]{2,1,0:T(8,128)(2,1)S(1)}, bf16[3,64,1024]{2,1,0:T(8,128)(2,1)}, u32[]{:S(2)}) copy-start(bf16[3,64,1024]{2,1,0:T(8,128)(2,1)} %get-tuple-element.15.smooth_ref) | copy-start | bytes 1179652
  57.5 12.5 %collective-permute-start.5 = (bf16[3,64,1024]{2,1,0:T(8,128)(2,1)}, bf16[3,64,1024]{2,1,0:T(8,128)(2,1)S(1)}, u32[]{:S(2)}, u32[]{:S(2)}) collective-permute-start(bf16[3,64,1024]{2,1,0:T(8,128)(2,1)} %get-tuple-element.15.smooth_ref), channel_id=1, source_target_pairs={{16,0},{1,17},{18,2},{3,19},{20,4},{5,21},{22,6},{7,23},{24,8},{9,... | collective-permute-start | bytes 1179656 | tf_op jit(solution)/shard_map/ppermute | solution.py:328
  59.5 12.4 %collective-permute-start.4 = (bf16[3,64,1024]{2,1,0:T(8,128)(2,1)}, bf16[3,64,1024]{2,1,0:T(8,128)(2,1)S(1)}, u32[]{:S(2)}, u32[]{:S(2)}) collective-permute-start(bf16[3,64,1024]{2,1,0:T(8,128)(2,1)} %get-tuple-element.15.smooth_ref), channel_id=1, source_target_pairs={{0,16},{17,1},{2,18},{19,3},{4,20},{21,5},{6,22},{23,7},{8,24},{25... | collective-permute-start | bytes 1179656 | tf_op jit(solution)/shard_map/ppermute | solution.py:327
  78.5 13.5 %copy-start.2 = (f32[64,1024]{1,0:T(8,128)S(1)}, f32[64,1024]{1,0:T(8,128)}, u32[]{:S(2)}) copy-start(f32[64,1024]{1,0:T(8,128)} %copy-done.1) | copy-start | bytes 786436

commit v12 on v10

--- a/solution.py
+++ b/solution.py
@@ -307,7 +307,7 @@
         (jax.ShapeDtypeStruct(strain_shape, bf16), jax.ShapeDtypeStruct((depth, nx), f32)),
         2 * 6 * depth * nx * nx,
         36 * depth * nx + 2 * nx * nx,
-        [vmem((6 * depth, nx), bf16), vmem(strain_shape, bf16), dma((2,))],
+        [vmem((6 * depth, nx), bf16), vmem(strain_shape, bf16), dma((1,))],
         "strain",
         (7,),
     )(lanes_x, velocity, one, two, sense, first, last)

time: 93.4 us -> 93.4 us (level)
  no operation moved by 1% of the time
where the time goes in v12:
time: 93.4 us; the launch traced here: 92.9 us
  starting transfers between devices  33.2 us (36%)
  waiting for transfers between devices  31.4 us (34%)
  Pallas kernels  13.7 us (15%)
  blocking collectives  12.2 us (13%)
  local copies, waits for them, and re-layouts  1.68 us (2%)
    pallas_call x7, Pallas kernels, run(): pl.pallas_call(kernel, out_shape=out_shape, in_specs=[space(i) for i in r...  13.7 us
    all_to_all x1, blocking collectives, body(): totals = lax.all_to_all(sums, 'pz', 0, 0, tiled=True)  12.2 us
    ppermute x1, waiting for transfers between devices, body(): two = lax.ppermute(velocity, ('py', 'pz'), inward)  11.1 us
    all_to_all x1, starting transfers between devices, body(): received = lax.all_to_all(send, 'pz', 0, 0, tiled=True)  7.79 us
    ppermute x1, starting transfers between devices, body(): smooth_one = lax.ppermute(smooth, ('py', 'pz'), outward)  6.68 us
    all_to_all x1, waiting for transfers between devices, body(): received_strain = lax.all_to_all(send_strain, 'pz', 0, 0, tiled=True)  5.56 us
    ppermute x1, starting transfers between devices, body(): one = lax.ppermute(velocity, ('py', 'pz'), outward)  5.48 us
    all_to_all x1, starting transfers between devices, body(): received_strain = lax.all_to_all(send_strain, 'pz', 0, 0, tiled=True)  5.42 us
  transfers between devices with their start and end apart: 8, of which 7 were waited for; matrix products, arithmetic and copies ran while one was open for 0% of the time, Pallas kernels for 12%

profile of v12, /device:TPU:33, one launch (start us, length us, event | category | flops | bytes accessed | tf_op | source)
XLA Modules:
  0.0 92.9 jit_solution(5577569185076162406)
XLA Ops:
  0.6 1.0 %fusion = (f32[3,1,1024]{2,1,0:T(1,128)S(1)}, f32[3,1,1024]{2,1,0:T(1,128)S(1)}) fusion(f32[3,64,1024]{2,1,0:T(8,128)} %bitcast.9), kind=kLoop, calls=%fused_computation | loop fusion | bytes 49152 | tf_op jit(solution)/shard_map/slice | solution.py:287
  1.6 0.7 collective-permute-start.1
  2.3 2.0 %collective-permute-start = (f32[3,1,1024]{2,1,0:T(1,128)S(1)}, f32[3,1,1024]{2,1,0:T(1,128)S(1)}, u32[]{:S(2)}, u32[]{:S(2)}) collective-permute-start(f32[3,1,1024]{2,1,0:T(1,128)S(1)} %get-tuple-element.21), channel_id=1, source_target_pairs={{0,1},{1,2},{2,3},{3,4},{4,5},{5,6},{6,7},{7,8},{8,9},{9,10},{10,1... | collective-permute-start | bytes 36872 | tf_op jit(solution)/shard_map/ppermute | solution.py:286
  4.3 4.0 %products.1 = bf16[16,296,128]{2,1,0:T(8,128)(2,1)} custom-call(bf16[144,1024]{1,0:T(8,128)(2,1)} %constant.21.clone.table_ref, f32[3,64,1024]{2,1,0:T(8,128)} %bitcast.10), custom_call_target="tpu_custom_call" | custom-call | flops 1207959552 | bytes 2883584 | tf_op jit(solution)/shard_map/products/pallas_call | solution.py:36
  8.3 0.0 copy-start.3
  8.3 0.0 copy-start.4
  8.3 0.0 collective-permute-done.1.last_ref
  8.3 3.1 %collective-permute-done.first_ref = f32[3,1,1024]{2,1,0:T(1,128)S(1)} collective-permute-done((f32[3,1,1024]{2,1,0:T(1,128)S(1)}, f32[3,1,1024]{2,1,0:T(1,128)S(1)}, u32[]{:S(2)}, u32[]{:S(2)}) %collective-permute-start) | collective-permute-done | bytes 12320 | tf_op jit(solution)/shard_map/ppermute | solution.py:286
  11.4 7.8 %all-to-all-start = ((bf16[16,296,128]{2,1,0:T(8,128)(2,1)}), bf16[16,296,128]{2,1,0:T(8,128)(2,1)S(1)}, u32[]{:S(2)}, u32[]{:S(2)}) async-start(bf16[16,296,128]{2,1,0:T(8,128)(2,1)} %products.1), calls=%async_computation | async-start | bytes 2424832 | tf_op jit(solution)/shard_map/all_to_all | solution.py:300
  19.2 0.0 copy-done.3
  19.2 3.1 %collective-permute-start.3 = (f32[3,64,1024]{2,1,0:T(8,128)S(1)}, f32[3,64,1024]{2,1,0:T(8,128)S(1)}, u32[]{:S(2)}, u32[]{:S(2)}) collective-permute-start(f32[3,64,1024]{2,1,0:T(8,128)S(1)} %bitcast.11), channel_id=1, source_target_pairs={{16,0},{1,17},{18,2},{3,19},{20,4},{5,21},{22,6},{7,23},{24,8},{9,... | collective-permute-start | bytes 2359304 | tf_op jit(solution)/shard_map/ppermute | solution.py:303
  22.4 5.5 %collective-permute-start.2 = (f32[3,64,1024]{2,1,0:T(8,128)S(1)}, f32[3,64,1024]{2,1,0:T(8,128)}, u32[]{:S(2)}, u32[]{:S(2)}) collective-permute-start(f32[3,64,1024]{2,1,0:T(8,128)S(1)} %bitcast.12), channel_id=1, source_target_pairs={{0,16},{17,1},{2,18},{19,3},{4,20},{21,5},{6,22},{23,7},{8,24},{25... | collective-permute-start | bytes 2359304 | tf_op jit(solution)/shard_map/ppermute | solution.py:302
  27.9 11.1 %collective-permute-done.3.two_ref = f32[3,64,1024]{2,1,0:T(8,128)S(1)} collective-permute-done((f32[3,64,1024]{2,1,0:T(8,128)S(1)}, f32[3,64,1024]{2,1,0:T(8,128)S(1)}, u32[]{:S(2)}, u32[]{:S(2)}) %collective-permute-start.3) | collective-permute-done | bytes 786464 | tf_op jit(solution)/shard_map/ppermute | solution.py:303
  38.9 2.5 %collective-permute-done.2.one_ref = f32[3,64,1024]{2,1,0:T(8,128)} collective-permute-done((f32[3,64,1024]{2,1,0:T(8,128)S(1)}, f32[3,64,1024]{2,1,0:T(8,128)}, u32[]{:S(2)}, u32[]{:S(2)}) %collective-permute-start.2) | collective-permute-done | bytes 786464 | tf_op jit(solution)/shard_map/ppermute | solution.py:302
  41.4 0.0 copy-done.4
  41.4 3.8 %strain.1 = (bf16[16,192,128]{2,1,0:T(8,128)(2,1)}, f32[64,1024]{1,0:T(8,128)S(1)}) custom-call(bf16[144,1024]{1,0:T(8,128)(2,1)S(1)} %copy-done.4, f32[3,64,1024]{2,1,0:T(8,128)S(1)} %bitcast.13, f32[3,64,1024]{2,1,0:T(8,128)} %collective-permute-done.2.one_ref, f32[3,64,1024]{2,1,0:T(8,128)S(1)} %collective-permute-done.3.two_ref, ...), custom_call_target="tpu_custom_call" | custom-call | flops 805306368 | bytes 4456448 | tf_op jit(solution)/shard_map/strain/pallas_call | solution.py:36
  45.2 0.0 copy-start.1
  45.2 0.7 copy-done.1
  45.9 4.5 %all-to-all-done.recv_ref = bf16[16,296,128]{2,1,0:T(8,128)(2,1)S(1)} async-done(((bf16[16,296,128]{2,1,0:T(8,128)(2,1)}), bf16[16,296,128]{2,1,0:T(8,128)(2,1)S(1)}, u32[]{:S(2)}, u32[]{:S(2)}) %all-to-all-start) | async-done | bytes 1212448 | tf_op jit(solution)/shard_map/all_to_all | solution.py:300
  50.4 5.4 %all-to-all-start.1 = ((bf16[16,192,128]{2,1,0:T(8,128)(2,1)}), bf16[16,192,128]{2,1,0:T(8,128)(2,1)S(1)}, u32[]{:S(2)}, u32[]{:S(2)}) async-start(bf16[16,192,128]{2,1,0:T(8,128)(2,1)} %get-tuple-element.14), calls=%async_computation.1 | async-start | bytes 1572864 | tf_op jit(solution)/shard_map/all_to_all | solution.py:314
  55.9 0.0 copy-start.5
  55.9 1.6 %smooth.1 = (bf16[3,64,1024]{2,1,0:T(8,128)(2,1)}, f32[16,1024]{1,0:T(8,128)S(1)}, bf16[8,1024]{1,0:T(8,128)(2,1)S(1)}) custom-call(bf16[144,1024]{1,0:T(8,128)(2,1)S(1)} %copy-done.4, bf16[16,296,128]{2,1,0:T(8,128)(2,1)S(1)} %all-to-all-done.recv_ref), custom_call_target="tpu_custom_call" | custom-call | flops 536870912 | bytes 2097152 | tf_op jit(solution)/shard_map/smooth/pallas_call | solution.py:36
  57.5 0.0 copy-start
  57.5 2.0 %collective-permute-start.5 = (bf16[3,64,1024]{2,1,0:T(8,128)(2,1)}, bf16[3,64,1024]{2,1,0:T(8,128)(2,1)S(1)}, u32[]{:S(2)}, u32[]{:S(2)}) collective-permute-start(bf16[3,64,1024]{2,1,0:T(8,128)(2,1)} %get-tuple-element.15.smooth_ref), channel_id=1, source_target_pairs={{16,0},{1,17},{18,2},{3,19},{20,4},{5,21},{22,6},{7,23},{24,8},{9,... | collective-permute-start | bytes 1179656 | tf_op jit(solution)/shard_map/ppermute | solution.py:329
  59.5 6.7 %collective-permute-start.4 = (bf16[3,64,1024]{2,1,0:T(8,128)(2,1)}, bf16[3,64,1024]{2,1,0:T(8,128)(2,1)S(1)}, u32[]{:S(2)}, u32[]{:S(2)}) collective-permute-start(bf16[3,64,1024]{2,1,0:T(8,128)(2,1)} %get-tuple-element.15.smooth_ref), channel_id=1, source_target_pairs={{0,16},{17,1},{2,18},{19,3},{4,20},{21,5},{6,22},{23,7},{8,24},{25... | collective-permute-start | bytes 1179656 | tf_op jit(solution)/shard_map/ppermute | solution.py:328
  66.2 0.0 copy-done.5
  66.2 1.1 %squares.1.squares_ref = bf16[6,64,1024]{2,1,0:T(8,128)(2,1)S(1)} custom-call(bf16[144,1024]{1,0:T(8,128)(2,1)S(1)} %copy-done.5, bf16[16,296,128]{2,1,0:T(8,128)(2,1)S(1)} %all-to-all-done.recv_ref), custom_call_target="tpu_custom_call" | custom-call | flops 805306368 | bytes 1572864 | tf_op jit(solution)/shard_map/squares/pallas_call | solution.py:36
  67.3 2.6 %collective-permute-done.5.two_ref = bf16[3,64,1024]{2,1,0:T(8,128)(2,1)S(1)} collective-permute-done((bf16[3,64,1024]{2,1,0:T(8,128)(2,1)}, bf16[3,64,1024]{2,1,0:T(8,128)(2,1)S(1)}, u32[]{:S(2)}, u32[]{:S(2)}) %collective-permute-start.5) | collective-permute-done | bytes 393248 | tf_op jit(solution)/shard_map/ppermute | solution.py:329
  69.9 2.0 %collective-permute-done.4.one_ref = bf16[3,64,1024]{2,1,0:T(8,128)(2,1)S(1)} collective-permute-done((bf16[3,64,1024]{2,1,0:T(8,128)(2,1)}, bf16[3,64,1024]{2,1,0:T(8,128)(2,1)S(1)}, u32[]{:S(2)}, u32[]{:S(2)}) %collective-permute-start.4) | collective-permute-done | bytes 393248 | tf_op jit(solution)/shard_map/ppermute | solution.py:328
  71.9 0.0 copy-done
  71.9 1.1 %model.1.model_ref = f32[6,64,1024]{2,1,0:T(8,128)S(1)} custom-call(bf16[3,64,1024]{2,1,0:T(8,128)(2,1)S(1)} %copy-done, bf16[3,64,1024]{2,1,0:T(8,128)(2,1)S(1)} %collective-permute-done.4.one_ref, bf16[3,64,1024]{2,1,0:T(8,128)(2,1)S(1)} %collective-permute-done.5.two_ref, f32[1,1]{1,0:T(1,128)} %bitcast.1.sense_ref, ...), custom_call_target="tpu_custom_call" | custom-call | flops 6553600 | bytes 1572864 | tf_op jit(solution)/shard_map/model/pallas_call | solution.py:36
  73.0 5.6 %all-to-all-done.1.recv_ref = bf16[16,192,128]{2,1,0:T(8,128)(2,1)S(1)} async-done(((bf16[16,192,128]{2,1,0:T(8,128)(2,1)}), bf16[16,192,128]{2,1,0:T(8,128)(2,1)S(1)}, u32[]{:S(2)}, u32[]{:S(2)}) %all-to-all-start.1) | async-done | bytes 786464 | tf_op jit(solution)/shard_map/all_to_all | solution.py:314
  78.5 0.0 copy-start.2
  78.5 1.3 %sums.1 = f32[16,1,128]{2,1,0:T(1,128)S(1)} custom-call(bf16[8,1024]{1,0:T(8,128)(2,1)S(1)} %get-tuple-element.11.table_ref, bf16[16,192,128]{2,1,0:T(8,128)(2,1)S(1)} %all-to-all-done.1.recv_ref, bf16[3,64,1024]{2,1,0:T(8,128)(2,1)S(1)} %copy-done, bf16[6,64,1024]{2,1,0:T(8,128)(2,1)S(1)} %squares.1.squares_ref, f32[6,64,1024]{2,1,0:T(8,128)S(1)} %model.1.model_ref), custom_call_target="tpu_custom_call" | custom-call | flops 805306368 | bytes 3145728 | tf_op jit(solution)/shard_map/sums/pallas_call | solution.py:36
  79.9 12.2 %all_to_all.15.refs_0_ = f32[16,1,128]{2,1,0:T(1,128)S(1)} all-to-all(f32[16,1,128]{2,1,0:T(1,128)S(1)} %sums.1), channel_id=1, replica_groups=mesh['py'=32,'pz'=16] {'pz'}, dimensions={0} | all-to-all | bytes 16384 | tf_op jit(solution)/shard_map/all_to_all | solution.py:354
  92.1 0.0 copy-done.2
  92.1 0.8 viscosity.1
Async XLA Ops:
  1.6 6.7 %collective-permute-start.1 = (f32[3,1,1024]{2,1,0:T(1,128)S(1)}, f32[3,1,1024]{2,1,0:T(1,128)S(1)}, u32[]{:S(2)}, u32[]{:S(2)}) collective-permute-start(f32[3,1,1024]{2,1,0:T(1,128)S(1)} %get-tuple-element.20), channel_id=1, source_target_pairs={{1,0},{2,1},{3,2},{4,3},{5,4},{6,5},{7,6},{8,7},{9,8},{10,9},{11,1... | collective-permute-start | bytes 36872 | tf_op jit(solution)/shard_map/ppermute | solution.py:287
  2.3 9.2 %collective-permute-start = (f32[3,1,1024]{2,1,0:T(1,128)S(1)}, f32[3,1,1024]{2,1,0:T(1,128)S(1)}, u32[]{:S(2)}, u32[]{:S(2)}) collective-permute-start(f32[3,1,1024]{2,1,0:T(1,128)S(1)} %get-tuple-element.21), channel_id=1, source_target_pairs={{0,1},{1,2},{2,3},{3,4},{4,5},{5,6},{6,7},{7,8},{8,9},{9,10},{10,1... | collective-permute-start | bytes 36872 | tf_op jit(solution)/shard_map/ppermute | solution.py:286
  8.3 10.9 %copy-start.3 = (f32[3,1,64,1024]{3,2,1,0:T(8,128)S(1)}, f32[3,1,64,1024]{3,2,1,0:T(8,128)}, u32[]{:S(2)}) copy-start(f32[3,1,64,1024]{3,2,1,0:T(8,128)} %param.2) | copy-start | bytes 2359300
  8.3 33.1 %copy-start.4 = (bf16[144,1024]{1,0:T(8,128)(2,1)S(1)}, bf16[144,1024]{1,0:T(8,128)(2,1)}, u32[]{:S(2)}) copy-start(bf16[144,1024]{1,0:T(8,128)(2,1)} %constant.21.clone.table_ref) | copy-start | bytes 884740
  11.4 39.0 %all-to-all-start = ((bf16[16,296,128]{2,1,0:T(8,128)(2,1)}), bf16[16,296,128]{2,1,0:T(8,128)(2,1)S(1)}, u32[]{:S(2)}, u32[]{:S(2)}) async-start(bf16[16,296,128]{2,1,0:T(8,128)(2,1)} %products.1), calls=%async_computation | async-start | bytes 2424832 | tf_op jit(solution)/shard_map/all_to_all | solution.py:300
  19.2 19.7 %collective-permute-start.3 = (f32[3,64,1024]{2,1,0:T(8,128)S(1)}, f32[3,64,1024]{2,1,0:T(8,128)S(1)}, u32[]{:S(2)}, u32[]{:S(2)}) collective-permute-start(f32[3,64,1024]{2,1,0:T(8,128)S(1)} %bitcast.11), channel_id=1, source_target_pairs={{16,0},{1,17},{18,2},{3,19},{20,4},{5,21},{22,6},{7,23},{24,8},{9,... | collective-permute-start | bytes 2359304 | tf_op jit(solution)/shard_map/ppermute | solution.py:303
  22.4 19.1 %collective-permute-start.2 = (f32[3,64,1024]{2,1,0:T(8,128)S(1)}, f32[3,64,1024]{2,1,0:T(8,128)}, u32[]{:S(2)}, u32[]{:S(2)}) collective-permute-start(f32[3,64,1024]{2,1,0:T(8,128)S(1)} %bitcast.12), channel_id=1, source_target_pairs={{0,16},{17,1},{2,18},{19,3},{4,20},{21,5},{6,22},{23,7},{8,24},{25... | collective-permute-start | bytes 2359304 | tf_op jit(solution)/shard_map/ppermute | solution.py:302
  45.2 0.7 copy-start.1
  50.4 28.1 %all-to-all-start.1 = ((bf16[16,192,128]{2,1,0:T(8,128)(2,1)}), bf16[16,192,128]{2,1,0:T(8,128)(2,1)S(1)}, u32[]{:S(2)}, u32[]{:S(2)}) async-start(bf16[16,192,128]{2,1,0:T(8,128)(2,1)} %get-tuple-element.14), calls=%async_computation.1 | async-start | bytes 1572864 | tf_op jit(solution)/shard_map/all_to_all | solution.py:314
  55.9 10.3 %copy-start.5 = (bf16[144,1024]{1,0:T(8,128)(2,1)S(1)}, bf16[144,1024]{1,0:T(8,128)(2,1)}, u32[]{:S(2)}) copy-start(bf16[144,1024]{1,0:T(8,128)(2,1)} %constant.21.clone.table_ref) | copy-start | bytes 884740
  57.5 14.4 %copy-start = (bf16[3,64,1024]{2,1,0:T(8,128)(2,1)S(1)}, bf16[3,64,1024]{2,1,0:T(8,128)(2,1)}, u32[]{:S(2)}) copy-start(bf16[3,64,1024]{2,1,0:T(8,128)(2,1)} %get-tuple-element.15.smooth_ref) | copy-start | bytes 1179652
  57.5 12.5 %collective-permute-start.5 = (bf16[3,64,1024]{2,1,0:T(8,128)(2,1)}, bf16[3,64,1024]{2,1,0:T(8,128)(2,1)S(1)}, u32[]{:S(2)}, u32[]{:S(2)}) collective-permute-start(bf16[3,64,1024]{2,1,0:T(8,128)(2,1)} %get-tuple-element.15.smooth_ref), channel_id=1, source_target_pairs={{16,0},{1,17},{18,2},{3,19},{20,4},{5,21},{22,6},{7,23},{24,8},{9,... | collective-permute-start | bytes 1179656 | tf_op jit(solution)/shard_map/ppermute | solution.py:329
  59.5 12.4 %collective-permute-start.4 = (bf16[3,64,1024]{2,1,0:T(8,128)(2,1)}, bf16[3,64,1024]{2,1,0:T(8,128)(2,1)S(1)}, u32[]{:S(2)}, u32[]{:S(2)}) collective-permute-start(bf16[3,64,1024]{2,1,0:T(8,128)(2,1)} %get-tuple-element.15.smooth_ref), channel_id=1, source_target_pairs={{0,16},{17,1},{2,18},{19,3},{4,20},{21,5},{6,22},{23,7},{8,24},{25... | collective-permute-start | bytes 1179656 | tf_op jit(solution)/shard_map/ppermute | solution.py:328
  78.5 13.5 %copy-start.2 = (f32[64,1024]{1,0:T(8,128)S(1)}, f32[64,1024]{1,0:T(8,128)}, u32[]{:S(2)}) copy-start(f32[64,1024]{1,0:T(8,128)} %copy-done.1) | copy-start | bytes 786436
